TPU v7x, 32 devices: a whole 2x2x4 slice. The times are simulated.
32 devices in a mesh: section: 2 (over core), shard: 4 (over z), replica: 4 (over y, x).
Axes of the slice: x: 2, y: 2, z: 4, core: 2. Of those that a mesh axis runs over, the one named last changes fastest.
Arguments:
- hidden_in: bfloat16 [2, 4, 256, 960], P(None, 'replica', 'shard'), may hold values from -6 to 6
- segment_ids: int32 [2, 4, 256], P(None, 'replica'), may hold values from 0 to 3, as said below
- norm_attn: bfloat16 [2, 960], P('section', 'shard'), may hold values from 0.099609375 to 1.8984375
- w_query: bfloat16 [2, 960, 960], P('section', 'shard'), may hold values from -0.1875 to 0.1875
- w_key: bfloat16 [2, 960, 320], P('section', 'shard'), may hold values from -0.1875 to 0.1875
- w_value: bfloat16 [2, 960, 320], P('section', 'shard'), may hold values from -0.1875 to 0.1875
- w_out: bfloat16 [2, 960, 960], P('section', 'shard'), may hold values from -0.75 to 0.75
- norm_ffn: bfloat16 [2, 960], P('section', 'shard'), may hold values from 0.099609375 to 1.8984375
- w_gate: bfloat16 [2, 960, 2560], P('section', 'shard'), may hold values from -0.1875 to 0.1875
- w_up: bfloat16 [2, 960, 2560], P('section', 'shard'), may hold values from -0.1875 to 0.1875
- w_down: bfloat16 [2, 2560, 960], P('section', 'shard'), may hold values from -0.125 to 0.125
- out_grad: bfloat16 [2, 4, 256, 960], P(None, 'replica', 'shard'), may hold values from -6 to 6
Outputs:
- layer_out: bfloat16 [2, 2, 4, 256, 960], P('section', None, 'replica', 'shard')
- input_grad: bfloat16 [2, 2, 4, 256, 960], P('section', None, 'replica', 'shard')
- grad_norm_attn: float32 [2, 960], P('section', 'shard')
- grad_w_query: float32 [2, 960, 960], P('section', 'shard')
- grad_w_key: float32 [2, 960, 320], P('section', 'shard')
- grad_w_value: float32 [2, 960, 320], P('section', 'shard')
- grad_w_out: float32 [2, 960, 960], P('section', 'shard')
- grad_norm_ffn: float32 [2, 960], P('section', 'shard')
- grad_w_gate: float32 [2, 960, 2560], P('section', 'shard')
- grad_w_up: float32 [2, 960, 2560], P('section', 'shard')
- grad_w_down: float32 [2, 2560, 960], P('section', 'shard')
Inputs may be any that keep to these rules, and one draw needn't show every extreme that they name: `segment_ids`: along each sequence the segment numbers start at 0, never fall, and take every value up to the largest.
All inputs are finite; a program needn't handle non-finite values.
Results may differ from a plain program's by a relative error of at most 0.025.
Values may be sent and summed in bfloat16 or wider, within the bound.
No kernel may reach another device: no remote copies, remote signals or barrier semaphores. Data moves between devices by JAX's collectives and lax.ppermute only.
A program may use at most 192 MiB of HBM per device.

v0:
```python
import jax
import jax.numpy as jnp
from jax import lax
from jax.sharding import PartitionSpec as P

QH = 15
KVH = 5
HD = 64


rope_base = 100000.0
norm_eps = 1e-05
mask_fill = -1000000000.0


def passed_along(value, axis, steps):
    count = lax.axis_size(axis)
    first, last = (max(0, -steps), min(count, count - steps))
    return lax.ppermute(value, axis, [(source, source + steps) for source in range(first, last)])


def rope_tables(positions):
    frequency = rope_base ** (-jnp.arange(HD // 2).astype(jnp.float32) * (2.0 / HD))
    angles = positions.astype(jnp.float32)[:, None] * frequency[None, :]
    angles = jnp.concatenate([angles, angles], axis=1)
    return (jnp.cos(angles)[:, None, :], jnp.sin(angles)[:, None, :])


def rotate_fwd(values, cos_tab, sin_tab):
    half_size = values.shape[-1] // 2
    turned = jnp.concatenate([-values[..., half_size:], values[..., :half_size]], axis=-1)
    return values * cos_tab + turned * sin_tab


def rotate_back(grad_vals, cos_tab, sin_tab):
    half_size = grad_vals.shape[-1] // 2
    shifted = grad_vals * sin_tab
    turned = jnp.concatenate([shifted[..., half_size:], -shifted[..., :half_size]], axis=-1)
    return grad_vals * cos_tab + turned


def outer_sum(left_rows, right_rows):
    return lax.dot_general(
        left_rows, right_rows, (((0,), (0,)), ((), ())), preferred_element_type=jnp.float32
    )


def times_trans(left_rows, matrix):
    return lax.dot_general(
        left_rows, matrix, (((1,), (1,)), ((), ())), preferred_element_type=jnp.float32
    )


def row_scale(values):
    return lax.rsqrt(jnp.mean(values * values, axis=-1, keepdims=True) + norm_eps)


def norm_back(grad_normed, values, factor, gain_vec):
    gain_grad = jnp.sum(grad_normed * values * factor, axis=0)
    weighted = grad_normed * gain_vec
    inner_mean = jnp.mean(weighted * values, axis=-1, keepdims=True)
    return (gain_grad, factor * weighted - values * factor * factor * factor * inner_mean)


def local_layout(segments, shard_pos, length):
    start_row = shard_pos * length
    local_rows = start_row + jnp.arange(length, dtype=jnp.int32)
    own_segments = lax.dynamic_slice_in_dim(segments, start_row, length)
    before = jnp.sum((segments[None, :] < own_segments[:, None]).astype(jnp.int32), axis=1)
    key_rows = jnp.arange(segments.shape[0], dtype=jnp.int32)
    allowed = (segments[None, :] == own_segments[:, None]) & (
        key_rows[None, :] <= local_rows[:, None]
    )
    cos_tab, sin_tab = rope_tables(local_rows - before)
    return (allowed, cos_tab, sin_tab)


def attention_scores(queries, keys_all, allowed):
    length = queries.shape[0]
    query_heads = queries.reshape(length, KVH, QH // KVH, HD)
    key_heads = keys_all.reshape(keys_all.shape[0], KVH, HD)
    scores = jnp.einsum(
        "cgrd,sgd->grcs", query_heads, key_heads, preferred_element_type=jnp.float32
    ) * HD ** (-0.5)
    return jnp.where(allowed[None, None], scores, mask_fill)


def forward_layer(layer_in, segments, weights, shard_pos):
    gain_attn, query_w, key_w, value_w, out_w, gain_ffn, gate_w, up_w, down_w = weights
    length = layer_in.shape[0]
    allowed, cos_tab, sin_tab = local_layout(segments, shard_pos, length)
    wide_in = layer_in.astype(jnp.float32)
    normed = (wide_in * row_scale(wide_in) * gain_attn.astype(jnp.float32)).astype(jnp.bfloat16)
    query_pre = jnp.dot(normed, query_w, preferred_element_type=jnp.float32).reshape(length, QH, HD)
    key_pre = jnp.dot(normed, key_w, preferred_element_type=jnp.float32).reshape(length, KVH, HD)
    queries = rotate_fwd(query_pre, cos_tab, sin_tab).astype(jnp.bfloat16).reshape(length, QH * HD)
    keys_own = rotate_fwd(key_pre, cos_tab, sin_tab).astype(jnp.bfloat16).reshape(length, KVH * HD)
    values_own = jnp.dot(normed, value_w, preferred_element_type=jnp.float32).astype(jnp.bfloat16)
    keys_all, values_all = (
        lax.all_gather(keys_own, "shard", axis=0, tiled=True),
        lax.all_gather(values_own, "shard", axis=0, tiled=True),
    )
    scores = attention_scores(queries, keys_all, allowed)
    row_max = jnp.max(scores, axis=-1, keepdims=True)
    exponent = jnp.exp(scores - row_max)
    denom_sum = jnp.sum(exponent, axis=-1, keepdims=True)
    log_total = row_max + jnp.log(denom_sum)
    weights_low = (exponent / denom_sum).astype(jnp.bfloat16)
    attended = jnp.einsum(
        "grcs,sgd->cgrd",
        weights_low,
        values_all.reshape(-1, KVH, HD),
        preferred_element_type=jnp.float32,
    )
    attended = attended.reshape(length, QH * HD).astype(jnp.bfloat16)
    middle = wide_in + jnp.dot(attended, out_w, preferred_element_type=jnp.float32)
    normed_ffn = (middle * row_scale(middle) * gain_ffn.astype(jnp.float32)).astype(jnp.bfloat16)
    gate_pre = jnp.dot(normed_ffn, gate_w, preferred_element_type=jnp.float32)
    up_pre = jnp.dot(normed_ffn, up_w, preferred_element_type=jnp.float32)
    hidden_act = (gate_pre * jax.nn.sigmoid(gate_pre) * up_pre).astype(jnp.bfloat16)
    result = middle + jnp.dot(hidden_act, down_w, preferred_element_type=jnp.float32)
    kept = (
        layer_in,
        normed,
        queries,
        keys_all,
        values_all,
        log_total,
        attended,
        middle,
        normed_ffn,
        gate_pre,
        up_pre,
        hidden_act,
    )
    return (result.astype(jnp.bfloat16), kept)


def backward_layer(grad_low, segments, weights, kept, shard_pos):
    gain_attn, query_w, key_w, value_w, out_w, gain_ffn, gate_w, up_w, down_w = weights
    (
        layer_in,
        normed,
        queries,
        keys_all,
        values_all,
        log_total,
        attended,
        middle,
        normed_ffn,
        gate_pre,
        up_pre,
        hidden_act,
    ) = kept
    length = layer_in.shape[0]
    allowed, cos_tab, sin_tab = local_layout(segments, shard_pos, length)
    grad_out = grad_low.astype(jnp.float32)
    grad_hidden = times_trans(grad_low, down_w)
    sigmoid_gate = jax.nn.sigmoid(gate_pre)
    grad_gate_pre = (
        grad_hidden * up_pre * sigmoid_gate * (1.0 + gate_pre * (1.0 - sigmoid_gate))
    ).astype(jnp.bfloat16)
    grad_up_pre = (grad_hidden * gate_pre * sigmoid_gate).astype(jnp.bfloat16)
    grad_normed_ffn = times_trans(grad_gate_pre, gate_w) + times_trans(grad_up_pre, up_w)
    grad_gain_ffn, through_ffn = norm_back(
        grad_normed_ffn, middle, row_scale(middle), gain_ffn.astype(jnp.float32)
    )
    grad_middle = grad_out + through_ffn
    grad_branch = grad_middle.astype(jnp.bfloat16)
    grad_attended = times_trans(grad_branch, out_w).astype(jnp.bfloat16)
    scores = attention_scores(queries, keys_all, allowed)
    prob_vals = jnp.exp(scores - log_total)
    grad_heads = grad_attended.reshape(length, KVH, QH // KVH, HD)
    value_heads = values_all.reshape(-1, KVH, HD)
    grad_probs = jnp.einsum(
        "cgrd,sgd->grcs", grad_heads, value_heads, preferred_element_type=jnp.float32
    )
    centre = jnp.sum(prob_vals * grad_probs, axis=-1, keepdims=True)
    grad_scores = (prob_vals * (grad_probs - centre)).astype(jnp.bfloat16)
    grad_queries = jnp.einsum(
        "grcs,sgd->cgrd",
        grad_scores,
        keys_all.reshape(-1, KVH, HD),
        preferred_element_type=jnp.float32,
    ) * HD ** (-0.5)
    grad_keys_all = jnp.einsum(
        "grcs,cgrd->sgd",
        grad_scores,
        queries.reshape(length, KVH, QH // KVH, HD),
        preferred_element_type=jnp.float32,
    ) * HD ** (-0.5)
    grad_values_all = jnp.einsum(
        "grcs,cgrd->sgd",
        prob_vals.astype(jnp.bfloat16),
        grad_heads,
        preferred_element_type=jnp.float32,
    )
    full_len = keys_all.shape[0]
    grad_keys, grad_values = (
        lax.psum_scatter(
            grad_keys_all.reshape(full_len, KVH * HD).astype(jnp.bfloat16),
            "shard",
            scatter_dimension=0,
            tiled=True,
        ).astype(jnp.float32),
        lax.psum_scatter(
            grad_values_all.reshape(full_len, KVH * HD).astype(jnp.bfloat16),
            "shard",
            scatter_dimension=0,
            tiled=True,
        ).astype(jnp.float32),
    )
    grad_query_pre = (
        rotate_back(grad_queries.reshape(length, QH, HD), cos_tab, sin_tab)
        .reshape(length, QH * HD)
        .astype(jnp.bfloat16)
    )
    grad_key_pre = (
        rotate_back(grad_keys.reshape(length, KVH, HD), cos_tab, sin_tab)
        .reshape(length, KVH * HD)
        .astype(jnp.bfloat16)
    )
    grad_value_pre = grad_values.astype(jnp.bfloat16)
    grad_normed = (
        times_trans(grad_query_pre, query_w)
        + times_trans(grad_key_pre, key_w)
        + times_trans(grad_value_pre, value_w)
    )
    wide_in = layer_in.astype(jnp.float32)
    grad_gain_attn, through_attn = norm_back(
        grad_normed, wide_in, row_scale(wide_in), gain_attn.astype(jnp.float32)
    )
    grad_input = grad_middle + through_attn
    operand_pairs = (
        (normed, grad_query_pre),
        (normed, grad_key_pre),
        (normed, grad_value_pre),
        (attended, grad_branch),
        (normed_ffn, grad_gate_pre),
        (normed_ffn, grad_up_pre),
        (hidden_act, grad_low),
    )
    return (grad_input.astype(jnp.bfloat16), (grad_gain_attn, grad_gain_ffn), operand_pairs)


def local(
    hidden_in,
    segment_ids,
    norm_attn,
    w_query,
    w_key,
    w_value,
    w_out,
    norm_ffn,
    w_gate,
    w_up,
    w_down,
    out_grad,
):
    section_pos = lax.axis_index("section")
    shard_pos = lax.axis_index("shard")
    is_first = section_pos == 0
    weights = (
        lax.all_gather(norm_attn[0], "shard", axis=0, tiled=True),
        lax.all_gather(w_query[0], "shard", axis=0, tiled=True),
        lax.all_gather(w_key[0], "shard", axis=0, tiled=True),
        lax.all_gather(w_value[0], "shard", axis=0, tiled=True),
        lax.all_gather(w_out[0], "shard", axis=0, tiled=True),
        lax.all_gather(norm_ffn[0], "shard", axis=0, tiled=True),
        lax.all_gather(w_gate[0], "shard", axis=0, tiled=True),
        lax.all_gather(w_up[0], "shard", axis=0, tiled=True),
        lax.all_gather(w_down[0], "shard", axis=0, tiled=True),
    )
    micro_count = hidden_in.shape[0]
    outputs = []
    kept_list = []
    sent_out = jnp.zeros_like(hidden_in[0, 0])
    for slot_num in range(micro_count + 1):
        early_mb = min(slot_num, micro_count - 1)
        late_mb = max(slot_num - 1, 0)
        segments = jnp.where(is_first, segment_ids[early_mb, 0], segment_ids[late_mb, 0])
        if slot_num > 0:
            arrived = passed_along(sent_out, "section", 1)
        else:
            arrived = jnp.zeros_like(sent_out)
        layer_in = jnp.where(is_first, hidden_in[early_mb, 0], arrived)
        sent_out, kept = forward_layer(layer_in, segments, weights, shard_pos)
        outputs.append(sent_out)
        kept_list.append((kept, segments))
    gain_totals = None
    pair_slots = []
    grad_slots = []
    sent_grad = jnp.zeros_like(out_grad[0, 0])
    for slot_num in range(micro_count + 1):
        if slot_num > 0:
            arrived = passed_along(sent_grad, "section", -1)
        else:
            arrived = jnp.zeros_like(sent_grad)
        grad_low = jnp.where(is_first, arrived, out_grad[min(slot_num, micro_count - 1), 0])
        kept, segments = jax.tree.map(
            lambda earlier, later: jnp.where(is_first, earlier, later),
            kept_list[max(slot_num - 1, 0)],
            kept_list[min(slot_num + 1, micro_count)],
        )
        live_flag = jnp.where(
            is_first, 1.0 if slot_num > 0 else 0.0, 1.0 if slot_num < micro_count else 0.0
        ).astype(jnp.float32)
        sent_grad, gain_grads, operand_pairs = backward_layer(
            grad_low, segments, weights, kept, shard_pos
        )
        gain_grads = tuple((piece_grad * live_flag for piece_grad in gain_grads))
        live_low = live_flag.astype(jnp.bfloat16)
        pair_slots.append(
            tuple(((left_rows, right_rows * live_low) for left_rows, right_rows in operand_pairs))
        )
        if gain_totals is None:
            gain_totals = gain_grads
        else:
            gain_totals = tuple(
                (total_val + piece_grad for total_val, piece_grad in zip(gain_totals, gain_grads))
            )
        grad_slots.append(sent_grad)
    products = []
    for which in range(7):
        left_all = jnp.concatenate([pairs[which][0] for pairs in pair_slots], axis=0)
        right_all = jnp.concatenate([pairs[which][1] for pairs in pair_slots], axis=0)
        products.append(outer_sum(left_all, right_all))
    totals = (
        gain_totals[0],
        products[0],
        products[1],
        products[2],
        products[3],
        gain_totals[1],
        products[4],
        products[5],
        products[6],
    )
    layer_out = jnp.stack(
        [
            jnp.where(is_first, outputs[index_mb], outputs[index_mb + 1])
            for index_mb in range(micro_count)
        ]
    )[None, :, None]
    input_grad = jnp.stack(
        [
            jnp.where(is_first, grad_slots[index_mb + 1], grad_slots[index_mb])
            for index_mb in range(micro_count)
        ]
    )[None, :, None]
    pieces = (
        lax.psum_scatter(totals[0], ("shard", "replica"), scatter_dimension=0, tiled=True),
        lax.psum_scatter(totals[1], ("shard", "replica"), scatter_dimension=0, tiled=True),
        lax.psum_scatter(totals[2], ("shard", "replica"), scatter_dimension=0, tiled=True),
        lax.psum_scatter(totals[3], ("shard", "replica"), scatter_dimension=0, tiled=True),
        lax.psum_scatter(totals[4], ("shard", "replica"), scatter_dimension=0, tiled=True),
        lax.psum_scatter(totals[5], ("shard", "replica"), scatter_dimension=0, tiled=True),
        lax.psum_scatter(totals[6], ("shard", "replica"), scatter_dimension=0, tiled=True),
        lax.psum_scatter(totals[7], ("shard", "replica"), scatter_dimension=0, tiled=True),
        lax.psum_scatter(totals[8], ("shard", "replica"), scatter_dimension=0, tiled=True),
    )
    summed = (
        lax.all_gather(pieces[0].astype(jnp.bfloat16), "replica", axis=0, tiled=True).astype(
            jnp.float32
        ),
        lax.all_gather(pieces[1].astype(jnp.bfloat16), "replica", axis=0, tiled=True).astype(
            jnp.float32
        ),
        lax.all_gather(pieces[2].astype(jnp.bfloat16), "replica", axis=0, tiled=True).astype(
            jnp.float32
        ),
        lax.all_gather(pieces[3].astype(jnp.bfloat16), "replica", axis=0, tiled=True).astype(
            jnp.float32
        ),
        lax.all_gather(pieces[4].astype(jnp.bfloat16), "replica", axis=0, tiled=True).astype(
            jnp.float32
        ),
        lax.all_gather(pieces[5].astype(jnp.bfloat16), "replica", axis=0, tiled=True).astype(
            jnp.float32
        ),
        lax.all_gather(pieces[6].astype(jnp.bfloat16), "replica", axis=0, tiled=True).astype(
            jnp.float32
        ),
        lax.all_gather(pieces[7].astype(jnp.bfloat16), "replica", axis=0, tiled=True).astype(
            jnp.float32
        ),
        lax.all_gather(pieces[8].astype(jnp.bfloat16), "replica", axis=0, tiled=True).astype(
            jnp.float32
        ),
    )
    return (
        layer_out,
        input_grad,
        summed[0][None],
        summed[1][None],
        summed[2][None],
        summed[3][None],
        summed[4][None],
        summed[5][None],
        summed[6][None],
        summed[7][None],
        summed[8][None],
    )


def solution(mesh):
    placed = (
        P(None, "replica", "shard", None),
        P(None, "replica", None),
        P("section", "shard"),
        P("section", "shard", None),
        P("section", "shard", None),
        P("section", "shard", None),
        P("section", "shard", None),
        P("section", "shard"),
        P("section", "shard", None),
        P("section", "shard", None),
        P("section", "shard", None),
        P(None, "replica", "shard", None),
    )
    return jax.shard_map(
        local,
        mesh=mesh,
        in_specs=placed,
        out_specs=(
            P("section", None, "replica", "shard", None),
            P("section", None, "replica", "shard", None),
            P("section", "shard"),
            P("section", "shard", None),
            P("section", "shard", None),
            P("section", "shard", None),
            P("section", "shard", None),
            P("section", "shard"),
            P("section", "shard", None),
            P("section", "shard", None),
            P("section", "shard", None),
        ),
        check_vma=False,
    )
```

profile of v0, /device:TPU:0, one launch (start us, length us, event | category | flops | bytes accessed | tf_op | source)
XLA Modules:
  0.0 1799.2 jit_solution(1458240660427917498)
XLA Ops:
  13.6 13.7 all-reduce.20
  39.3 40.4 %all-gather.1 = bf16[1,960,320]{2,0,1:T(2,128)(2,1)S(1)} all-gather(bf16[1,240,320]{2,0,1:T(2,128)(2,1)S(1)} %copy.237), channel_id=3, replica_groups=mesh['section'=2,'shard'=4,'replica'=4] {'shard'}, dimensions={1}, use_global_device_ids=true | all-gather | bytes 768000 | tf_op jit(solution)/shard_map/all_gather | solution.py:267
  82.6 15.3 all_gather.74
  98.7 44.2 %all-gather.2 = bf16[1,960,320]{2,0,1:T(2,128)(2,1)S(1)} all-gather(bf16[1,240,320]{2,0,1:T(2,128)(2,1)S(1)} %copy.240), channel_id=4, replica_groups=mesh['section'=2,'shard'=4,'replica'=4] {'shard'}, dimensions={1}, use_global_device_ids=true | all-gather | bytes 768000 | tf_op jit(solution)/shard_map/all_gather | solution.py:266
  146.0 17.4 all_gather.76
  165.0 2.9 copy.244
  175.0 58.2 %all-gather.30.cloned.1.call-done = bf16[1,960,2560]{2,1,0:T(8,128)(2,1)} async-done(((bf16[1,240,2560]{2,1,0:T(8,128)(2,1)}), bf16[1,960,2560]{2,1,0:T(8,128)(2,1)}) %all-gather.30.cloned.1.call-update) | async-done | bytes 4915216 | tf_op jit(solution)/shard_map/all_gather | solution.py:270
  233.1 3.4 fusion.40
  236.6 89.5 %all-gather.32.cloned.1.call-done = bf16[1,960,2560]{2,1,0:T(8,128)(2,1)} async-done(((bf16[1,240,2560]{2,1,0:T(8,128)(2,1)}), bf16[1,960,2560]{2,1,0:T(8,128)(2,1)}) %all-gather.32.cloned.1.call-update) | async-done | bytes 4915216 | tf_op jit(solution)/shard_map/all_gather | solution.py:271
  326.1 4.3 multiply_convert_fusion.11
  330.4 88.3 %all-gather.34.cloned.1.call-done = bf16[1,2560,960]{1,2,0:T(8,128)(2,1)} async-done(((bf16[1,640,960]{1,2,0:T(8,128)(2,1)}), bf16[1,2560,960]{1,2,0:T(8,128)(2,1)}) %all-gather.34.cloned.1.call-update) | async-done | bytes 4915216 | tf_op jit(solution)/shard_map/all_gather | solution.py:272
  418.7 4.1 fusion.124
  435.2 14.9 all_gather.83
  457.7 14.3 all_gather.84
  490.7 2.5 broadcast_multiply_fusion.6
  502.7 13.8 all_gather.85
  519.4 14.2 all_gather.86
  592.7 4.2 fusion.36
  596.9 4.2 fusion.24
  608.4 14.5 reduce-scatter.36.cloned.1.call-done
  629.9 4.0 multiply_convert_fusion.6
  659.0 8.4 reduce-scatter.38.cloned.1.call-done
  673.3 14.0 reduce-scatter.40.cloned.1.call-done
  696.6 5.6 broadcast_multiply_fusion.4
  724.4 6.7 fusion.154
  759.6 3.9 fusion.191
  765.7 5.2 fusion.142
  770.9 5.2 fusion.148
  785.4 2.6 fusion.185
  788.0 845.9 %fusion.322 = (f32[64,960]{1,0:T(8,128)S(1)}, f32[64,320]{1,0:T(8,128)S(1)}, f32[64,320]{1,0:T(8,128)S(1)}, f32[64,960]{1,0:T(8,128)}, f32[64,2560]{1,0:T(8,128)}, /*index=5*/f32[64,2560]{1,0:T(8,128)}) fusion(f32[960,960]{1,0:T(8,128)} %fusion.185, f32[960,320]{1,0:T(8,128)S(1)} %fusion.256, f32[960,320]{1,0:T(8,128)S(1)} %fusion.262, ...), kind=kCustom, calls=%all-reduce-scatter.6 | all-reduce-scatter fusion | flops 7864321 | bytes 31457792
  1638.6 5.0 collective-permute-done.8
  1643.6 4.0 concatenate.209
  1649.7 5.2 collective-permute-start.9
  1654.9 8.2 collective-permute-done.9
  1663.1 2.4 concatenate.210
  1670.6 4.3 fusion.139
  1675.7 4.5 collective-permute-start.6
  1684.1 5.6 collective-permute-start.4
  1690.5 37.5 %all-reduce.18 = (bf16[960]{0:T(1024)(128)(2,1)S(1)}, bf16[960]{0:T(1024)(128)(2,1)S(1)}) all-reduce(f32[960]{0:T(1024)S(1)} %multiply_add_fusion.1, f32[960]{0:T(1024)S(1)} %multiply_add_fusion), channel_id=17, replica_groups=mesh['section'=2,'shard'=4,'replica'=4] {'shard','replica'}, use_global_device_ids=true, to_apply=%region_42.43.clone | all-reduce | flops 1920 | bytes 11520
  1728.6 9.3 all-reduce.19
  1739.4 9.6 all-gather.11
  1750.2 7.4 all-gather.10
  1758.9 10.7 all-gather.12
  1771.0 8.5 all-gather.9
  1780.6 2.6 reshape.1112
  1783.3 2.6 reshape.1113
  1785.9 3.2 bitcast_convert_fusion
  1789.1 3.2 copy.310
  (719 shorter events, 279.5 us)
Async XLA Ops:
  7.2 157.7 %all-gather.26.cloned.1.call-start = ((), (), s32[]{:S(2)}) async-start(), calls=%async_computation.9 | async-start | bytes 2457600 | tf_op jit(solution)/shard_map/all_gather | solution.py:265
  8.0 164.8 %all-gather.28.cloned.1.call-start = ((), (), s32[]{:S(2)}) async-start(), calls=%async_computation.10 | async-start | bytes 2457600 | tf_op jit(solution)/shard_map/all_gather | solution.py:268
  8.7 224.4 %all-gather.30.cloned.1.call-start = ((), (), s32[]{:S(2)}) async-start(), calls=%async_computation.11 | async-start | bytes 6144000 | tf_op jit(solution)/shard_map/all_gather | solution.py:270
  9.5 316.7 %all-gather.32.cloned.1.call-start = ((), (), s32[]{:S(2)}) async-start(), calls=%async_computation.12 | async-start | bytes 6144000 | tf_op jit(solution)/shard_map/all_gather | solution.py:271
  10.0 408.6 %all-gather.34.cloned.1.call-start = ((), (), s32[]{:S(2)}) async-start(), calls=%async_computation.13 | async-start | bytes 6144000 | tf_op jit(solution)/shard_map/all_gather | solution.py:272
  10.6 592.4 %reduce-scatter.34.cloned.1.call-start = ((), (), s32[]{:S(2)}) async-start(), calls=%async_computation.16 | async-start | bytes 245760
  36.5 45.5 %copy-start.18 = (bf16[2,1,64,960]{3,2,1,0:T(8,128)(2,1)S(1)}, bf16[2,1,64,960]{3,2,1,0:T(8,128)(2,1)}, u32[]{:S(2)}) copy-start(bf16[2,1,64,960]{3,2,1,0:T(8,128)(2,1)} %param.12) | copy-start | bytes 737284
  82.2 85.7 %copy-start.141 = (f32[64]{0:T(128)}, f32[64]{0:T(128)S(1)}, u32[]{:S(2)}) copy-start(f32[64]{0:T(128)S(1)} %add_rsqrt_fusion.11) | copy-start | bytes 772
  82.2 82.0 %copy-start.145 = (s32[64]{0:T(128)S(1)}, s32[64]{0:T(128)}, u32[]{:S(2)}) copy-start(s32[64]{0:T(128)} %copy-done.144) | copy-start | bytes 772
  82.2 82.0 %copy-start.147 = (s32[64]{0:T(128)S(1)}, s32[64]{0:T(128)}, u32[]{:S(2)}) copy-start(s32[64]{0:T(128)} %copy-done.146) | copy-start | bytes 772
  82.2 82.0 %copy-start.149 = (s32[64]{0:T(128)S(1)}, s32[64]{0:T(128)}, u32[]{:S(2)}) copy-start(s32[64]{0:T(128)} %copy-done.148) | copy-start | bytes 772
  82.2 82.0 %copy-start.151 = (s32[64]{0:T(128)S(1)}, s32[64]{0:T(128)}, u32[]{:S(2)}) copy-start(s32[64]{0:T(128)} %copy-done.150) | copy-start | bytes 772
  97.9 67.1 %copy-start.46 = (bf16[256,320]{1,0:T(8,128)(2,1)}, bf16[256,320]{1,0:T(8,128)(2,1)S(1)}, u32[]{:S(2)}) copy-start(bf16[256,320]{1,0:T(8,128)(2,1)S(1)} %all_gather.74) | copy-start | bytes 491524
  145.3 356.3 %copy-start.6 = (bf16[1,960,320]{1,2,0:T(8,128)(2,1)}, bf16[1,960,320]{1,2,0:T(8,128)(2,1)S(1)}, u32[]{:S(2)}) copy-start(bf16[1,960,320]{1,2,0:T(8,128)(2,1)S(1)} %copy.241) | copy-start | bytes 1843204
  172.2 64.4 %copy-start.131 = (f32[5,3,64]{2,1,0:T(4,128)}, f32[5,3,64]{2,1,0:T(4,128)S(1)}, u32[]{:S(2)}) copy-start(f32[5,3,64]{2,1,0:T(4,128)S(1)} %fusion.160) | copy-start | bytes 11524
  172.7 63.9 %copy-start.77 = (bf16[5,64,3,64]{3,1,2,0:T(8,128)(2,1)}, bf16[5,64,3,64]{3,1,2,0:T(8,128)(2,1)S(1)}, u32[]{:S(2)}) copy-start(bf16[5,64,3,64]{3,1,2,0:T(8,128)(2,1)S(1)} %convolution_convert_fusion.2) | copy-start | bytes 368644
  174.9 243.7 %copy-start.8 = (f32[64,960]{1,0:T(8,128)}, f32[64,960]{1,0:T(8,128)S(1)}, u32[]{:S(2)}) copy-start(f32[64,960]{1,0:T(8,128)S(1)} %get-tuple-element.230) | copy-start | bytes 737284
  236.6 182.1 %copy-start.15 = (f32[64,2560]{1,0:T(8,128)}, f32[64,2560]{1,0:T(8,128)S(1)}, u32[]{:S(2)}) copy-start(f32[64,2560]{1,0:T(8,128)S(1)} %fusion.40) | copy-start | bytes 1966084
  330.4 88.3 %copy-start.53 = (bf16[64,2560]{1,0:T(8,128)(2,1)}, bf16[64,2560]{1,0:T(8,128)(2,1)S(1)}, u32[]{:S(2)}) copy-start(bf16[64,2560]{1,0:T(8,128)(2,1)S(1)} %get-tuple-element.231) | copy-start | bytes 983044
  422.8 3.8 collective-permute-start
  431.3 48.7 %copy-start.120 = (f32[64,64]{1,0:T(8,128)S(1)}, f32[64,64]{1,0:T(8,128)}, u32[]{:S(2)}) copy-start(f32[64,64]{1,0:T(8,128)} %copy.266) | copy-start | bytes 49156
  494.8 4.2 collective-permute-start.1
  501.3 35.9 %copy-start.139 = (f32[64]{0:T(128)}, f32[64]{0:T(128)S(1)}, u32[]{:S(2)}) copy-start(f32[64]{0:T(128)S(1)} %add_rsqrt_fusion.7) | copy-start | bytes 772
  584.1 38.8 %reduce-scatter.36.cloned.1.call-start = ((), (), s32[]{:S(2)}) async-start(), calls=%async_computation.17 | async-start | bytes 245760
  590.9 76.4 %reduce-scatter.38.cloned.1.call-start = ((), (), s32[]{:S(2)}) async-start(), calls=%async_computation.18 | async-start | bytes 245760
  625.7 3.2 collective-permute-start.2
  649.5 37.9 %reduce-scatter.40.cloned.1.call-start = ((), (), s32[]{:S(2)}) async-start(), calls=%async_computation.19 | async-start | bytes 245760
  652.8 34.6 %copy-start.143 = (f32[64]{0:T(128)S(1)}, f32[64]{0:T(128)}, u32[]{:S(2)}) copy-start(f32[64]{0:T(128)} %add_rsqrt_fusion.2) | copy-start | bytes 772
  655.7 120.5 %reduce-scatter.42.cloned.1.call-start = ((), (), s32[]{:S(2)}) async-start(), calls=%async_computation.20 | async-start | bytes 245760
  657.6 35.4 %copy-start.158 = (f32[64]{0:T(128)S(1)}, f32[64]{0:T(128)}, u32[]{:S(2)}) copy-start(f32[64]{0:T(128)} %get-tuple-element.123) | copy-start | bytes 772
  691.6 3.2 collective-permute-start.3
  718.3 59.6 %reduce-scatter.44.cloned.1.call-start = ((), (), s32[]{:S(2)}) async-start(), calls=%async_computation.21 | async-start | bytes 245760
  724.1 944.5 %reduce-scatter.32.cloned.1.call-start = ((), (), s32[]{:S(2)}) async-start(), calls=%async_computation.7 | async-start | bytes 11141120 | tf_op jit(solution)/shard_map/reduce_scatter | solution.py:360
  731.2 1049.5 %all-gather.36.cloned.1.call-start = ((), (), s32[]{:S(2)}) async-start(), calls=%async_computation.14 | async-start | bytes 1638400 | tf_op jit(solution)/shard_map/all_gather | solution.py:381
  788.0 849.3 %copy-start.153 = (u32[32]{0:T(128)S(1)}, u32[32]{0:T(128)}, u32[]{:S(2)}) copy-start(u32[32]{0:T(128)} %constant.99) | copy-start | bytes 388
  1633.9 33.4 %copy-start.159 = (u32[32]{0:T(128)S(1)}, u32[32]{0:T(128)}, u32[]{:S(2)}) copy-start(u32[32]{0:T(128)} %constant.85) | copy-start | bytes 388
  1633.9 36.6 %copy-start.64 = (bf16[64,960]{1,0:T(8,128)(2,1)S(1)}, bf16[64,960]{1,0:T(8,128)(2,1)}, u32[]{:S(2)}) copy-start(bf16[64,960]{1,0:T(8,128)(2,1)} %copy-done.63) | copy-start | bytes 368644
  1633.9 36.6 %copy-start.92 = (bf16[64,960]{1,0:T(8,128)(2,1)S(1)}, bf16[64,960]{1,0:T(8,128)(2,1)}, u32[]{:S(2)}) copy-start(bf16[64,960]{1,0:T(8,128)(2,1)} %copy-done.91) | copy-start | bytes 368644
  1635.2 35.4 %copy-start.41 = (f32[64,960]{1,0:T(8,128)S(1)}, f32[64,960]{1,0:T(8,128)}, u32[]{:S(2)}) copy-start(f32[64,960]{1,0:T(8,128)} %copy-done.40) | copy-start | bytes 737284
  1635.2 35.4 %copy-start.56 = (bf16[64,2560]{1,0:T(8,128)(2,1)S(1)}, bf16[64,2560]{1,0:T(8,128)(2,1)}, u32[]{:S(2)}) copy-start(bf16[64,2560]{1,0:T(8,128)(2,1)} %get-tuple-element.141) | copy-start | bytes 983044
  1635.2 8.4 collective-permute-start.8
  1648.5 134.8 %all-gather.38.cloned.1.call-start = ((), (), s32[]{:S(2)}) async-start(), calls=%async_computation.15 | async-start | bytes 1638400 | tf_op jit(solution)/shard_map/all_gather | solution.py:384
  1649.7 13.4 collective-permute-start.9
  1666.4 119.5 %all-gather.24.cloned.1.call-start = ((), (), s32[]{:S(2)}) async-start(), calls=%async_computation.8 | async-start | bytes 1638400 | tf_op jit(solution)/shard_map/all_gather | solution.py:387
  1675.7 63.4 %collective-permute-start.6 = (bf16[60,320]{1,0:T(8,128)(2,1)S(1)}, bf16[60,320]{1,0:T(8,128)(2,1)S(1)}, u32[]{:S(2)}, u32[]{:S(2)}) collective-permute-start(bf16[60,320]{1,0:T(8,128)(2,1)S(1)} %slice.152), channel_id=1, source_target_pairs={{0,1},{1,2},{2,3},{3,4},{4,5},{5,6},{6,7},{7,8},{8,9},{9,10},{10,1... | collective-permute-start | bytes 115208
  1680.2 69.7 %collective-permute-start.5 = (bf16[60,320]{1,0:T(8,128)(2,1)S(1)}, bf16[60,320]{1,0:T(8,128)(2,1)S(1)}, u32[]{:S(2)}, u32[]{:S(2)}) collective-permute-start(bf16[60,320]{1,0:T(8,128)(2,1)S(1)} %slice.151), channel_id=1, source_target_pairs={{0,1},{1,2},{2,3},{3,4},{4,5},{5,6},{6,7},{7,8},{8,9},{9,10},{10,1... | collective-permute-start | bytes 115208
  1682.2 76.4 %collective-permute-start.7 = (bf16[60,960]{1,0:T(8,128)(2,1)S(1)}, bf16[60,960]{1,0:T(8,128)(2,1)S(1)}, u32[]{:S(2)}, u32[]{:S(2)}) collective-permute-start(bf16[60,960]{1,0:T(8,128)(2,1)S(1)} %slice.153), channel_id=1, source_target_pairs={{0,1},{1,2},{2,3},{3,4},{4,5},{5,6},{6,7},{7,8},{8,9},{9,10},{10,1... | collective-permute-start | bytes 345608
  1684.1 86.6 %collective-permute-start.4 = (bf16[60,960]{1,0:T(8,128)(2,1)S(1)}, bf16[60,960]{1,0:T(8,128)(2,1)S(1)}, u32[]{:S(2)}, u32[]{:S(2)}) collective-permute-start(bf16[60,960]{1,0:T(8,128)(2,1)S(1)} %slice.150), channel_id=1, source_target_pairs={{0,1},{1,2},{2,3},{3,4},{4,5},{5,6},{6,7},{7,8},{8,9},{9,10},{10,1... | collective-permute-start | bytes 345608
  (154 other events, 971.1 us)
Sparse Core Ops, SparseCore 0:
  9.6 63.2 all-gather.25
  74.5 64.0 all-gather.27
  140.1 92.9 all-gather.29
  234.6 91.5 all-gather.31
  327.5 91.0 all-gather.33
  584.2 18.7 reduce-scatter.33
  605.4 17.4 reduce-scatter.35
  649.6 17.7 reduce-scatter.37
  669.7 17.6 reduce-scatter.39
  718.4 17.5 reduce-scatter.41
  738.3 17.6 reduce-scatter.43
  758.2 438.3 reduce-scatter.31
  1648.6 34.1 all-gather.35
  1685.1 29.8 all-gather.37
  1716.6 30.4 all-gather.23
where the time goes:
time: 1810 us; the launch traced here: 1800 us
  blocking collectives  1120 us (62%)
  waiting for transfers between devices  293 us (16%)
  local copies, waits for them, and re-layouts  141 us (8%)
  matrix products  135 us (7%)
  other arithmetic  65.1 us (4%)
  starting transfers between devices  28.5 us (2%)
  between operations  19.7 us (1%)
    unnamed x4, blocking collectives  907 us
    all_gather x1, waiting for transfers between devices, local(): lax.all_gather(w_up[0], 'shard', axis=0, tiled=True)  89.5 us
    all_gather x1, waiting for transfers between devices, local(): lax.all_gather(w_down[0], 'shard', axis=0, tiled=True)  88.3 us
    all_gather x1, waiting for transfers between devices, local(): lax.all_gather(w_gate[0], 'shard', axis=0, tiled=True)  58.2 us
    unnamed x27, waiting for transfers between devices  53.9 us
    unnamed x402, local copies, waits for them, and re-layouts  47.9 us
    all_gather x3, blocking collectives, forward_layer(): lax.all_gather(keys_own, 'shard', axis=0, tiled=True)  46 us
    all_gather x1, blocking collectives, local(): lax.all_gather(w_key[0], 'shard', axis=0, tiled=True)  44.2 us
  transfers between devices with their start and end apart: 25, of which 11 were waited for; matrix products, arithmetic and copies ran while one was open for 57% of the time, Pallas kernels for 0%

commit v1 on v0

v1 whole, which is shorter than its diff:
```python
import jax
import jax.numpy as jnp
from jax import lax
from jax.sharding import PartitionSpec as P

QH = 15
KVH = 5
HD = 64
TEAM = 4

rope_base = 100000.0
norm_eps = 1e-05
mask_fill = -1000000000.0

low = jnp.bfloat16
wide = jnp.float32


def dot(a, b):
    return jnp.dot(a, b, preferred_element_type=wide)


def dot_t(a, b):
    return lax.dot_general(a, b, (((1,), (1,)), ((), ())), preferred_element_type=wide)


def dot_l(a, b):
    return lax.dot_general(a, b, (((0,), (0,)), ((), ())), preferred_element_type=wide)


def to_core(value, target):
    return lax.ppermute(value, "section", [(1 - target, target)])


def swap(value):
    return lax.ppermute(value, "section", [(0, 1), (1, 0)])


def z_send(value, hop, core=None):
    count = lax.axis_size("shard")
    cores = range(lax.axis_size("section")) if core is None else (core,)
    pairs = [(c * count + z, c * count + (z + hop) % count) for c in cores for z in range(count)]
    return lax.ppermute(value, ("section", "shard"), pairs)


def plane_send(value, flip, core=None):
    count = lax.axis_size("replica")
    cores = range(lax.axis_size("section")) if core is None else (core,)
    pairs = [(c * count + r, c * count + (r ^ flip)) for c in cores for r in range(count)]
    return lax.ppermute(value, ("section", "replica"), pairs)


def pick(stack, index):
    return lax.dynamic_index_in_dim(stack, index, 0, keepdims=False)


def place(parts):
    stack = jnp.zeros((len(parts),) + parts[0][1].shape, parts[0][1].dtype)
    for index, block in parts:
        stack = lax.dynamic_update_index_in_dim(stack, block, index, 0)
    return stack


def z_gather(block, z, core=None):
    return place([(z, block)] + [((z - hop) % 4, z_send(block, hop, core)) for hop in (1, 2, 3)])


def z_trade(stack, z, core=None):
    return [(z, pick(stack, z))] + [
        ((z - hop) % 4, z_send(pick(stack, (z + hop) % 4), hop, core)) for hop in (1, 2, 3)
    ]


def plane_gather(block, q, core=None):
    return place([(q, block)] + [(q ^ flip, plane_send(block, flip, core)) for flip in (1, 2, 3)])


def plane_trade(stack, q, core=None):
    return place(
        [(q, pick(stack, q))]
        + [(q ^ flip, plane_send(pick(stack, q ^ flip), flip, core)) for flip in (1, 2, 3)]
    )


def plane_sum(partial):
    half = partial.shape[0] // 2
    first, second = partial[:half].astype(low), partial[half:].astype(low)

    def both(mine, flip):
        return mine.astype(wide) + plane_send(mine, flip).astype(wide)

    first, second = both(first, 1).astype(low), both(second, 2).astype(low)
    return jnp.concatenate([both(first, 2), both(second, 1)])


def teams_sum(value):
    flip = TEAM
    while flip < lax.axis_size("replica"):
        sent = value.astype(low)
        value = sent.astype(wide) + plane_send(sent, flip).astype(wide)
        flip *= 2
    return value


def after(value, earlier):
    return lax.optimization_barrier((value, earlier))[0]


def tables(segments):
    count = segments.shape[0]
    rows = jnp.arange(count, dtype=jnp.int32)
    before = jnp.sum((segments[None, :] < segments[:, None]).astype(jnp.int32), axis=1)
    allowed = (segments[None, :] == segments[:, None]) & (rows[None, :] <= rows[:, None])
    frequency = rope_base ** (-jnp.arange(HD // 2).astype(wide) * (2.0 / HD))
    angles = (rows - before).astype(wide)[:, None] * frequency[None, :]
    angles = jnp.concatenate([angles, angles], axis=1)
    return allowed, jnp.cos(angles)[:, None, :], jnp.sin(angles)[:, None, :]


def rotate_fwd(values, cos_tab, sin_tab):
    half = HD // 2
    turned = jnp.concatenate([-values[..., half:], values[..., :half]], axis=-1)
    return values * cos_tab + turned * sin_tab


def rotate_back(values, cos_tab, sin_tab):
    half = HD // 2
    shifted = values * sin_tab
    return values * cos_tab + jnp.concatenate([shifted[..., half:], -shifted[..., :half]], axis=-1)


def row_scale(values):
    return lax.rsqrt(jnp.mean(values * values, axis=-1, keepdims=True) + norm_eps)


def norm_back(grad_normed, values, gain):
    factor = row_scale(values)
    gain_grad = jnp.sum(grad_normed * values * factor, axis=0)
    weighted = grad_normed * gain
    inner = jnp.mean(weighted * values, axis=-1, keepdims=True)
    return gain_grad, factor * weighted - values * factor * factor * factor * inner


def attention_fwd(layer_in, tabs, attn_w, gain):
    allowed, cos_tab, sin_tab = tabs
    count = layer_in.shape[0]
    x = layer_in.astype(wide)
    normed = (x * row_scale(x) * gain).astype(low)
    mixed = dot(normed, attn_w[1])
    query_pre = jnp.concatenate([dot(normed, attn_w[0]), mixed[:, :320]], axis=1)
    queries = rotate_fwd(query_pre.reshape(count, QH, HD), cos_tab, sin_tab).astype(low)
    queries = queries.reshape(count, KVH, QH // KVH, HD)
    keys = rotate_fwd(mixed[:, 320:].reshape(count, KVH, HD), cos_tab, sin_tab).astype(low)
    values = dot(normed, attn_w[2][:, :320]).astype(low).reshape(count, KVH, HD)
    scores = jnp.einsum("cgrd,sgd->grcs", queries, keys, preferred_element_type=wide) * HD**-0.5
    scores = jnp.where(allowed[None, None], scores, mask_fill)
    exponent = jnp.exp(scores - jnp.max(scores, axis=-1, keepdims=True))
    probs = exponent / jnp.sum(exponent, axis=-1, keepdims=True)
    attended = jnp.einsum("grcs,sgd->cgrd", probs.astype(low), values, preferred_element_type=wide)
    attended = attended.reshape(count, QH * HD).astype(low)
    branch = jnp.concatenate([dot(attended, attn_w[2][:, 320:]), dot(attended, attn_w[3])], axis=1)
    return x + branch, (normed, queries, keys, values, probs, attended)


def attention_back(layer_in, grad_middle, tabs, attn_w, gain, kept):
    allowed, cos_tab, sin_tab = tabs
    normed, queries, keys, values, probs, attended = kept
    count = layer_in.shape[0]
    branch = grad_middle.astype(low)
    grad_att = dot_t(branch[:, :320], attn_w[2][:, 320:]) + dot_t(branch[:, 320:], attn_w[3])
    grad_att = grad_att.astype(low).reshape(count, KVH, QH // KVH, HD)
    grad_probs = jnp.einsum("cgrd,sgd->grcs", grad_att, values, preferred_element_type=wide)
    centre = jnp.sum(probs * grad_probs, axis=-1, keepdims=True)
    grad_scores = (probs * (grad_probs - centre)).astype(low)
    scale = HD**-0.5
    grad_q = jnp.einsum("grcs,sgd->cgrd", grad_scores, keys, preferred_element_type=wide) * scale
    grad_k = jnp.einsum("grcs,cgrd->sgd", grad_scores, queries, preferred_element_type=wide) * scale
    grad_v = jnp.einsum(
        "grcs,cgrd->sgd", probs.astype(low), grad_att, preferred_element_type=wide
    )
    grad_q = rotate_back(grad_q.reshape(count, QH, HD), cos_tab, sin_tab).astype(low)
    grad_k = rotate_back(grad_k, cos_tab, sin_tab).astype(low)
    pieces = [
        grad_q.reshape(count, QH * HD),
        grad_k.reshape(count, KVH * HD),
        grad_v.astype(low).reshape(count, KVH * HD),
        branch,
    ]
    right = jnp.concatenate(pieces, axis=1)
    grad_normed = (
        dot_t(right[:, :640], attn_w[0])
        + dot_t(right[:, 640:1280], attn_w[1])
        + dot_t(right[:, 1280:1600], attn_w[2][:, :320])
    )
    x = layer_in.astype(wide)
    gain_grad, through = norm_back(grad_normed, x, gain)
    return grad_middle + through, right, gain_grad


def local(
    hidden_in,
    segment_ids,
    norm_attn,
    w_query,
    w_key,
    w_value,
    w_out,
    norm_ffn,
    w_gate,
    w_up,
    w_down,
    out_grad,
):
    core = lax.axis_index("section")
    z = lax.axis_index("shard")
    replica = lax.axis_index("replica")
    q = replica % TEAM
    layers = 2
    group, width = hidden_in.shape[2], hidden_in.shape[3]

    chunk = (w_query.shape[2] * 2 + w_key.shape[2] * 2) // TEAM
    hid = w_gate.shape[2] // TEAM
    down_rows = w_down.shape[1] // TEAM
    attn_all = jnp.concatenate([w_query[0], w_key[0], w_value[0], w_out[0]], axis=1)
    attn_share = lax.dynamic_slice_in_dim(attn_all, q * chunk, chunk, axis=1)
    ffn_share = jnp.concatenate(
        [
            lax.dynamic_slice_in_dim(w_gate[0], q * hid, hid, axis=1),
            lax.dynamic_slice_in_dim(w_up[0], q * hid, hid, axis=1),
        ],
        axis=1,
    )
    down_share = lax.dynamic_slice_in_dim(w_down[0], q * down_rows, down_rows, axis=0)

    def give(value, owner):
        return jnp.where(core == owner, value, to_core(value, 1 - owner))

    def load_attn(owner, share):
        rows = z_gather(share, z, owner).reshape(-1, chunk)
        return give(plane_gather(rows, q, owner), owner)

    def load_ffn(owner, share):
        return give(z_gather(share, z, owner).reshape(-1, 2 * hid), owner)

    def load_down(owner, share):
        blocks = plane_trade(z_gather(share, z, owner), q, owner)
        return give(blocks.reshape(-1, width), owner)

    def whole_sequence(shares):
        mine = pick(shares[:, 0], core)
        blocks = plane_gather(mine, q)
        return place(z_trade(blocks, z)).reshape(-1, width)

    hidden = whole_sequence(hidden_in)
    segments = pick(plane_gather(pick(segment_ids[:, 0], core), q), z)
    tabs = tables(segments)
    own_gains = jnp.concatenate([norm_attn, norm_ffn], axis=0)
    own_gains = z_gather(own_gains, z).transpose(1, 0, 2).reshape(2, -1).astype(wide)
    other_gains = swap(own_gains.astype(low)).astype(wide)
    gains = [jnp.where(core == layer, own_gains, other_gains) for layer in range(layers)]

    attn_w, ffn_w, down_w = [None] * 2, [None] * 2, [None] * 2
    attn_w[0] = load_attn(0, attn_share)
    ffn_w[0] = load_ffn(0, ffn_share)
    down_w[0] = load_down(0, down_share)
    attn_w[1] = load_attn(1, after(attn_share, attn_w[0]))
    ffn_w[1] = load_ffn(1, after(ffn_share, ffn_w[0]))
    down_w[1] = load_down(1, after(down_share, down_w[0]))
    top_grad = whole_sequence(after(out_grad, attn_w[0]))

    inputs, kept, outputs = [hidden], [], []
    for layer in range(layers):
        middle, kept_attn = attention_fwd(inputs[layer], tabs, attn_w[layer], gains[layer][0])
        normed = (middle * row_scale(middle) * gains[layer][1]).astype(low)
        both = dot(normed, ffn_w[layer])
        gate, up = both[:, :hid], both[:, hid:]
        act = (gate * jax.nn.sigmoid(gate) * up).astype(low)
        kept.append((kept_attn, middle, normed, gate, up, act))
        result = (middle + plane_sum(dot(act, down_w[layer]))).astype(low)
        outputs.append(result)
        inputs.append(result)

    gain_grads, input_grads, sums = [None] * 2, [None] * 2, [None] * 2
    grad = top_grad
    for layer in reversed(range(layers)):
        kept_attn, middle, normed, gate, up, act = kept[layer]
        grad_act = dot_t(grad, down_w[layer])
        sig = jax.nn.sigmoid(gate)
        grad_gate = (grad_act * up * sig * (1.0 + gate * (1.0 - sig))).astype(low)
        grad_up = (grad_act * gate * sig).astype(low)
        grad_both = jnp.concatenate([grad_gate, grad_up], axis=1)
        grad_normed = plane_sum(dot_t(grad_both, ffn_w[layer]))
        gain_ffn, through = norm_back(grad_normed, middle, gains[layer][1])
        grad_middle = grad.astype(wide) + through
        grad_in, right, gain_attn = attention_back(
            inputs[layer], grad_middle, tabs, attn_w[layer], gains[layer][0], kept_attn
        )
        gain_grads[layer] = jnp.stack([gain_attn, gain_ffn])

        def collect(partial):
            return partial + to_core(partial.astype(low), layer).astype(wide)

        def along_z(stack):
            blocks = z_trade(stack.astype(low), z, layer)
            total = sum(block.astype(wide) for _, block in blocks)
            return plane_gather(teams_sum(total).astype(low), q, layer)

        ffn_sum = along_z(collect(dot_l(normed, grad_both)).reshape(4, -1, 2 * hid))
        down_part = collect(dot_l(act, grad)).astype(low).reshape(TEAM, down_rows, width)
        down_sum = along_z(plane_trade(down_part, q, layer))
        own_right = lax.dynamic_slice_in_dim(right, q * chunk, chunk, axis=1)
        split = w_query.shape[2] + w_key.shape[2] * 2
        column = q * chunk + jnp.arange(chunk)
        attn_part = jnp.where(
            column[None, :] < split,
            dot_l(kept_attn[0], own_right),
            dot_l(kept_attn[5], own_right),
        )
        attn_sum = along_z(collect(attn_part).reshape(4, -1, chunk))
        sums[layer] = (attn_sum, ffn_sum, down_sum)
        grad = grad_in.astype(low)
        input_grads[layer] = grad

    def spread(by_layer):
        mine = jnp.where(core == 0, by_layer[0], by_layer[1])
        other = swap(jnp.where(core == 0, by_layer[1], by_layer[0]))
        stack = jnp.where(
            core == 0, jnp.stack([mine, other]), jnp.stack([other, mine])
        ).reshape(2, 4, group, width)
        replicas = lax.axis_size("replica")

        def slice_for(target):
            return lax.dynamic_index_in_dim(stack, target, 1, keepdims=False)

        total = jnp.where(z == q, slice_for(z), 0)
        for hop in (1, 2, 3):
            pairs = [
                ((r % TEAM) * replicas + r, (r % TEAM + hop) % 4 * replicas + r)
                for r in range(replicas)
            ]
            total = total + lax.ppermute(slice_for((z + hop) % 4), ("shard", "replica"), pairs)
        return total[None, :, None]

    layer_out = spread(outputs)
    input_grad = spread(input_grads)

    gain_all = jnp.stack(gain_grads)
    gain_all = gain_all + swap(gain_all)
    total = gain_all
    for hop in (1, 2, 3):
        total = total + z_send(gain_all, hop)
    flip = TEAM
    while flip < lax.axis_size("replica"):
        total = total + plane_send(total, flip)
        flip *= 2
    total = jnp.where(core == 0, total[0], total[1])
    total = lax.dynamic_index_in_dim(total.reshape(2, 4, -1), z, 1, keepdims=False)

    attn_sum, ffn_sum, down_sum = (
        jnp.where(core == 0, first, second).astype(wide) for first, second in zip(*sums)
    )
    attn_cols = jnp.concatenate([attn_sum[chunk_num] for chunk_num in range(TEAM)], axis=1)
    qw, kw = w_query.shape[2], w_key.shape[2]
    gate_cols = jnp.concatenate([ffn_sum[num, :, :hid] for num in range(TEAM)], axis=1)
    up_cols = jnp.concatenate([ffn_sum[num, :, hid:] for num in range(TEAM)], axis=1)
    return (
        layer_out,
        input_grad,
        total[0][None],
        attn_cols[None, :, :qw],
        attn_cols[None, :, qw : qw + kw],
        attn_cols[None, :, qw + kw : qw + 2 * kw],
        attn_cols[None, :, qw + 2 * kw :],
        total[1][None],
        gate_cols[None],
        up_cols[None],
        down_sum.reshape(1, -1, width),
    )


def solution(mesh):
    placed = (
        P(None, "replica", "shard", None),
        P(None, "replica", None),
        P("section", "shard"),
        P("section", "shard", None),
        P("section", "shard", None),
        P("section", "shard", None),
        P("section", "shard", None),
        P("section", "shard"),
        P("section", "shard", None),
        P("section", "shard", None),
        P("section", "shard", None),
        P(None, "replica", "shard", None),
    )
    return jax.shard_map(
        local,
        mesh=mesh,
        in_specs=placed,
        out_specs=(
            P("section", None, "replica", "shard", None),
            P("section", None, "replica", "shard", None),
            P("section", "shard"),
            P("section", "shard", None),
            P("section", "shard", None),
            P("section", "shard", None),
            P("section", "shard", None),
            P("section", "shard"),
            P("section", "shard", None),
            P("section", "shard", None),
            P("section", "shard", None),
        ),
        check_vma=False,
    )
```

time: 1810 us -> 790 us (0.44)
  blocking collectives: 1120 us -> 0 us
  starting transfers between devices: 28.5 us -> 313 us
  waiting for transfers between devices: 293 us -> 136 us
  matrix products: 135 us -> 71.3 us
  other arithmetic: 65.1 us -> 99.2 us
    unnamed x4 -> x0, blocking collectives: 907 us -> none
    ppermute x4 -> x131, starting transfers between devices: 6.15 us -> 313 us  [the longest x48 124 us: z_send(): return lax.ppermute(value, ('section', 'shard'), pairs)]
    all_gather x8 -> x0, waiting for transfers between devices: 236 us -> none  [the longest x1 89.5 us: local(): lax.all_gather(w_up[0], 'shard', axis=0, tiled=True)]
    all_gather x12 -> x0, blocking collectives: 211 us -> none  [the longest x3 46 us: forward_layer(): lax.all_gather(keys_own, 'shard', axis=0, tiled=True)]
    ppermute x4 -> x131, waiting for transfers between devices: 3.1 us -> 136 us  [the longest x61 74.6 us: plane_send(): return lax.ppermute(value, ('section', 'replica'), pairs)]
    dot_general x70 -> x46, matrix products: 135 us -> 62.5 us  [the longest x8 19.3 us: dot_l(): lax.dot_general(a, b, (((0,), (0,)), ((), ())), preferred_element_type=wide)]
    unnamed x27 -> x0, waiting for transfers between devices: 53.9 us -> none
    dynamic_update_slice x0 -> x83, local copies, waits for them, and re-layouts: none -> 52.6 us  [place(): stack = lax.dynamic_update_index_in_dim(stack, block, index, 0)]
  transfers between devices with their start and end apart: 25 -> 131, of which waited for: 11 -> 32; matrix products, arithmetic and copies ran while one was open for 57% -> 38% of each run, Pallas kernels for 0% -> 0%
where the time goes in v1:
time: 790 us; the launch traced here: 778 us
  starting transfers between devices  313 us (40%)
  local copies, waits for them, and re-layouts  154 us (19%)
  waiting for transfers between devices  136 us (17%)
  other arithmetic  99.2 us (13%)
  matrix products  71.3 us (9%)
    ppermute x48, starting transfers between devices, z_send(): return lax.ppermute(value, ('section', 'shard'), pairs)  124 us
    ppermute x61, starting transfers between devices, plane_send(): return lax.ppermute(value, ('section', 'replica'), pairs)  102 us
    ppermute x61, waiting for transfers between devices, plane_send(): return lax.ppermute(value, ('section', 'replica'), pairs)  74.6 us
    ppermute x12, starting transfers between devices, to_core(): return lax.ppermute(value, 'section', [(1 - target, target)])  68.9 us
    ppermute x48, waiting for transfers between devices, z_send(): return lax.ppermute(value, ('section', 'shard'), pairs)  56.6 us
    dynamic_update_slice x83, local copies, waits for them, and re-layouts, place(): stack = lax.dynamic_update_index_in_dim(stack, block, index, 0)  52.6 us
    unnamed x230, local copies, waits for them, and re-layouts  25.3 us
    dot_general x8, matrix products, dot_l(): lax.dot_general(a, b, (((0,), (0,)), ((), ())), preferred_element_type=wide)  19.3 us
  transfers between devices with their start and end apart: 131, of which 32 were waited for; matrix products, arithmetic and copies ran while one was open for 38% of the time, Pallas kernels for 0%

profile of v1, /device:TPU:0, one launch (start us, length us, event | category | flops | bytes accessed | tf_op | source)
XLA Modules:
  0.0 777.9 jit_solution(557978131774918441)
XLA Ops:
  34.2 4.7 collective-permute-start.22
  46.5 4.7 collective-permute-done.1
  56.0 7.5 collective-permute-done.3
  63.5 6.6 collective-permute-start.4
  70.1 6.2 collective-permute-done.4
  76.3 4.9 collective-permute-done.5
  83.2 4.3 collective-permute-start.11
  88.3 3.7 collective-permute-done.10
  94.6 3.9 collective-permute-done.11
  101.7 5.6 collective-permute-start.26
  108.0 3.9 collective-permute-done.25
  112.0 3.4 collective-permute-start.13
  126.0 3.5 collective-permute-start.28
  134.3 4.3 collective-permute-start.29
  144.2 4.5 collective-permute-start.15
  161.4 9.4 %collective-permute-done.14 = bf16[960,640]{1,0:T(8,128)(2,1)} collective-permute-done((bf16[960,640]{1,0:T(8,128)(2,1)}, bf16[960,640]{1,0:T(8,128)(2,1)}, u32[]{:S(2)}, u32[]{:S(2)}) %collective-permute-start.14) | collective-permute-done | bytes 1228832 | tf_op jit(solution)/shard_map/ppermute | solution.py:50
  175.8 3.5 collective-permute-start.16
  192.7 3.4 broadcast_select_fusion.3
  229.2 4.4 fusion.175
  277.6 5.2 collective-permute-done.63
  297.1 8.0 %collective-permute-done.33 = bf16[128,960]{0,1:T(8,128)(2,1)} collective-permute-done((bf16[128,960]{0,1:T(8,128)(2,1)}, bf16[128,960]{0,1:T(8,128)(2,1)}, u32[]{:S(2)}, u32[]{:S(2)}) %collective-permute-start.33) | collective-permute-done | bytes 245792 | tf_op jit(solution)/shard_map/ppermute | solution.py:50
  309.6 4.2 collective-permute-done.34
  348.0 4.3 fusion.176
  379.8 38.0 %collective-permute-start.121 = (bf16[640,960]{0,1:T(8,128)(2,1)}, bf16[640,960]{0,1:T(8,128)(2,1)}, u32[]{:S(2)}, u32[]{:S(2)}) collective-permute-start(bf16[640,960]{0,1:T(8,128)(2,1)} %get-tuple-element.249), channel_id=1, source_target_pairs={{0,16},{1,17},{2,18},{3,19},{4,20},{5,21},{6,22},{7,23},{8,24},{9,... | collective-permute-start | bytes 3686408 | tf_op jit(solution)/shard_map/ppermute | solution.py:32
  417.8 3.9 fusion.180
  426.9 3.9 collective-permute-done.70
  430.8 5.2 collective-permute-done.68
  460.4 4.3 fusion.179
  518.2 4.5 collective-permute-start.79
  528.1 3.8 collective-permute-start.82
  536.6 3.5 collective-permute-start.60
  552.6 4.6 collective-permute-done.58
  565.5 3.5 collective-permute-start.76
  571.2 11.1 %collective-permute-start.126 = (bf16[160,960]{1,0:T(8,128)(2,1)}, bf16[160,960]{1,0:T(8,128)(2,1)S(1)}, u32[]{:S(2)}, u32[]{:S(2)}) collective-permute-start(bf16[160,960]{1,0:T(8,128)(2,1)} %get-tuple-element.126), channel_id=1, source_target_pairs={{16,24},{20,28},{24,16},{28,20},{17,25},{21,29},{25,17},{29,21},{1... | collective-permute-start | bytes 921608 | tf_op jit(solution)/shard_map/ppermute | solution.py:43
  596.2 11.6 %collective-permute-start.104 = (bf16[960,1280]{1,0:T(8,128)(2,1)S(1)}, bf16[960,1280]{1,0:T(8,128)(2,1)S(1)}, u32[]{:S(2)}, u32[]{:S(2)}) collective-permute-start(bf16[960,1280]{1,0:T(8,128)(2,1)S(1)} %copy-done.23), channel_id=1, source_target_pairs={{0,16},{1,17},{2,18},{3,19},{4,20},{5,21},{6,22},{7,23},{8,24},{9,... | collective-permute-start | bytes 7372808 | tf_op jit(solution)/shard_map/ppermute | solution.py:32
  614.0 3.4 collective-permute-start.113
  623.7 7.2 collective-permute-done.114
  634.4 4.2 collective-permute-start.117
  645.1 5.4 collective-permute-start.86
  650.6 4.6 collective-permute-done.116
  676.6 3.6 collective-permute-start.87
  695.0 4.2 collective-permute-done.89
  706.0 17.1 %collective-permute-start.100 = (bf16[240,1280]{1,0:T(8,128)(2,1)}, bf16[240,1280]{1,0:T(8,128)(2,1)S(1)}, u32[]{:S(2)}, u32[]{:S(2)}) collective-permute-start(bf16[240,1280]{1,0:T(8,128)(2,1)} %get-tuple-element.114), channel_id=1, source_target_pairs={{0,12},{4,0},{8,4},{12,8},{1,13},{5,1},{9,5},{13,9},{2,14},{6,2},{... | collective-permute-start | bytes 1843208 | tf_op jit(solution)/shard_map/ppermute | solution.py:43
  725.0 3.7 collective-permute-start.98
  737.0 14.0 %collective-permute-done.99 = bf16[240,1280]{1,0:T(8,128)(2,1)S(1)} collective-permute-done((bf16[240,1280]{1,0:T(8,128)(2,1)}, bf16[240,1280]{1,0:T(8,128)(2,1)S(1)}, u32[]{:S(2)}, u32[]{:S(2)}) %collective-permute-start.99) | collective-permute-done | bytes 614432 | tf_op jit(solution)/shard_map/ppermute | solution.py:43
  754.8 3.8 collective-permute-start.102
  758.6 3.5 collective-permute-start.103
  765.0 8.5 %collective-permute-done.102 = bf16[240,1280]{1,0:T(8,128)(2,1)S(1)} collective-permute-done((bf16[240,1280]{1,0:T(8,128)(2,1)S(1)}, bf16[240,1280]{1,0:T(8,128)(2,1)S(1)}, u32[]{:S(2)}, u32[]{:S(2)}) %collective-permute-start.102) | collective-permute-done | bytes 614432 | tf_op jit(solution)/shard_map/ppermute | solution.py:50
  (792 shorter events, 478.8 us)
Async XLA Ops:
  1.5 27.1 %collective-permute-start.6 = (bf16[2,240]{1,0:T(2,128)(2,1)S(1)}, bf16[2,240]{1,0:T(2,128)(2,1)S(1)}, u32[]{:S(2)}, u32[]{:S(2)}) collective-permute-start(bf16[2,240]{1,0:T(2,128)(2,1)S(1)} %pad_maximum_fusion.25), channel_id=1, source_target_pairs={{0,4},{4,8},{8,12},{12,0},{16,20},{20,24},{24,28},{28,16},{1,5},{5... | collective-permute-start | bytes 2888 | tf_op jit(solution)/shard_map/ppermute | solution.py:43
  4.5 24.6 %collective-permute-start.7 = (bf16[2,240]{1,0:T(2,128)(2,1)S(1)}, bf16[2,240]{1,0:T(2,128)(2,1)S(1)}, u32[]{:S(2)}, u32[]{:S(2)}) collective-permute-start(bf16[2,240]{1,0:T(2,128)(2,1)S(1)} %pad_maximum_fusion.25), channel_id=1, source_target_pairs={{0,8},{4,12},{8,0},{12,4},{16,24},{20,28},{24,16},{28,20},{1,9},{5... | collective-permute-start | bytes 2888 | tf_op jit(solution)/shard_map/ppermute | solution.py:43
  7.1 24.6 %collective-permute-start.8 = (bf16[2,240]{1,0:T(2,128)(2,1)S(1)}, bf16[2,240]{1,0:T(2,128)(2,1)S(1)}, u32[]{:S(2)}, u32[]{:S(2)}) collective-permute-start(bf16[2,240]{1,0:T(2,128)(2,1)S(1)} %pad_maximum_fusion.25), channel_id=1, source_target_pairs={{0,12},{4,0},{8,4},{12,8},{16,28},{20,16},{24,20},{28,24},{1,13},{... | collective-permute-start | bytes 2888 | tf_op jit(solution)/shard_map/ppermute | solution.py:43
  9.2 25.1 %collective-permute-start.17 = (s32[256]{0:T(256)S(1)}, s32[256]{0:T(256)S(1)}, u32[]{:S(2)}, u32[]{:S(2)}) collective-permute-start(s32[256]{0:T(256)S(1)} %bitcast.765), channel_id=1, source_target_pairs={{0,1},{1,0},{2,3},{3,2},{16,17},{17,16},{18,19},{19,18},{4,5},{5,4... | collective-permute-start | bytes 3080 | tf_op jit(solution)/shard_map/ppermute | solution.py:50
  10.7 28.4 %collective-permute-start.18 = (s32[256]{0:T(256)S(1)}, s32[256]{0:T(256)S(1)}, u32[]{:S(2)}, u32[]{:S(2)}) collective-permute-start(s32[256]{0:T(256)S(1)} %bitcast.766), channel_id=1, source_target_pairs={{0,2},{1,3},{2,0},{3,1},{16,18},{17,19},{18,16},{19,17},{4,6},{5,7... | collective-permute-start | bytes 3080 | tf_op jit(solution)/shard_map/ppermute | solution.py:50
  29.1 96.8 %collective-permute-start.20 = (bf16[240,1280]{1,0:T(8,128)(2,1)}, bf16[240,1280]{1,0:T(8,128)(2,1)}, u32[]{:S(2)}, u32[]{:S(2)}) collective-permute-start(bf16[240,1280]{1,0:T(8,128)(2,1)} %pad_maximum_fusion.14), channel_id=1, source_target_pairs={{0,4},{4,8},{8,12},{12,0},{1,5},{5,9},{9,13},{13,1},{2,6},{6,10},{... | collective-permute-start | bytes 1843208 | tf_op jit(solution)/shard_map/ppermute | solution.py:43
  31.8 118.3 %collective-permute-start.21 = (bf16[240,1280]{1,0:T(8,128)(2,1)}, bf16[240,1280]{1,0:T(8,128)(2,1)}, u32[]{:S(2)}, u32[]{:S(2)}) collective-permute-start(bf16[240,1280]{1,0:T(8,128)(2,1)} %pad_maximum_fusion.14), channel_id=1, source_target_pairs={{0,8},{4,12},{8,0},{12,4},{1,9},{5,13},{9,1},{13,5},{2,10},{6,14},... | collective-permute-start | bytes 1843208 | tf_op jit(solution)/shard_map/ppermute | solution.py:43
  34.2 120.1 %collective-permute-start.22 = (bf16[240,1280]{1,0:T(8,128)(2,1)}, bf16[240,1280]{1,0:T(8,128)(2,1)}, u32[]{:S(2)}, u32[]{:S(2)}) collective-permute-start(bf16[240,1280]{1,0:T(8,128)(2,1)} %pad_maximum_fusion.14), channel_id=1, source_target_pairs={{0,12},{4,0},{8,4},{12,8},{1,13},{5,1},{9,5},{13,9},{2,14},{6,2},{... | collective-permute-start | bytes 1843208 | tf_op jit(solution)/shard_map/ppermute | solution.py:43
  51.2 32.0 %collective-permute-start.24 = (bf16[160,960]{1,0:T(8,128)(2,1)S(1)}, bf16[160,960]{1,0:T(8,128)(2,1)S(1)}, u32[]{:S(2)}, u32[]{:S(2)}) collective-permute-start(bf16[160,960]{1,0:T(8,128)(2,1)S(1)} %bitcast.688), channel_id=1, source_target_pairs={{0,4},{4,8},{8,12},{12,0},{1,5},{5,9},{9,13},{13,1},{2,6},{6,10},{... | collective-permute-start | bytes 921608 | tf_op jit(solution)/shard_map/ppermute | solution.py:43
  112.0 47.0 %collective-permute-start.13 = (bf16[960,640]{1,0:T(8,128)(2,1)}, bf16[960,640]{1,0:T(8,128)(2,1)}, u32[]{:S(2)}, u32[]{:S(2)}) collective-permute-start(bf16[960,640]{1,0:T(8,128)(2,1)} %bitcast.27), channel_id=1, source_target_pairs={{0,1},{1,0},{2,3},{3,2},{4,5},{5,4},{6,7},{7,6},{8,9},{9,8},{10,11... | collective-permute-start | bytes 3686408 | tf_op jit(solution)/shard_map/ppermute | solution.py:50
  138.7 32.1 %collective-permute-start.14 = (bf16[960,640]{1,0:T(8,128)(2,1)}, bf16[960,640]{1,0:T(8,128)(2,1)}, u32[]{:S(2)}, u32[]{:S(2)}) collective-permute-start(bf16[960,640]{1,0:T(8,128)(2,1)} %bitcast.27), channel_id=1, source_target_pairs={{0,2},{1,3},{2,0},{3,1},{4,6},{5,7},{6,4},{7,5},{8,10},{9,11},{10,... | collective-permute-start | bytes 3686408 | tf_op jit(solution)/shard_map/ppermute | solution.py:50
  144.2 29.1 %collective-permute-start.15 = (bf16[960,640]{1,0:T(8,128)(2,1)}, bf16[960,640]{1,0:T(8,128)(2,1)}, u32[]{:S(2)}, u32[]{:S(2)}) collective-permute-start(bf16[960,640]{1,0:T(8,128)(2,1)} %bitcast.27), channel_id=1, source_target_pairs={{0,3},{1,2},{2,1},{3,0},{4,7},{5,6},{6,5},{7,4},{8,11},{9,10},{10,... | collective-permute-start | bytes 3686408 | tf_op jit(solution)/shard_map/ppermute | solution.py:50
  150.1 29.2 %collective-permute-start.30 = (bf16[640,960]{0,1:T(8,128)(2,1)}, bf16[640,960]{0,1:T(8,128)(2,1)}, u32[]{:S(2)}, u32[]{:S(2)}) collective-permute-start(bf16[640,960]{0,1:T(8,128)(2,1)} %copy.329), channel_id=1, source_target_pairs={{0,16},{1,17},{2,18},{3,19},{4,20},{5,21},{6,22},{7,23},{8,24},{9,... | collective-permute-start | bytes 3686408 | tf_op jit(solution)/shard_map/ppermute | solution.py:32
  156.3 36.4 %collective-permute-start.23 = (bf16[960,1280]{1,0:T(8,128)(2,1)}, bf16[960,1280]{1,0:T(8,128)(2,1)}, u32[]{:S(2)}, u32[]{:S(2)}) collective-permute-start(bf16[960,1280]{1,0:T(8,128)(2,1)} %bitcast.65), channel_id=1, source_target_pairs={{0,16},{1,17},{2,18},{3,19},{4,20},{5,21},{6,22},{7,23},{8,24},{9,... | collective-permute-start | bytes 7372808 | tf_op jit(solution)/shard_map/ppermute | solution.py:32
  175.8 33.4 %collective-permute-start.16 = (bf16[4,960,640]{2,1,0:T(8,128)(2,1)}, bf16[4,960,640]{2,1,0:T(8,128)(2,1)}, u32[]{:S(2)}, u32[]{:S(2)}) collective-permute-start(bf16[4,960,640]{2,1,0:T(8,128)(2,1)} %bitcast_dynamic-update-slice_fusion.4), channel_id=1, source_target_pairs={{0,16},{1,17},{2,18},{3,19},{4,20},{5,21},{6,22},{7,23},{8,24},{9,... | collective-permute-start | bytes 14745608 | tf_op jit(solution)/shard_map/ppermute | solution.py:32
  199.2 87.0 %collective-permute-start.52 = (bf16[640,960]{0,1:T(8,128)(2,1)}, bf16[640,960]{0,1:T(8,128)(2,1)}, u32[]{:S(2)}, u32[]{:S(2)}) collective-permute-start(bf16[640,960]{0,1:T(8,128)(2,1)} %copy.339), channel_id=1, source_target_pairs={{16,0},{17,1},{18,2},{19,3},{20,4},{21,5},{22,6},{23,7},{24,8},{25... | collective-permute-start | bytes 3686408 | tf_op jit(solution)/shard_map/ppermute | solution.py:32
  201.2 83.0 %collective-permute-start.44 = (bf16[240,1280]{1,0:T(8,128)(2,1)}, bf16[240,1280]{1,0:T(8,128)(2,1)}, u32[]{:S(2)}, u32[]{:S(2)}) collective-permute-start(bf16[240,1280]{1,0:T(8,128)(2,1)} %pad_maximum_fusion.14), channel_id=1, source_target_pairs={{16,28},{20,16},{24,20},{28,24},{17,29},{21,17},{25,21},{29,25},{1... | collective-permute-start | bytes 1843208 | tf_op jit(solution)/shard_map/ppermute | solution.py:43
  218.9 22.7 %collective-permute-start.37 = (bf16[240,640]{1,0:T(8,128)(2,1)S(1)}, bf16[240,640]{1,0:T(8,128)(2,1)}, u32[]{:S(2)}, u32[]{:S(2)}) collective-permute-start(bf16[240,640]{1,0:T(8,128)(2,1)S(1)} %copy-done.73), channel_id=1, source_target_pairs={{16,28},{20,16},{24,20},{28,24},{17,29},{21,17},{25,21},{29,25},{1... | collective-permute-start | bytes 921608 | tf_op jit(solution)/shard_map/ppermute | solution.py:43
  269.5 59.3 %collective-permute-start.41 = (bf16[4,960,640]{2,1,0:T(8,128)(2,1)}, bf16[4,960,640]{2,1,0:T(8,128)(2,1)}, u32[]{:S(2)}, u32[]{:S(2)}) collective-permute-start(bf16[4,960,640]{2,1,0:T(8,128)(2,1)} %bitcast_dynamic-update-slice_fusion), channel_id=1, source_target_pairs={{16,0},{17,1},{18,2},{19,3},{20,4},{21,5},{22,6},{23,7},{24,8},{25... | collective-permute-start | bytes 14745608 | tf_op jit(solution)/shard_map/ppermute | solution.py:32
  286.1 79.8 %collective-permute-start.45 = (bf16[960,1280]{1,0:T(8,128)(2,1)}, bf16[960,1280]{1,0:T(8,128)(2,1)}, u32[]{:S(2)}, u32[]{:S(2)}) collective-permute-start(bf16[960,1280]{1,0:T(8,128)(2,1)} %bitcast.117), channel_id=1, source_target_pairs={{16,0},{17,1},{18,2},{19,3},{20,4},{21,5},{22,6},{23,7},{24,8},{25... | collective-permute-start | bytes 7372808 | tf_op jit(solution)/shard_map/ppermute | solution.py:32
  373.1 49.4 %collective-permute-start.53 = (bf16[128,960]{0,1:T(8,128)(2,1)S(1)}, bf16[128,960]{0,1:T(8,128)(2,1)S(1)}, u32[]{:S(2)}, u32[]{:S(2)}) collective-permute-start(bf16[128,960]{0,1:T(8,128)(2,1)S(1)} %get-tuple-element.199), channel_id=1, source_target_pairs={{0,1},{1,0},{2,3},{3,2},{16,17},{17,16},{18,19},{19,18},{4,5},{5,4... | collective-permute-start | bytes 737288 | tf_op jit(solution)/shard_map/ppermute | solution.py:50
  374.0 48.5 %collective-permute-start.55 = (bf16[128,960]{0,1:T(8,128)(2,1)S(1)}, bf16[128,960]{0,1:T(8,128)(2,1)S(1)}, u32[]{:S(2)}, u32[]{:S(2)}) collective-permute-start(bf16[128,960]{0,1:T(8,128)(2,1)S(1)} %get-tuple-element.200), channel_id=1, source_target_pairs={{0,2},{1,3},{2,0},{3,1},{16,18},{17,19},{18,16},{19,17},{4,6},{5,7... | collective-permute-start | bytes 737288 | tf_op jit(solution)/shard_map/ppermute | solution.py:50
  377.2 44.5 %collective-permute-start.67 = (bf16[128,960]{0,1:T(8,128)(2,1)S(1)}, bf16[128,960]{0,1:T(8,128)(2,1)S(1)}, u32[]{:S(2)}, u32[]{:S(2)}) collective-permute-start(bf16[128,960]{0,1:T(8,128)(2,1)S(1)} %get-tuple-element.187), channel_id=1, source_target_pairs={{0,1},{1,0},{2,3},{3,2},{16,17},{17,16},{18,19},{19,18},{4,5},{5,4... | collective-permute-start | bytes 737288 | tf_op jit(solution)/shard_map/ppermute | solution.py:50
  378.4 43.3 %collective-permute-start.69 = (bf16[128,960]{0,1:T(8,128)(2,1)S(1)}, bf16[128,960]{0,1:T(8,128)(2,1)S(1)}, u32[]{:S(2)}, u32[]{:S(2)}) collective-permute-start(bf16[128,960]{0,1:T(8,128)(2,1)S(1)} %get-tuple-element.188), channel_id=1, source_target_pairs={{0,2},{1,3},{2,0},{3,1},{16,18},{17,19},{18,16},{19,17},{4,6},{5,7... | collective-permute-start | bytes 737288 | tf_op jit(solution)/shard_map/ppermute | solution.py:50
  379.8 162.9 %collective-permute-start.121 = (bf16[640,960]{0,1:T(8,128)(2,1)}, bf16[640,960]{0,1:T(8,128)(2,1)}, u32[]{:S(2)}, u32[]{:S(2)}) collective-permute-start(bf16[640,960]{0,1:T(8,128)(2,1)} %get-tuple-element.249), channel_id=1, source_target_pairs={{0,16},{1,17},{2,18},{3,19},{4,20},{5,21},{6,22},{7,23},{8,24},{9,... | collective-permute-start | bytes 3686408 | tf_op jit(solution)/shard_map/ppermute | solution.py:32
  423.4 43.0 %collective-permute-start.56 = (bf16[128,960]{0,1:T(8,128)(2,1)}, bf16[128,960]{0,1:T(8,128)(2,1)}, u32[]{:S(2)}, u32[]{:S(2)}) collective-permute-start(bf16[128,960]{0,1:T(8,128)(2,1)} %get-tuple-element.198), channel_id=1, source_target_pairs={{0,1},{1,0},{2,3},{3,2},{16,17},{17,16},{18,19},{19,18},{4,5},{5,4... | collective-permute-start | bytes 737288 | tf_op jit(solution)/shard_map/ppermute | solution.py:50
  424.8 42.7 %collective-permute-start.54 = (bf16[128,960]{0,1:T(8,128)(2,1)}, bf16[128,960]{0,1:T(8,128)(2,1)}, u32[]{:S(2)}, u32[]{:S(2)}) collective-permute-start(bf16[128,960]{0,1:T(8,128)(2,1)} %get-tuple-element.197), channel_id=1, source_target_pairs={{0,2},{1,3},{2,0},{3,1},{16,18},{17,19},{18,16},{19,17},{4,6},{5,7... | collective-permute-start | bytes 737288 | tf_op jit(solution)/shard_map/ppermute | solution.py:50
  469.7 56.9 %collective-permute-start.57 = (bf16[256,960]{0,1:T(8,128)(2,1)}, bf16[256,960]{0,1:T(8,128)(2,1)}, u32[]{:S(2)}, u32[]{:S(2)}) collective-permute-start(bf16[256,960]{0,1:T(8,128)(2,1)} %fusion.95), channel_id=1, source_target_pairs={{0,16},{16,0},{1,17},{17,1},{2,18},{18,2},{3,19},{19,3},{4,20},{20... | collective-permute-start | bytes 1474568 | tf_op jit(solution)/shard_map/ppermute | solution.py:36
  478.5 105.2 %collective-permute-start.90 = (bf16[960,640]{1,0:T(8,128)(2,1)}, bf16[960,640]{1,0:T(8,128)(2,1)}, u32[]{:S(2)}, u32[]{:S(2)}) collective-permute-start(bf16[960,640]{1,0:T(8,128)(2,1)} %get-tuple-element.241), channel_id=1, source_target_pairs={{0,16},{1,17},{2,18},{3,19},{4,20},{5,21},{6,22},{7,23},{8,24},{9,... | collective-permute-start | bytes 3686408 | tf_op jit(solution)/shard_map/ppermute | solution.py:32
  533.9 26.6 %collective-permute-start.75 = (bf16[256,960]{0,1:T(8,128)(2,1)}, bf16[256,960]{0,1:T(8,128)(2,1)S(1)}, u32[]{:S(2)}, u32[]{:S(2)}) collective-permute-start(bf16[256,960]{0,1:T(8,128)(2,1)} %broadcast_select_fusion.11), channel_id=1, source_target_pairs={{0,16},{16,0},{1,17},{17,1},{2,18},{18,2},{3,19},{19,3},{4,20},{20... | collective-permute-start | bytes 1474568 | tf_op jit(solution)/shard_map/ppermute | solution.py:36
  550.4 37.6 %collective-permute-start.111 = (bf16[640,960]{0,1:T(8,128)(2,1)}, bf16[640,960]{0,1:T(8,128)(2,1)}, u32[]{:S(2)}, u32[]{:S(2)}) collective-permute-start(bf16[640,960]{0,1:T(8,128)(2,1)} %get-tuple-element.247), channel_id=1, source_target_pairs={{16,0},{17,1},{18,2},{19,3},{20,4},{21,5},{22,6},{23,7},{24,8},{25... | collective-permute-start | bytes 3686408 | tf_op jit(solution)/shard_map/ppermute | solution.py:32
  570.1 23.6 %collective-permute-start.127 = (bf16[160,960]{1,0:T(8,128)(2,1)}, bf16[160,960]{1,0:T(8,128)(2,1)S(1)}, u32[]{:S(2)}, u32[]{:S(2)}) collective-permute-start(bf16[160,960]{1,0:T(8,128)(2,1)} %get-tuple-element.125), channel_id=1, source_target_pairs={{16,28},{20,16},{24,20},{28,24},{17,29},{21,17},{25,21},{29,25},{1... | collective-permute-start | bytes 921608 | tf_op jit(solution)/shard_map/ppermute | solution.py:43
  571.2 23.4 %collective-permute-start.126 = (bf16[160,960]{1,0:T(8,128)(2,1)}, bf16[160,960]{1,0:T(8,128)(2,1)S(1)}, u32[]{:S(2)}, u32[]{:S(2)}) collective-permute-start(bf16[160,960]{1,0:T(8,128)(2,1)} %get-tuple-element.126), channel_id=1, source_target_pairs={{16,24},{20,28},{24,16},{28,20},{17,25},{21,29},{25,17},{29,21},{1... | collective-permute-start | bytes 921608 | tf_op jit(solution)/shard_map/ppermute | solution.py:43
  582.3 25.4 %collective-permute-start.125 = (bf16[160,960]{1,0:T(8,128)(2,1)}, bf16[160,960]{1,0:T(8,128)(2,1)S(1)}, u32[]{:S(2)}, u32[]{:S(2)}) collective-permute-start(bf16[160,960]{1,0:T(8,128)(2,1)} %get-tuple-element.124), channel_id=1, source_target_pairs={{16,20},{20,24},{24,28},{28,16},{17,21},{21,25},{25,29},{29,17},{1... | collective-permute-start | bytes 921608 | tf_op jit(solution)/shard_map/ppermute | solution.py:43
  586.6 26.1 %collective-permute-start.93 = (bf16[240,640]{1,0:T(8,128)(2,1)}, bf16[240,640]{1,0:T(8,128)(2,1)}, u32[]{:S(2)}, u32[]{:S(2)}) collective-permute-start(bf16[240,640]{1,0:T(8,128)(2,1)} %get-tuple-element.148), channel_id=1, source_target_pairs={{16,28},{20,16},{24,20},{28,24},{17,29},{21,17},{25,21},{29,25},{1... | collective-permute-start | bytes 921608 | tf_op jit(solution)/shard_map/ppermute | solution.py:43
  588.0 26.1 %collective-permute-start.92 = (bf16[240,640]{1,0:T(8,128)(2,1)}, bf16[240,640]{1,0:T(8,128)(2,1)}, u32[]{:S(2)}, u32[]{:S(2)}) collective-permute-start(bf16[240,640]{1,0:T(8,128)(2,1)} %get-tuple-element.149), channel_id=1, source_target_pairs={{16,24},{20,28},{24,16},{28,20},{17,25},{21,29},{25,17},{29,21},{1... | collective-permute-start | bytes 921608 | tf_op jit(solution)/shard_map/ppermute | solution.py:43
  593.6 23.8 %collective-permute-start.91 = (bf16[240,640]{1,0:T(8,128)(2,1)}, bf16[240,640]{1,0:T(8,128)(2,1)S(1)}, u32[]{:S(2)}, u32[]{:S(2)}) collective-permute-start(bf16[240,640]{1,0:T(8,128)(2,1)} %get-tuple-element.147), channel_id=1, source_target_pairs={{16,20},{20,24},{24,28},{28,16},{17,21},{21,25},{25,29},{29,17},{1... | collective-permute-start | bytes 921608 | tf_op jit(solution)/shard_map/ppermute | solution.py:43
  596.2 64.6 %collective-permute-start.104 = (bf16[960,1280]{1,0:T(8,128)(2,1)S(1)}, bf16[960,1280]{1,0:T(8,128)(2,1)S(1)}, u32[]{:S(2)}, u32[]{:S(2)}) collective-permute-start(bf16[960,1280]{1,0:T(8,128)(2,1)S(1)} %copy-done.23), channel_id=1, source_target_pairs={{0,16},{1,17},{2,18},{3,19},{4,20},{5,21},{6,22},{7,23},{8,24},{9,... | collective-permute-start | bytes 7372808 | tf_op jit(solution)/shard_map/ppermute | solution.py:32
  643.8 56.8 %collective-permute-start.97 = (bf16[960,1280]{1,0:T(8,128)(2,1)}, bf16[960,1280]{1,0:T(8,128)(2,1)}, u32[]{:S(2)}, u32[]{:S(2)}) collective-permute-start(bf16[960,1280]{1,0:T(8,128)(2,1)} %get-tuple-element.243), channel_id=1, source_target_pairs={{16,0},{17,1},{18,2},{19,3},{20,4},{21,5},{22,6},{23,7},{24,8},{25... | collective-permute-start | bytes 7372808 | tf_op jit(solution)/shard_map/ppermute | solution.py:32
  673.3 51.7 %collective-permute-start.107 = (bf16[240,1280]{1,0:T(8,128)(2,1)}, bf16[240,1280]{1,0:T(8,128)(2,1)}, u32[]{:S(2)}, u32[]{:S(2)}) collective-permute-start(bf16[240,1280]{1,0:T(8,128)(2,1)} %get-tuple-element.111), channel_id=1, source_target_pairs={{16,28},{20,16},{24,20},{28,24},{17,29},{21,17},{25,21},{29,25},{1... | collective-permute-start | bytes 1843208 | tf_op jit(solution)/shard_map/ppermute | solution.py:43
  675.1 53.6 %collective-permute-start.106 = (bf16[240,1280]{1,0:T(8,128)(2,1)}, bf16[240,1280]{1,0:T(8,128)(2,1)}, u32[]{:S(2)}, u32[]{:S(2)}) collective-permute-start(bf16[240,1280]{1,0:T(8,128)(2,1)} %get-tuple-element.112), channel_id=1, source_target_pairs={{16,24},{20,28},{24,16},{28,20},{17,25},{21,29},{25,17},{29,21},{1... | collective-permute-start | bytes 1843208 | tf_op jit(solution)/shard_map/ppermute | solution.py:43
  693.2 35.5 %collective-permute-start.105 = (bf16[240,1280]{1,0:T(8,128)(2,1)}, bf16[240,1280]{1,0:T(8,128)(2,1)S(1)}, u32[]{:S(2)}, u32[]{:S(2)}) collective-permute-start(bf16[240,1280]{1,0:T(8,128)(2,1)} %get-tuple-element.110), channel_id=1, source_target_pairs={{16,20},{20,24},{24,28},{28,16},{17,21},{21,25},{25,29},{29,17},{1... | collective-permute-start | bytes 1843208 | tf_op jit(solution)/shard_map/ppermute | solution.py:43
  706.0 30.3 %collective-permute-start.100 = (bf16[240,1280]{1,0:T(8,128)(2,1)}, bf16[240,1280]{1,0:T(8,128)(2,1)S(1)}, u32[]{:S(2)}, u32[]{:S(2)}) collective-permute-start(bf16[240,1280]{1,0:T(8,128)(2,1)} %get-tuple-element.114), channel_id=1, source_target_pairs={{0,12},{4,0},{8,4},{12,8},{1,13},{5,1},{9,5},{13,9},{2,14},{6,2},{... | collective-permute-start | bytes 1843208 | tf_op jit(solution)/shard_map/ppermute | solution.py:43
  723.1 27.9 %collective-permute-start.99 = (bf16[240,1280]{1,0:T(8,128)(2,1)}, bf16[240,1280]{1,0:T(8,128)(2,1)S(1)}, u32[]{:S(2)}, u32[]{:S(2)}) collective-permute-start(bf16[240,1280]{1,0:T(8,128)(2,1)} %get-tuple-element.115), channel_id=1, source_target_pairs={{0,8},{4,12},{8,0},{12,4},{1,9},{5,13},{9,1},{13,5},{2,10},{6,14},... | collective-permute-start | bytes 1843208 | tf_op jit(solution)/shard_map/ppermute | solution.py:43
  725.0 25.9 %collective-permute-start.98 = (bf16[240,1280]{1,0:T(8,128)(2,1)}, bf16[240,1280]{1,0:T(8,128)(2,1)}, u32[]{:S(2)}, u32[]{:S(2)}) collective-permute-start(bf16[240,1280]{1,0:T(8,128)(2,1)} %get-tuple-element.113), channel_id=1, source_target_pairs={{0,4},{4,8},{8,12},{12,0},{1,5},{5,9},{9,13},{13,1},{2,6},{6,10},{... | collective-permute-start | bytes 1843208 | tf_op jit(solution)/shard_map/ppermute | solution.py:43
  730.7 27.9 %collective-permute-start.108 = (bf16[240,1280]{1,0:T(8,128)(2,1)S(1)}, bf16[240,1280]{1,0:T(8,128)(2,1)}, u32[]{:S(2)}, u32[]{:S(2)}) collective-permute-start(bf16[240,1280]{1,0:T(8,128)(2,1)S(1)} %get-tuple-element.87), channel_id=1, source_target_pairs={{16,17},{17,16},{18,19},{19,18},{20,21},{21,20},{22,23},{23,22},{2... | collective-permute-start | bytes 1843208 | tf_op jit(solution)/shard_map/ppermute | solution.py:50
  735.6 27.7 %collective-permute-start.109 = (bf16[240,1280]{1,0:T(8,128)(2,1)S(1)}, bf16[240,1280]{1,0:T(8,128)(2,1)S(1)}, u32[]{:S(2)}, u32[]{:S(2)}) collective-permute-start(bf16[240,1280]{1,0:T(8,128)(2,1)S(1)} %get-tuple-element.87), channel_id=1, source_target_pairs={{16,18},{17,19},{18,16},{19,17},{20,22},{21,23},{22,20},{23,21},{2... | collective-permute-start | bytes 1843208 | tf_op jit(solution)/shard_map/ppermute | solution.py:50
  736.3 27.1 %collective-permute-start.110 = (bf16[240,1280]{1,0:T(8,128)(2,1)S(1)}, bf16[240,1280]{1,0:T(8,128)(2,1)S(1)}, u32[]{:S(2)}, u32[]{:S(2)}) collective-permute-start(bf16[240,1280]{1,0:T(8,128)(2,1)S(1)} %get-tuple-element.87), channel_id=1, source_target_pairs={{16,19},{17,18},{18,17},{19,16},{20,23},{21,22},{22,21},{23,20},{2... | collective-permute-start | bytes 1843208 | tf_op jit(solution)/shard_map/ppermute | solution.py:50
  (196 other events, 1796.8 us)

commit v2 on v1

--- a/solution.py
+++ b/solution.py
@@ -104,6 +104,30 @@
 
 def after(value, earlier):
     return lax.optimization_barrier((value, earlier))[0]
+
+
+def fold(block, width):
+    rows, cols = block.shape[-2], block.shape[-1]
+    if cols % width == 0:
+        return jnp.concatenate(
+            [block[..., start : start + width] for start in range(0, cols, width)], axis=-2
+        )
+    tail = block[..., width:]
+    tail = jnp.concatenate([tail[..., : rows // 2, :], tail[..., rows // 2 :, :]], axis=-1)
+    return jnp.concatenate([block[..., :width], tail], axis=-2)
+
+
+def unfold(block, cols):
+    width = block.shape[-1]
+    if cols % width == 0:
+        rows = block.shape[-2] * width // cols
+        return jnp.concatenate(
+            [block[..., k * rows : (k + 1) * rows, :] for k in range(cols // width)], axis=-1
+        )
+    rows = block.shape[-2] * width // cols
+    tail = block[..., rows:, :]
+    tail = jnp.concatenate([tail[..., : width // 2], tail[..., width // 2 :]], axis=-2)
+    return jnp.concatenate([block[..., :rows, :], tail], axis=-1)
 
 
 def tables(segments):
@@ -235,38 +259,39 @@
     def give(value, owner):
         return jnp.where(core == owner, value, to_core(value, 1 - owner))
 
-    def load_attn(owner, share):
-        rows = z_gather(share, z, owner).reshape(-1, chunk)
-        return give(plane_gather(rows, q, owner), owner)
-
-    def load_ffn(owner, share):
-        return give(z_gather(share, z, owner).reshape(-1, 2 * hid), owner)
-
-    def load_down(owner, share):
-        blocks = plane_trade(z_gather(share, z, owner), q, owner)
-        return give(blocks.reshape(-1, width), owner)
-
-    def whole_sequence(shares):
-        mine = pick(shares[:, 0], core)
+    def both_layers(own):
+        other = swap(own)
+        return [jnp.where(core == layer, own, other) for layer in range(layers)]
+
+    def whole_sequence(mine):
         blocks = plane_gather(mine, q)
-        return place(z_trade(blocks, z)).reshape(-1, width)
-
-    hidden = whole_sequence(hidden_in)
-    segments = pick(plane_gather(pick(segment_ids[:, 0], core), q), z)
+        return lax.all_to_all(blocks, "shard", 0, 0, tiled=False)
+
+    attn_rows = z_gather(attn_share, z, 0).reshape(-1, chunk)
+    turn = to_core(attn_rows[:16, :128], 1)
+    own_segments = lax.dynamic_slice_in_dim(pick(segment_ids[:, 0], core), z * group, group)
+    marks = jnp.zeros((16, width), low).at[0, :group].set(own_segments.astype(low))
+    entry = whole_sequence(jnp.concatenate([pick(hidden_in[:, 0], core), marks]))
+    hidden = entry[:, :group].reshape(-1, width)
+    segments = entry[:, group, :group].reshape(-1).astype(jnp.int32)
     tabs = tables(segments)
-    own_gains = jnp.concatenate([norm_attn, norm_ffn], axis=0)
-    own_gains = z_gather(own_gains, z).transpose(1, 0, 2).reshape(2, -1).astype(wide)
-    other_gains = swap(own_gains.astype(low)).astype(wide)
-    gains = [jnp.where(core == layer, own_gains, other_gains) for layer in range(layers)]
-
-    attn_w, ffn_w, down_w = [None] * 2, [None] * 2, [None] * 2
-    attn_w[0] = load_attn(0, attn_share)
-    ffn_w[0] = load_ffn(0, ffn_share)
-    down_w[0] = load_down(0, down_share)
-    attn_w[1] = load_attn(1, after(attn_share, attn_w[0]))
-    ffn_w[1] = load_ffn(1, after(ffn_share, ffn_w[0]))
-    down_w[1] = load_down(1, after(down_share, down_w[0]))
-    top_grad = whole_sequence(after(out_grad, attn_w[0]))
+
+    own_gains = lax.all_gather(jnp.concatenate([norm_attn, norm_ffn]), "shard")
+    gains = both_layers(own_gains.transpose(1, 0, 2).reshape(2, -1))
+    gains = [gain.astype(wide) for gain in gains]
+
+    ffn_pair = jnp.concatenate([ffn_share, fold(down_share, chunk)], axis=1)
+    ffn_pair = lax.all_gather(ffn_pair, "shard")
+
+    attn_w = [None] * 2
+    attn_w[0] = give(plane_gather(attn_rows, q, 0), 0)
+    rows = z_gather(after(attn_share, turn), z, 1).reshape(-1, chunk)
+    attn_w[1] = give(plane_gather(after(rows, attn_w[0]), q, 1), 1)
+    ffn_w = both_layers(ffn_pair[:, :, : 2 * hid].reshape(-1, 2 * hid))
+    down_w = both_layers(
+        unfold(plane_trade(ffn_pair[:, :, 2 * hid :], q), width).reshape(-1, width)
+    )
+    top_grad = whole_sequence(pick(after(out_grad, attn_w[1])[:, 0], core)).reshape(-1, width)
 
     inputs, kept, outputs = [hidden], [], []
     for layer in range(layers):
@@ -277,10 +302,55 @@
         act = (gate * jax.nn.sigmoid(gate) * up).astype(low)
         kept.append((kept_attn, middle, normed, gate, up, act))
         result = (middle + plane_sum(dot(act, down_w[layer]))).astype(low)
+        if layer == 0:
+            result, top_grad = lax.optimization_barrier((result, top_grad))
         outputs.append(result)
         inputs.append(result)
 
-    gain_grads, input_grads, sums = [None] * 2, [None] * 2, [None] * 2
+    def spread(by_layer):
+        mine = jnp.where(core == 0, by_layer[0], by_layer[1])
+        other = swap(jnp.where(core == 0, by_layer[1], by_layer[0]))
+        stack = jnp.where(
+            core == 0, jnp.stack([mine, other]), jnp.stack([other, mine])
+        ).reshape(2, 4, group, width)
+        replicas = lax.axis_size("replica")
+
+        def slice_for(target):
+            return lax.dynamic_index_in_dim(stack, target, 1, keepdims=False)
+
+        total = jnp.where(z == q, slice_for(z), 0)
+        for hop in (1, 2, 3):
+            pairs = [
+                ((r % TEAM) * replicas + r, (r % TEAM + hop) % 4 * replicas + r)
+                for r in range(replicas)
+            ]
+            total = total + lax.ppermute(slice_for((z + hop) % 4), ("shard", "replica"), pairs)
+        return total[None, :, None]
+
+    def exchange(mine, other):
+        return (mine + swap(other.astype(low)).astype(wide)).astype(low)
+
+    def halves(value):
+        first, second = value
+        return jnp.where(core == 0, first, second), jnp.where(core == 0, second, first)
+
+    def sum_z(stack):
+        total = lax.psum_scatter(stack, "shard", scatter_dimension=0, tiled=False)
+        return teams_sum(total.astype(wide)).astype(low)
+
+    half = chunk // 2
+    split = w_query.shape[2] + w_key.shape[2] * 2
+
+    def attn_half(kept_attn, right, which):
+        start = q * chunk + which * half
+        part = lax.dynamic_slice_in_dim(right, start, half, axis=1)
+        column = start + jnp.arange(half)
+        return jnp.where(
+            column[None, :] < split, dot_l(kept_attn[0], part), dot_l(kept_attn[5], part)
+        )
+
+    gain_grads, input_grads = [None] * 2, [None] * 2
+    attn_sums, pair_sums = [None] * 2, [None] * 2
     grad = top_grad
     for layer in reversed(range(layers)):
         kept_attn, middle, normed, gate, up, act = kept[layer]
@@ -290,59 +360,50 @@
         grad_up = (grad_act * gate * sig).astype(low)
         grad_both = jnp.concatenate([grad_gate, grad_up], axis=1)
         grad_normed = plane_sum(dot_t(grad_both, ffn_w[layer]))
+
+        mine, other = halves((grad_gate, grad_up))
+        ffn_part = exchange(dot_l(normed, mine), dot_l(normed, other))
+        step = down_rows // 2
+        strips = [
+            jnp.concatenate(
+                [act[:, k * down_rows + c * step :][:, :step] for k in range(TEAM)], axis=1
+            )
+            for c in (0, 1)
+        ]
+        mine, other = halves(strips)
+        down_part = exchange(dot_l(mine, grad), dot_l(other, grad))
+        grad_normed, ffn_part, down_part = lax.optimization_barrier(
+            (grad_normed, ffn_part, down_part)
+        )
+        down_part = plane_trade(down_part.reshape(TEAM, step, width), q)
         gain_ffn, through = norm_back(grad_normed, middle, gains[layer][1])
         grad_middle = grad.astype(wide) + through
         grad_in, right, gain_attn = attention_back(
             inputs[layer], grad_middle, tabs, attn_w[layer], gains[layer][0], kept_attn
         )
+        grad = grad_in.astype(low)
+        grad, down_part = lax.optimization_barrier((grad, down_part))
+        pair = jnp.concatenate(
+            [ffn_part.reshape(4, -1, hid), fold(down_part, half)], axis=2
+        )
+        pair_sums[layer] = sum_z(pair)
+        attn_part = exchange(
+            attn_half(kept_attn, right, core), attn_half(kept_attn, right, 1 - core)
+        )
+        attn_sums[layer] = sum_z(attn_part.reshape(4, -1, half))
         gain_grads[layer] = jnp.stack([gain_attn, gain_ffn])
-
-        def collect(partial):
-            return partial + to_core(partial.astype(low), layer).astype(wide)
-
-        def along_z(stack):
-            blocks = z_trade(stack.astype(low), z, layer)
-            total = sum(block.astype(wide) for _, block in blocks)
-            return plane_gather(teams_sum(total).astype(low), q, layer)
-
-        ffn_sum = along_z(collect(dot_l(normed, grad_both)).reshape(4, -1, 2 * hid))
-        down_part = collect(dot_l(act, grad)).astype(low).reshape(TEAM, down_rows, width)
-        down_sum = along_z(plane_trade(down_part, q, layer))
-        own_right = lax.dynamic_slice_in_dim(right, q * chunk, chunk, axis=1)
-        split = w_query.shape[2] + w_key.shape[2] * 2
-        column = q * chunk + jnp.arange(chunk)
-        attn_part = jnp.where(
-            column[None, :] < split,
-            dot_l(kept_attn[0], own_right),
-            dot_l(kept_attn[5], own_right),
-        )
-        attn_sum = along_z(collect(attn_part).reshape(4, -1, chunk))
-        sums[layer] = (attn_sum, ffn_sum, down_sum)
-        grad = grad_in.astype(low)
         input_grads[layer] = grad
-
-    def spread(by_layer):
-        mine = jnp.where(core == 0, by_layer[0], by_layer[1])
-        other = swap(jnp.where(core == 0, by_layer[1], by_layer[0]))
-        stack = jnp.where(
-            core == 0, jnp.stack([mine, other]), jnp.stack([other, mine])
-        ).reshape(2, 4, group, width)
-        replicas = lax.axis_size("replica")
-
-        def slice_for(target):
-            return lax.dynamic_index_in_dim(stack, target, 1, keepdims=False)
-
-        total = jnp.where(z == q, slice_for(z), 0)
-        for hop in (1, 2, 3):
-            pairs = [
-                ((r % TEAM) * replicas + r, (r % TEAM + hop) % 4 * replicas + r)
-                for r in range(replicas)
-            ]
-            total = total + lax.ppermute(slice_for((z + hop) % 4), ("shard", "replica"), pairs)
-        return total[None, :, None]
-
-    layer_out = spread(outputs)
+        if layer == 1:
+            layer_out = spread(outputs)
+
     input_grad = spread(input_grads)
+    whole_1 = plane_gather(jnp.concatenate([pair_sums[1], attn_sums[1]], axis=1), q)
+    whole_0 = jnp.concatenate(
+        [plane_gather(pair_sums[0], q), plane_gather(attn_sums[0], q)], axis=2
+    )
+    own = jnp.where(core == 0, whole_0, whole_1)
+    other = swap(jnp.where(core == 0, whole_1, whole_0))
+    by_half = (jnp.where(core == 0, own, other), jnp.where(core == 0, other, own))
 
     gain_all = jnp.stack(gain_grads)
     gain_all = gain_all + swap(gain_all)
@@ -356,13 +417,17 @@
     total = jnp.where(core == 0, total[0], total[1])
     total = lax.dynamic_index_in_dim(total.reshape(2, 4, -1), z, 1, keepdims=False)
 
-    attn_sum, ffn_sum, down_sum = (
-        jnp.where(core == 0, first, second).astype(wide) for first, second in zip(*sums)
-    )
-    attn_cols = jnp.concatenate([attn_sum[chunk_num] for chunk_num in range(TEAM)], axis=1)
+    attn_cols = jnp.concatenate(
+        [part[num, :, hid + half :] for num in range(TEAM) for part in by_half], axis=1
+    ).astype(wide)
+    gate_cols, up_cols = (
+        jnp.concatenate([part[num, :, :hid] for num in range(TEAM)], axis=1).astype(wide)
+        for part in by_half
+    )
+    down_sum = jnp.stack(
+        [unfold(part[:, :, hid : hid + half], width) for part in by_half], axis=1
+    ).astype(wide)
     qw, kw = w_query.shape[2], w_key.shape[2]
-    gate_cols = jnp.concatenate([ffn_sum[num, :, :hid] for num in range(TEAM)], axis=1)
-    up_cols = jnp.concatenate([ffn_sum[num, :, hid:] for num in range(TEAM)], axis=1)
     return (
         layer_out,
         input_grad,

time: 790 us -> 648 us (0.82)
  starting transfers between devices: 313 us -> 121 us
  waiting for transfers between devices: 136 us -> 222 us
  local copies, waits for them, and re-layouts: 154 us -> 118 us
  other arithmetic: 99.2 us -> 66.8 us
  between operations: 4.08 us -> 16.6 us
  blocking collectives: 0 us -> 10.4 us
  matrix products: 71.3 us -> 81.3 us
    ppermute x48 -> x9, starting transfers between devices: 124 us -> 24.8 us  [z_send(): return lax.ppermute(value, ('section', 'shard'), pairs)]
    ppermute x12 -> x2, starting transfers between devices: 68.9 us -> 5.3 us  [to_core(): return lax.ppermute(value, 'section', [(1 - target, target)])]
    ppermute x48 -> x9, waiting for transfers between devices: 56.6 us -> 2.33 us  [z_send(): return lax.ppermute(value, ('section', 'shard'), pairs)]
    reduce_scatter x0 -> x4, waiting for transfers between devices: none -> 48.7 us  [sum_z(): total = lax.psum_scatter(stack, 'shard', scatter_dimension=0, tiled=False)]
    ppermute x61 -> x46, waiting for transfers between devices: 74.6 us -> 115 us  [plane_send(): return lax.ppermute(value, ('section', 'replica'), pairs)]
    ppermute x61 -> x46, starting transfers between devices: 102 us -> 64.2 us  [plane_send(): return lax.ppermute(value, ('section', 'replica'), pairs)]
    all_to_all x0 -> x2, waiting for transfers between devices: none -> 36.8 us  [whole_sequence(): return lax.all_to_all(blocks, 'shard', 0, 0, tiled=False)]
    dynamic_update_slice x83 -> x43, local copies, waits for them, and re-layouts: 52.6 us -> 34.2 us  [place(): stack = lax.dynamic_update_index_in_dim(stack, block, index, 0)]
  transfers between devices with their start and end apart: 131 -> 83, of which waited for: 32 -> 36; matrix products, arithmetic and copies ran while one was open for 38% -> 26% of each run, Pallas kernels for 0% -> 0%
where the time goes in v2:
time: 648 us; the launch traced here: 637 us
  waiting for transfers between devices  222 us (34%)
  starting transfers between devices  121 us (19%)
  local copies, waits for them, and re-layouts  118 us (18%)
  matrix products  81.3 us (13%)
  other arithmetic  66.8 us (10%)
  between operations  16.6 us (3%)
  blocking collectives  10.4 us (2%)
    ppermute x46, waiting for transfers between devices, plane_send(): return lax.ppermute(value, ('section', 'replica'), pairs)  115 us
    ppermute x46, starting transfers between devices, plane_send(): return lax.ppermute(value, ('section', 'replica'), pairs)  64.2 us
    reduce_scatter x4, waiting for transfers between devices, sum_z(): total = lax.psum_scatter(stack, 'shard', scatter_dimension=0, tiled=False)  48.7 us
    all_to_all x2, waiting for transfers between devices, whole_sequence(): return lax.all_to_all(blocks, 'shard', 0, 0, tiled=False)  36.8 us
    dynamic_update_slice x43, local copies, waits for them, and re-layouts, place(): stack = lax.dynamic_update_index_in_dim(stack, block, index, 0)  34.2 us
    dot_general x14, matrix products, dot(): return jnp.dot(a, b, preferred_element_type=wide)  26.6 us
    ppermute x9, starting transfers between devices, z_send(): return lax.ppermute(value, ('section', 'shard'), pairs)  24.8 us
    unnamed x235, local copies, waits for them, and re-layouts  19.5 us
  transfers between devices with their start and end apart: 83, of which 36 were waited for; matrix products, arithmetic and copies ran while one was open for 26% of the time, Pallas kernels for 0%

profile of v2, /device:TPU:0, one launch (start us, length us, event | category | flops | bytes accessed | tf_op | source)
XLA Modules:
  0.0 636.8 jit_solution(9726010713370771320)
XLA Ops:
  9.5 3.4 concatenate.189
  14.1 4.9 collective-permute-start.4
  19.0 4.5 collective-permute-start.5
  23.6 3.3 collective-permute-start.6
  26.9 10.4 %all-gather.2 = bf16[4,2,240]{2,1,0:T(2,128)(2,1)S(1)} all-gather(bf16[1,2,240]{2,1,0:T(2,128)(2,1)S(1)} %maximum_bitcast_fusion.4), channel_id=2, replica_groups=mesh['section'=2,'shard'=4,'replica'=4] {'shard'}, dimensions={0}, use_global_device_ids=true | all-gather | bytes 4800 | tf_op jit(solution)/shard_map/all_gather | solution.py:279
  43.2 3.4 collective-permute-start.7
  48.0 3.4 collective-permute-start.8
  53.3 3.3 collective-permute-start.9
  64.1 2.9 collective-permute-start.2
  68.1 17.0 %collective-permute-done.8 = bf16[960,640]{1,0:T(8,128)(2,1)} collective-permute-done((bf16[960,640]{1,0:T(8,128)(2,1)S(1)}, bf16[960,640]{1,0:T(8,128)(2,1)}, u32[]{:S(2)}, u32[]{:S(2)}) %collective-permute-start.8) | collective-permute-done | bytes 1228832 | tf_op jit(solution)/shard_map/ppermute | solution.py:50
  91.4 3.5 collective-permute-start.10
  97.6 3.9 all-to-all-start
  103.8 31.4 %all-to-all-done = bf16[4,80,960]{2,1,0:T(8,128)(2,1)S(1)} async-done(((bf16[4,80,960]{2,1,0:T(8,128)(2,1)}), bf16[4,80,960]{2,1,0:T(8,128)(2,1)S(1)}, u32[]{:S(2)}, u32[]{:S(2)}) %all-to-all-start) | async-done | bytes 614432 | tf_op jit(solution)/shard_map/all_to_all | solution.py:268
  147.8 3.9 collective-permute-done.12
  151.7 7.4 %collective-permute-done.13 = bf16[240,640]{1,0:T(8,128)(2,1)S(1)} collective-permute-done((bf16[240,640]{1,0:T(8,128)(2,1)S(1)}, bf16[240,640]{1,0:T(8,128)(2,1)S(1)}, u32[]{:S(2)}, u32[]{:S(2)}) %collective-permute-start.13) | collective-permute-done | bytes 307232 | tf_op jit(solution)/shard_map/ppermute | solution.py:50
  163.1 5.1 broadcast_select_fusion.1
  200.9 3.3 fusion.214
  216.1 2.8 fusion.62
  224.3 2.9 collective-permute-done.16
  232.0 5.1 broadcast_select_fusion
  247.6 3.5 all-to-all-start.1
  255.9 5.5 all-to-all-done.1
  263.6 3.0 fusion.33
  277.3 4.3 fusion.215
  287.8 2.8 fusion.63
  292.2 2.8 convolution_convert_fusion.5
  302.8 5.0 collective-permute-start.42
  314.5 4.1 collective-permute-done.41
  340.2 3.0 collective-permute-done.44
  343.3 3.0 collective-permute-done.46
  353.0 3.6 collective-permute-done.47
  360.1 3.4 collective-permute-done.50
  363.5 4.3 collective-permute-done.48
  416.0 3.1 collective-permute-done.54
  425.1 4.9 collective-permute-done.33
  437.8 39.2 %reduce-scatter.9.cloned.1.call-done = bf16[1,240,960]{2,1,0:T(8,128)(2,1)} async-done(((bf16[4,240,960]{2,1,0:T(8,128)(2,1)}), bf16[1,240,960]{2,1,0:T(8,128)(2,1)}) %reduce-scatter.9.cloned.1.call-update) | async-done | bytes 460816 | tf_op jit(solution)/shard_map/reduce_scatter | solution.py:338
  485.5 10.5 %collective-permute-done.72 = bf16[240,1280]{1,0:T(8,128)(2,1)S(1)} collective-permute-done((bf16[240,1280]{1,0:T(8,128)(2,1)}, bf16[240,1280]{1,0:T(8,128)(2,1)S(1)}, u32[]{:S(2)}, u32[]{:S(2)}) %collective-permute-start.72) | collective-permute-done | bytes 614432 | tf_op jit(solution)/shard_map/ppermute | solution.py:50
  496.0 14.9 %collective-permute-done.73 = bf16[240,1280]{1,0:T(8,128)(2,1)S(1)} collective-permute-done((bf16[240,1280]{1,0:T(8,128)(2,1)}, bf16[240,1280]{1,0:T(8,128)(2,1)S(1)}, u32[]{:S(2)}, u32[]{:S(2)}) %collective-permute-start.73) | collective-permute-done | bytes 614432 | tf_op jit(solution)/shard_map/ppermute | solution.py:50
  511.0 9.4 %reduce-scatter.5.cloned.1.call-done = bf16[1,240,960]{2,1,0:T(8,128)(2,1)} async-done(((bf16[4,240,960]{2,1,0:T(8,128)(2,1)}), bf16[1,240,960]{2,1,0:T(8,128)(2,1)}) %reduce-scatter.5.cloned.1.call-update) | async-done | bytes 460816 | tf_op jit(solution)/shard_map/reduce_scatter | solution.py:338
  525.5 9.4 %collective-permute-done.64 = bf16[240,960]{1,0:T(8,128)(2,1)S(1)} collective-permute-done((bf16[240,960]{1,0:T(8,128)(2,1)}, bf16[240,960]{1,0:T(8,128)(2,1)S(1)}, u32[]{:S(2)}, u32[]{:S(2)}) %collective-permute-start.64) | collective-permute-done | bytes 460832 | tf_op jit(solution)/shard_map/ppermute | solution.py:50
  534.9 10.3 %collective-permute-done.65 = bf16[240,960]{1,0:T(8,128)(2,1)S(1)} collective-permute-done((bf16[240,960]{1,0:T(8,128)(2,1)}, bf16[240,960]{1,0:T(8,128)(2,1)S(1)}, u32[]{:S(2)}, u32[]{:S(2)}) %collective-permute-start.65) | collective-permute-done | bytes 460832 | tf_op jit(solution)/shard_map/ppermute | solution.py:50
  555.1 3.7 collective-permute-start.37
  565.4 4.3 collective-permute-start.63
  571.0 3.4 collective-permute-start.62
  598.7 5.6 collective-permute-done.58
  604.3 3.0 collective-permute-done.57
  609.3 3.6 broadcast_select_fusion.2
  625.6 2.8 maximum_convert_fusion
  (642 shorter events, 318.1 us)
Async XLA Ops:
  7.2 132.6 %all-gather.5.cloned.1.call-start = ((), (), s32[]{:S(2)}) async-start(), calls=%async_computation.10 | async-start | bytes 4608000 | tf_op jit(solution)/shard_map/all_gather | solution.py:284
  14.1 26.0 %collective-permute-start.4 = (bf16[240,640]{1,0:T(8,128)(2,1)S(1)}, bf16[240,640]{1,0:T(8,128)(2,1)}, u32[]{:S(2)}, u32[]{:S(2)}) collective-permute-start(bf16[240,640]{1,0:T(8,128)(2,1)S(1)} %get-tuple-element.134), channel_id=1, source_target_pairs={{0,4},{4,8},{8,12},{12,0},{1,5},{5,9},{9,13},{13,1},{2,6},{6,10},{... | collective-permute-start | bytes 921608 | tf_op jit(solution)/shard_map/ppermute | solution.py:43
  19.0 22.1 %collective-permute-start.5 = (bf16[240,640]{1,0:T(8,128)(2,1)S(1)}, bf16[240,640]{1,0:T(8,128)(2,1)}, u32[]{:S(2)}, u32[]{:S(2)}) collective-permute-start(bf16[240,640]{1,0:T(8,128)(2,1)S(1)} %get-tuple-element.134), channel_id=1, source_target_pairs={{0,8},{4,12},{8,0},{12,4},{1,9},{5,13},{9,1},{13,5},{2,10},{6,14},... | collective-permute-start | bytes 921608 | tf_op jit(solution)/shard_map/ppermute | solution.py:43
  23.6 18.6 %collective-permute-start.6 = (bf16[240,640]{1,0:T(8,128)(2,1)S(1)}, bf16[240,640]{1,0:T(8,128)(2,1)}, u32[]{:S(2)}, u32[]{:S(2)}) collective-permute-start(bf16[240,640]{1,0:T(8,128)(2,1)S(1)} %get-tuple-element.134), channel_id=1, source_target_pairs={{0,12},{4,0},{8,4},{12,8},{1,13},{5,1},{9,5},{13,9},{2,14},{6,2},{... | collective-permute-start | bytes 921608 | tf_op jit(solution)/shard_map/ppermute | solution.py:43
  37.3 21.5 %collective-permute-start.3 = (bf16[2,960]{1,0:T(2,128)(2,1)S(1)}, bf16[2,960]{1,0:T(2,128)(2,1)S(1)}, u32[]{:S(2)}, u32[]{:S(2)}) collective-permute-start(bf16[2,960]{1,0:T(2,128)(2,1)S(1)} %reshape.544), channel_id=1, source_target_pairs={{0,16},{16,0},{1,17},{17,1},{2,18},{18,2},{3,19},{19,3},{4,20},{20... | collective-permute-start | bytes 11528 | tf_op jit(solution)/shard_map/ppermute | solution.py:36
  43.2 20.9 %collective-permute-start.7 = (bf16[960,640]{1,0:T(8,128)(2,1)S(1)}, bf16[960,640]{1,0:T(8,128)(2,1)S(1)}, u32[]{:S(2)}, u32[]{:S(2)}) collective-permute-start(bf16[960,640]{1,0:T(8,128)(2,1)S(1)} %bitcast.461), channel_id=1, source_target_pairs={{0,1},{1,0},{2,3},{3,2},{4,5},{5,4},{6,7},{7,6},{8,9},{9,8},{10,11... | collective-permute-start | bytes 3686408 | tf_op jit(solution)/shard_map/ppermute | solution.py:50
  47.4 44.0 %collective-permute-start = (bf16[80,960]{1,0:T(8,128)(2,1)S(1)}, bf16[80,960]{1,0:T(8,128)(2,1)S(1)}, u32[]{:S(2)}, u32[]{:S(2)}) collective-permute-start(bf16[80,960]{1,0:T(8,128)(2,1)S(1)} %fusion.136), channel_id=1, source_target_pairs={{0,1},{1,0},{2,3},{3,2},{16,17},{17,16},{18,19},{19,18},{4,5},{5,4... | collective-permute-start | bytes 460808 | tf_op jit(solution)/shard_map/ppermute | solution.py:50
  48.0 37.2 %collective-permute-start.8 = (bf16[960,640]{1,0:T(8,128)(2,1)S(1)}, bf16[960,640]{1,0:T(8,128)(2,1)}, u32[]{:S(2)}, u32[]{:S(2)}) collective-permute-start(bf16[960,640]{1,0:T(8,128)(2,1)S(1)} %bitcast.462), channel_id=1, source_target_pairs={{0,2},{1,3},{2,0},{3,1},{4,6},{5,7},{6,4},{7,5},{8,10},{9,11},{10,... | collective-permute-start | bytes 3686408 | tf_op jit(solution)/shard_map/ppermute | solution.py:50
  53.3 35.0 %collective-permute-start.9 = (bf16[960,640]{1,0:T(8,128)(2,1)S(1)}, bf16[960,640]{1,0:T(8,128)(2,1)}, u32[]{:S(2)}, u32[]{:S(2)}) collective-permute-start(bf16[960,640]{1,0:T(8,128)(2,1)S(1)} %bitcast.463), channel_id=1, source_target_pairs={{0,3},{1,2},{2,1},{3,0},{4,7},{5,6},{6,5},{7,4},{8,11},{9,10},{10,... | collective-permute-start | bytes 3686408 | tf_op jit(solution)/shard_map/ppermute | solution.py:50
  58.8 36.7 %collective-permute-start.1 = (bf16[80,960]{1,0:T(8,128)(2,1)S(1)}, bf16[80,960]{1,0:T(8,128)(2,1)S(1)}, u32[]{:S(2)}, u32[]{:S(2)}) collective-permute-start(bf16[80,960]{1,0:T(8,128)(2,1)S(1)} %fusion.136), channel_id=1, source_target_pairs={{0,2},{1,3},{2,0},{3,1},{16,18},{17,19},{18,16},{19,17},{4,6},{5,7... | collective-permute-start | bytes 460808 | tf_op jit(solution)/shard_map/ppermute | solution.py:50
  64.1 32.9 %collective-permute-start.2 = (bf16[80,960]{1,0:T(8,128)(2,1)S(1)}, bf16[80,960]{1,0:T(8,128)(2,1)S(1)}, u32[]{:S(2)}, u32[]{:S(2)}) collective-permute-start(bf16[80,960]{1,0:T(8,128)(2,1)S(1)} %fusion.136), channel_id=1, source_target_pairs={{0,3},{1,2},{2,1},{3,0},{16,19},{17,18},{18,17},{19,16},{4,7},{5,6... | collective-permute-start | bytes 460808 | tf_op jit(solution)/shard_map/ppermute | solution.py:50
  85.1 16.4 %collective-permute-start.20 = (bf16[240,640]{1,0:T(8,128)(2,1)S(1)}, bf16[240,640]{1,0:T(8,128)(2,1)S(1)}, u32[]{:S(2)}, u32[]{:S(2)}) collective-permute-start(bf16[240,640]{1,0:T(8,128)(2,1)S(1)} %get-tuple-element.134), channel_id=1, source_target_pairs={{16,20},{20,24},{24,28},{28,16},{17,21},{21,25},{25,29},{29,17},{1... | collective-permute-start | bytes 921608 | tf_op jit(solution)/shard_map/ppermute | solution.py:43
  88.3 14.0 %collective-permute-start.21 = (bf16[240,640]{1,0:T(8,128)(2,1)S(1)}, bf16[240,640]{1,0:T(8,128)(2,1)S(1)}, u32[]{:S(2)}, u32[]{:S(2)}) collective-permute-start(bf16[240,640]{1,0:T(8,128)(2,1)S(1)} %get-tuple-element.134), channel_id=1, source_target_pairs={{16,24},{20,28},{24,16},{28,20},{17,25},{21,29},{25,17},{29,21},{1... | collective-permute-start | bytes 921608 | tf_op jit(solution)/shard_map/ppermute | solution.py:43
  91.4 71.7 %collective-permute-start.10 = (bf16[4,960,640]{2,1,0:T(8,128)(2,1)}, bf16[4,960,640]{2,1,0:T(8,128)(2,1)}, u32[]{:S(2)}, u32[]{:S(2)}) collective-permute-start(bf16[4,960,640]{2,1,0:T(8,128)(2,1)} %bitcast_dynamic-update-slice_fusion.4), channel_id=1, source_target_pairs={{0,16},{1,17},{2,18},{3,19},{4,20},{5,21},{6,22},{7,23},{8,24},{9,... | collective-permute-start | bytes 14745608 | tf_op jit(solution)/shard_map/ppermute | solution.py:32
  97.6 37.6 %all-to-all-start = ((bf16[4,80,960]{2,1,0:T(8,128)(2,1)}), bf16[4,80,960]{2,1,0:T(8,128)(2,1)S(1)}, u32[]{:S(2)}, u32[]{:S(2)}) async-start(bf16[4,80,960]{2,1,0:T(8,128)(2,1)} %bitcast_dynamic-update-slice_fusion.35), calls=%async_computation | async-start | bytes 1310720 | tf_op jit(solution)/shard_map/all_to_all | solution.py:268
  143.1 16.0 %collective-permute-start.13 = (bf16[240,640]{1,0:T(8,128)(2,1)S(1)}, bf16[240,640]{1,0:T(8,128)(2,1)S(1)}, u32[]{:S(2)}, u32[]{:S(2)}) collective-permute-start(bf16[240,640]{1,0:T(8,128)(2,1)S(1)} %get-tuple-element.171), channel_id=1, source_target_pairs={{0,2},{1,3},{2,0},{3,1},{16,18},{17,19},{18,16},{19,17},{4,6},{5,7... | collective-permute-start | bytes 921608 | tf_op jit(solution)/shard_map/ppermute | solution.py:50
  147.0 69.1 %collective-permute-start.11 = (bf16[960,1280]{1,0:T(8,128)(2,1)}, bf16[960,1280]{1,0:T(8,128)(2,1)}, u32[]{:S(2)}, u32[]{:S(2)}) collective-permute-start(bf16[960,1280]{1,0:T(8,128)(2,1)} %bitcast.49), channel_id=1, source_target_pairs={{0,16},{16,0},{1,17},{17,1},{2,18},{18,2},{3,19},{19,3},{4,20},{20... | collective-permute-start | bytes 7372808 | tf_op jit(solution)/shard_map/ppermute | solution.py:36
  163.1 50.4 %collective-permute-start.15 = (bf16[640,960]{0,1:T(8,128)(2,1)}, bf16[640,960]{0,1:T(8,128)(2,1)}, u32[]{:S(2)}, u32[]{:S(2)}) collective-permute-start(bf16[640,960]{0,1:T(8,128)(2,1)} %copy.449), channel_id=1, source_target_pairs={{0,16},{16,0},{1,17},{17,1},{2,18},{18,2},{3,19},{19,3},{4,20},{20... | collective-permute-start | bytes 3686408 | tf_op jit(solution)/shard_map/ppermute | solution.py:36
  168.2 22.5 %collective-permute-start.23 = (bf16[960,640]{1,0:T(8,128)(2,1)}, bf16[960,640]{1,0:T(8,128)(2,1)}, u32[]{:S(2)}, u32[]{:S(2)}) collective-permute-start(bf16[960,640]{1,0:T(8,128)(2,1)} %bitcast.61), channel_id=1, source_target_pairs={{16,17},{17,16},{18,19},{19,18},{20,21},{21,20},{22,23},{23,22},{2... | collective-permute-start | bytes 3686408 | tf_op jit(solution)/shard_map/ppermute | solution.py:50
  170.0 23.2 %collective-permute-start.24 = (bf16[960,640]{1,0:T(8,128)(2,1)}, bf16[960,640]{1,0:T(8,128)(2,1)}, u32[]{:S(2)}, u32[]{:S(2)}) collective-permute-start(bf16[960,640]{1,0:T(8,128)(2,1)} %bitcast.61), channel_id=1, source_target_pairs={{16,18},{17,19},{18,16},{19,17},{20,22},{21,23},{22,20},{23,21},{2... | collective-permute-start | bytes 3686408 | tf_op jit(solution)/shard_map/ppermute | solution.py:50
  171.7 23.9 %collective-permute-start.25 = (bf16[960,640]{1,0:T(8,128)(2,1)}, bf16[960,640]{1,0:T(8,128)(2,1)}, u32[]{:S(2)}, u32[]{:S(2)}) collective-permute-start(bf16[960,640]{1,0:T(8,128)(2,1)} %bitcast.61), channel_id=1, source_target_pairs={{16,19},{17,18},{18,17},{19,16},{20,23},{21,22},{22,21},{23,20},{2... | collective-permute-start | bytes 3686408 | tf_op jit(solution)/shard_map/ppermute | solution.py:50
  198.1 33.9 %collective-permute-start.26 = (bf16[4,960,640]{2,1,0:T(8,128)(2,1)}, bf16[4,960,640]{2,1,0:T(8,128)(2,1)}, u32[]{:S(2)}, u32[]{:S(2)}) collective-permute-start(bf16[4,960,640]{2,1,0:T(8,128)(2,1)} %bitcast_dynamic-update-slice_fusion), channel_id=1, source_target_pairs={{16,0},{17,1},{18,2},{19,3},{20,4},{21,5},{22,6},{23,7},{24,8},{25... | collective-permute-start | bytes 14745608 | tf_op jit(solution)/shard_map/ppermute | solution.py:32
  230.5 20.8 %collective-permute-start.17 = (bf16[128,960]{0,1:T(8,128)(2,1)S(1)}, bf16[128,960]{0,1:T(8,128)(2,1)}, u32[]{:S(2)}, u32[]{:S(2)}) collective-permute-start(bf16[128,960]{0,1:T(8,128)(2,1)S(1)} %get-tuple-element.220), channel_id=1, source_target_pairs={{0,2},{1,3},{2,0},{3,1},{16,18},{17,19},{18,16},{19,17},{4,6},{5,7... | collective-permute-start | bytes 737288 | tf_op jit(solution)/shard_map/ppermute | solution.py:50
  247.6 13.7 %all-to-all-start.1 = ((bf16[4,64,960]{2,1,0:T(8,128)(2,1)}), bf16[4,64,960]{2,1,0:T(8,128)(2,1)S(1)}, u32[]{:S(2)}, u32[]{:S(2)}) async-start(bf16[4,64,960]{2,1,0:T(8,128)(2,1)} %bitcast_dynamic-update-slice_fusion.39), calls=%async_computation.1 | async-start | bytes 1048576 | tf_op jit(solution)/shard_map/all_to_all | solution.py:268
  251.1 182.2 %reduce-scatter.7.cloned.1.call-start = ((), (), s32[]{:S(2)}) async-start(), calls=%async_computation.7 | async-start | bytes 921600 | tf_op jit(solution)/shard_map/reduce_scatter | solution.py:338
  302.8 19.5 %collective-permute-start.42 = (bf16[960,640]{1,0:T(8,128)(2,1)}, bf16[960,640]{1,0:T(8,128)(2,1)S(1)}, u32[]{:S(2)}, u32[]{:S(2)}) collective-permute-start(bf16[960,640]{1,0:T(8,128)(2,1)} %convolution_convert_fusion.1), channel_id=1, source_target_pairs={{0,16},{16,0},{1,17},{17,1},{2,18},{18,2},{3,19},{19,3},{4,20},{20... | collective-permute-start | bytes 3686408 | tf_op jit(solution)/shard_map/ppermute | solution.py:36
  352.9 16.6 %collective-permute-start.51 = (bf16[960,640]{1,0:T(8,128)(2,1)S(1)}, bf16[960,640]{1,0:T(8,128)(2,1)S(1)}, u32[]{:S(2)}, u32[]{:S(2)}) collective-permute-start(bf16[960,640]{1,0:T(8,128)(2,1)S(1)} %convolution_convert_fusion), channel_id=1, source_target_pairs={{0,16},{16,0},{1,17},{17,1},{2,18},{18,2},{3,19},{19,3},{4,20},{20... | collective-permute-start | bytes 3686408 | tf_op jit(solution)/shard_map/ppermute | solution.py:36
  387.4 50.4 %reduce-scatter.11.cloned.1.call-start = ((), (), s32[]{:S(2)}) async-start(), calls=%async_computation.9 | async-start | bytes 921600 | tf_op jit(solution)/shard_map/reduce_scatter | solution.py:338
  396.9 80.1 %reduce-scatter.9.cloned.1.call-start = ((), (), s32[]{:S(2)}) async-start(), calls=%async_computation.8 | async-start | bytes 2457600 | tf_op jit(solution)/shard_map/reduce_scatter | solution.py:338
  400.2 120.3 %reduce-scatter.5.cloned.1.call-start = ((), (), s32[]{:S(2)}) async-start(), calls=%async_computation.6 | async-start | bytes 2457600 | tf_op jit(solution)/shard_map/reduce_scatter | solution.py:338
  403.5 17.5 %collective-permute-start.30 = (bf16[128,960]{0,1:T(8,128)(2,1)}, bf16[128,960]{0,1:T(8,128)(2,1)}, u32[]{:S(2)}, u32[]{:S(2)}) collective-permute-start(bf16[128,960]{0,1:T(8,128)(2,1)} %get-tuple-element.218), channel_id=1, source_target_pairs={{0,1},{1,0},{2,3},{3,2},{16,17},{17,16},{18,19},{19,18},{4,5},{5,4... | collective-permute-start | bytes 737288 | tf_op jit(solution)/shard_map/ppermute | solution.py:50
  404.2 16.8 %collective-permute-start.32 = (bf16[128,960]{0,1:T(8,128)(2,1)}, bf16[128,960]{0,1:T(8,128)(2,1)}, u32[]{:S(2)}, u32[]{:S(2)}) collective-permute-start(bf16[128,960]{0,1:T(8,128)(2,1)} %get-tuple-element.219), channel_id=1, source_target_pairs={{0,2},{1,3},{2,0},{3,1},{16,18},{17,19},{18,16},{19,17},{4,6},{5,7... | collective-permute-start | bytes 737288 | tf_op jit(solution)/shard_map/ppermute | solution.py:50
  406.3 12.9 %collective-permute-start.54 = (bf16[80,960]{1,0:T(8,128)(2,1)S(1)}, bf16[80,960]{1,0:T(8,128)(2,1)S(1)}, u32[]{:S(2)}, u32[]{:S(2)}) collective-permute-start(bf16[80,960]{1,0:T(8,128)(2,1)S(1)} %get-tuple-element.197), channel_id=1, source_target_pairs={{0,2},{1,3},{2,0},{3,1},{16,18},{17,19},{18,16},{19,17},{4,6},{5,7... | collective-permute-start | bytes 460808 | tf_op jit(solution)/shard_map/ppermute | solution.py:50
  433.3 117.8 %collective-permute-start.34 = (bf16[256,960]{0,1:T(8,128)(2,1)}, bf16[256,960]{0,1:T(8,128)(2,1)}, u32[]{:S(2)}, u32[]{:S(2)}) collective-permute-start(bf16[256,960]{0,1:T(8,128)(2,1)} %broadcast_select_fusion.20), channel_id=1, source_target_pairs={{0,16},{16,0},{1,17},{17,1},{2,18},{18,2},{3,19},{19,3},{4,20},{20... | collective-permute-start | bytes 1474568 | tf_op jit(solution)/shard_map/ppermute | solution.py:36
  433.3 47.2 %collective-permute-start.68 = (bf16[240,320]{1,0:T(8,128)(2,1)}, bf16[240,320]{1,0:T(8,128)(2,1)}, u32[]{:S(2)}, u32[]{:S(2)}) collective-permute-start(bf16[240,320]{1,0:T(8,128)(2,1)} %bitcast.524), channel_id=1, source_target_pairs={{0,1},{1,0},{2,3},{3,2},{16,17},{17,16},{18,19},{19,18},{4,5},{5,4... | collective-permute-start | bytes 460808 | tf_op jit(solution)/shard_map/ppermute | solution.py:50
  433.7 47.7 %collective-permute-start.69 = (bf16[240,320]{1,0:T(8,128)(2,1)}, bf16[240,320]{1,0:T(8,128)(2,1)}, u32[]{:S(2)}, u32[]{:S(2)}) collective-permute-start(bf16[240,320]{1,0:T(8,128)(2,1)} %bitcast.525), channel_id=1, source_target_pairs={{0,2},{1,3},{2,0},{3,1},{16,18},{17,19},{18,16},{19,17},{4,6},{5,7... | collective-permute-start | bytes 460808 | tf_op jit(solution)/shard_map/ppermute | solution.py:50
  435.1 48.8 %collective-permute-start.70 = (bf16[240,320]{1,0:T(8,128)(2,1)}, bf16[240,320]{1,0:T(8,128)(2,1)}, u32[]{:S(2)}, u32[]{:S(2)}) collective-permute-start(bf16[240,320]{1,0:T(8,128)(2,1)} %bitcast.526), channel_id=1, source_target_pairs={{0,3},{1,2},{2,1},{3,0},{16,19},{17,18},{18,17},{19,16},{4,7},{5,6... | collective-permute-start | bytes 460808 | tf_op jit(solution)/shard_map/ppermute | solution.py:50
  479.0 17.0 %collective-permute-start.72 = (bf16[240,1280]{1,0:T(8,128)(2,1)}, bf16[240,1280]{1,0:T(8,128)(2,1)S(1)}, u32[]{:S(2)}, u32[]{:S(2)}) collective-permute-start(bf16[240,1280]{1,0:T(8,128)(2,1)} %get-tuple-element.126), channel_id=1, source_target_pairs={{0,1},{1,0},{2,3},{3,2},{16,17},{17,16},{18,19},{19,18},{4,5},{5,4... | collective-permute-start | bytes 1843208 | tf_op jit(solution)/shard_map/ppermute | solution.py:50
  482.4 28.6 %collective-permute-start.73 = (bf16[240,1280]{1,0:T(8,128)(2,1)}, bf16[240,1280]{1,0:T(8,128)(2,1)S(1)}, u32[]{:S(2)}, u32[]{:S(2)}) collective-permute-start(bf16[240,1280]{1,0:T(8,128)(2,1)} %get-tuple-element.126), channel_id=1, source_target_pairs={{0,2},{1,3},{2,0},{3,1},{16,18},{17,19},{18,16},{19,17},{4,6},{5,7... | collective-permute-start | bytes 1843208 | tf_op jit(solution)/shard_map/ppermute | solution.py:50
  484.9 38.5 %collective-permute-start.74 = (bf16[240,1280]{1,0:T(8,128)(2,1)}, bf16[240,1280]{1,0:T(8,128)(2,1)}, u32[]{:S(2)}, u32[]{:S(2)}) collective-permute-start(bf16[240,1280]{1,0:T(8,128)(2,1)} %get-tuple-element.126), channel_id=1, source_target_pairs={{0,3},{1,2},{2,1},{3,0},{16,19},{17,18},{18,17},{19,16},{4,7},{5,6... | collective-permute-start | bytes 1843208 | tf_op jit(solution)/shard_map/ppermute | solution.py:50
  520.5 14.3 %collective-permute-start.64 = (bf16[240,960]{1,0:T(8,128)(2,1)}, bf16[240,960]{1,0:T(8,128)(2,1)S(1)}, u32[]{:S(2)}, u32[]{:S(2)}) collective-permute-start(bf16[240,960]{1,0:T(8,128)(2,1)} %bitcast.514), channel_id=1, source_target_pairs={{0,1},{1,0},{2,3},{3,2},{16,17},{17,16},{18,19},{19,18},{4,5},{5,4... | collective-permute-start | bytes 1382408 | tf_op jit(solution)/shard_map/ppermute | solution.py:50
  522.0 23.2 %collective-permute-start.65 = (bf16[240,960]{1,0:T(8,128)(2,1)}, bf16[240,960]{1,0:T(8,128)(2,1)S(1)}, u32[]{:S(2)}, u32[]{:S(2)}) collective-permute-start(bf16[240,960]{1,0:T(8,128)(2,1)} %bitcast.515), channel_id=1, source_target_pairs={{0,2},{1,3},{2,0},{3,1},{16,18},{17,19},{18,16},{19,17},{4,6},{5,7... | collective-permute-start | bytes 1382408 | tf_op jit(solution)/shard_map/ppermute | solution.py:50
  524.5 20.7 %collective-permute-start.66 = (bf16[240,960]{1,0:T(8,128)(2,1)}, bf16[240,960]{1,0:T(8,128)(2,1)S(1)}, u32[]{:S(2)}, u32[]{:S(2)}) collective-permute-start(bf16[240,960]{1,0:T(8,128)(2,1)} %bitcast.516), channel_id=1, source_target_pairs={{0,3},{1,2},{2,1},{3,0},{16,19},{17,18},{18,17},{19,16},{4,7},{5,6... | collective-permute-start | bytes 1382408 | tf_op jit(solution)/shard_map/ppermute | solution.py:50
  549.0 60.2 %collective-permute-start.75 = (bf16[4,240,1280]{2,1,0:T(8,128)(2,1)}, bf16[4,240,1280]{2,1,0:T(8,128)(2,1)}, u32[]{:S(2)}, u32[]{:S(2)}) collective-permute-start(bf16[4,240,1280]{2,1,0:T(8,128)(2,1)} %broadcast_select_fusion.4), channel_id=1, source_target_pairs={{0,16},{16,0},{1,17},{17,1},{2,18},{18,2},{3,19},{19,3},{4,20},{20... | collective-permute-start | bytes 7372808 | tf_op jit(solution)/shard_map/ppermute | solution.py:36
  560.1 16.6 %collective-permute-start.35 = (bf16[2,64,960]{2,1,0:T(8,128)(2,1)S(1)}, bf16[2,64,960]{2,1,0:T(8,128)(2,1)S(1)}, u32[]{:S(2)}, u32[]{:S(2)}) collective-permute-start(bf16[2,64,960]{2,1,0:T(8,128)(2,1)S(1)} %get-tuple-element.177), channel_id=1, source_target_pairs={{0,4},{5,9},{10,14},{15,3},{16,20},{21,25},{26,30},{31,19}} | collective-permute-start | bytes 737288 | tf_op jit(solution)/shard_map/ppermute | solution.py:327
  562.8 21.4 %collective-permute-start.56 = (bf16[256,960]{0,1:T(8,128)(2,1)}, bf16[256,960]{0,1:T(8,128)(2,1)}, u32[]{:S(2)}, u32[]{:S(2)}) collective-permute-start(bf16[256,960]{0,1:T(8,128)(2,1)} %get-tuple-element.181), channel_id=1, source_target_pairs={{0,16},{16,0},{1,17},{17,1},{2,18},{18,2},{3,19},{19,3},{4,20},{20... | collective-permute-start | bytes 1474568 | tf_op jit(solution)/shard_map/ppermute | solution.py:36
  565.4 14.5 %collective-permute-start.63 = (f32[2,2,960]{2,1,0:T(2,128)S(1)}, f32[2,2,960]{2,1,0:T(2,128)S(1)}, u32[]{:S(2)}, u32[]{:S(2)}) collective-permute-start(f32[2,2,960]{2,1,0:T(2,128)S(1)} %fusion.182), channel_id=1, source_target_pairs={{0,12},{4,0},{8,4},{12,8},{16,28},{20,16},{24,20},{28,24},{1,13},{... | collective-permute-start | bytes 46088 | tf_op jit(solution)/shard_map/ppermute | solution.py:43
  594.4 12.9 %collective-permute-start.57 = (bf16[2,64,960]{2,1,0:T(8,128)(2,1)S(1)}, bf16[2,64,960]{2,1,0:T(8,128)(2,1)}, u32[]{:S(2)}, u32[]{:S(2)}) collective-permute-start(bf16[2,64,960]{2,1,0:T(8,128)(2,1)S(1)} %get-tuple-element.174), channel_id=1, source_target_pairs={{0,4},{5,9},{10,14},{15,3},{16,20},{21,25},{26,30},{31,19}} | collective-permute-start | bytes 737288 | tf_op jit(solution)/shard_map/ppermute | solution.py:327
  (151 other events, 951.9 us)
Sparse Core Ops, SparseCore 0:
  40.1 99.6 all-gather.4
  387.5 21.1 reduce-scatter.6
  411.6 21.9 reduce-scatter.10
  436.4 40.6 reduce-scatter.8
  479.8 40.6 reduce-scatter.4

commit v3 on v2

--- a/solution.py
+++ b/solution.py
@@ -1,6 +1,8 @@
 import jax
 import jax.numpy as jnp
 from jax import lax
+from jax.experimental import pallas as pl
+from jax.experimental.pallas import tpu as pltpu
 from jax.sharding import PartitionSpec as P
 
 QH = 15
@@ -54,11 +56,32 @@
     return lax.dynamic_index_in_dim(stack, index, 0, keepdims=False)
 
 
+def place_kernel(index_ref, *refs):
+    *blocks, stack, sems = refs
+    copies = [
+        pltpu.make_async_copy(block, stack.at[index_ref[k]], sems.at[k])
+        for k, block in enumerate(blocks)
+    ]
+    for copy in copies:
+        copy.start()
+    for copy in copies:
+        copy.wait()
+
+
 def place(parts):
-    stack = jnp.zeros((len(parts),) + parts[0][1].shape, parts[0][1].dtype)
-    for index, block in parts:
-        stack = lax.dynamic_update_index_in_dim(stack, block, index, 0)
-    return stack
+    count, block = len(parts), parts[0][1]
+    shape = jax.ShapeDtypeStruct((count,) + block.shape, block.dtype)
+    moved = 2 * count * block.size * block.dtype.itemsize
+    return pl.pallas_call(
+        place_kernel,
+        out_shape=shape,
+        in_specs=[pl.BlockSpec(memory_space=pltpu.SMEM)]
+        + [pl.BlockSpec(memory_space=pltpu.VMEM)] * count,
+        out_specs=pl.BlockSpec(memory_space=pl.ANY),
+        scratch_shapes=[pltpu.SemaphoreType.DMA((count,))],
+        cost_estimate=pl.CostEstimate(flops=0, bytes_accessed=moved, transcendentals=0),
+        compiler_params=pltpu.CompilerParams(vmem_limit_bytes=24 * 2**20),
+    )(jnp.stack([jnp.asarray(i, jnp.int32) for i, _ in parts]), *(b for _, b in parts))
 
 
 def z_gather(block, z, core=None):
@@ -247,14 +270,21 @@
     down_rows = w_down.shape[1] // TEAM
     attn_all = jnp.concatenate([w_query[0], w_key[0], w_value[0], w_out[0]], axis=1)
     attn_share = lax.dynamic_slice_in_dim(attn_all, q * chunk, chunk, axis=1)
-    ffn_share = jnp.concatenate(
-        [
-            lax.dynamic_slice_in_dim(w_gate[0], q * hid, hid, axis=1),
-            lax.dynamic_slice_in_dim(w_up[0], q * hid, hid, axis=1),
-        ],
-        axis=1,
-    )
-    down_share = lax.dynamic_slice_in_dim(w_down[0], q * down_rows, down_rows, axis=0)
+    half, strip = chunk // 2, down_rows // 2
+    own_hid = hid // 2
+
+    def ffn_half(which):
+        start = q * hid + which * own_hid
+        gate, up = (
+            lax.dynamic_slice_in_dim(w[0], start, own_hid, axis=1) for w in (w_gate, w_up)
+        )
+        down = lax.dynamic_slice_in_dim(w_down[0], which * own_hid + q * strip, strip, axis=0)
+        return jnp.concatenate([gate, up, fold(down, half)], axis=1)
+
+    ffn_low, ffn_high = ffn_half(0), ffn_half(1)
+    ffn_keep = jnp.where(core == 0, ffn_low, ffn_high)
+    ffn_got = swap(jnp.where(core == 0, ffn_high, ffn_low))
+    ffn_shares = [jnp.where(core == layer, ffn_keep, ffn_got) for layer in range(layers)]
 
     def give(value, owner):
         return jnp.where(core == owner, value, to_core(value, 1 - owner))
@@ -267,41 +297,51 @@
         blocks = plane_gather(mine, q)
         return lax.all_to_all(blocks, "shard", 0, 0, tiled=False)
 
+    own_segments = lax.dynamic_slice_in_dim(pick(segment_ids[:, 0], core), z * group, group)
+    marks = jnp.zeros((16, width), low)
+    marks = marks.at[0, :group].set(own_segments.astype(low))
+    marks = marks.at[1, : norm_attn.shape[1]].set(norm_attn[0])
+    marks = marks.at[2, : norm_ffn.shape[1]].set(norm_ffn[0])
+    entry = whole_sequence(jnp.concatenate([pick(hidden_in[:, 0], core), marks]))
     attn_rows = z_gather(attn_share, z, 0).reshape(-1, chunk)
+    attn_rows, entry, ffn_shares = lax.optimization_barrier((attn_rows, entry, ffn_shares))
     turn = to_core(attn_rows[:16, :128], 1)
-    own_segments = lax.dynamic_slice_in_dim(pick(segment_ids[:, 0], core), z * group, group)
-    marks = jnp.zeros((16, width), low).at[0, :group].set(own_segments.astype(low))
-    entry = whole_sequence(jnp.concatenate([pick(hidden_in[:, 0], core), marks]))
     hidden = entry[:, :group].reshape(-1, width)
     segments = entry[:, group, :group].reshape(-1).astype(jnp.int32)
     tabs = tables(segments)
-
-    own_gains = lax.all_gather(jnp.concatenate([norm_attn, norm_ffn]), "shard")
+    own_gains = entry[:, group + 1 : group + 3, : norm_attn.shape[1]]
     gains = both_layers(own_gains.transpose(1, 0, 2).reshape(2, -1))
     gains = [gain.astype(wide) for gain in gains]
 
-    ffn_pair = jnp.concatenate([ffn_share, fold(down_share, chunk)], axis=1)
-    ffn_pair = lax.all_gather(ffn_pair, "shard")
-
-    attn_w = [None] * 2
+    attn_w, ffn_w, down_w = [None] * 2, [None] * 2, [None] * 2
     attn_w[0] = give(plane_gather(attn_rows, q, 0), 0)
     rows = z_gather(after(attn_share, turn), z, 1).reshape(-1, chunk)
+    earlier = entry
+    for layer in range(layers):
+        blocks = lax.all_gather(after(ffn_shares[layer], earlier), "shard")
+        own = blocks[:, :, : 2 * own_hid].reshape(-1, 2 * own_hid)
+        ffn_w[layer] = (own, swap(own))
+        own = unfold(plane_trade(blocks[:, :, 2 * own_hid :], q), width).reshape(-1, width)
+        down_w[layer] = (own, swap(own))
+        earlier = blocks
     attn_w[1] = give(plane_gather(after(rows, attn_w[0]), q, 1), 1)
-    ffn_w = both_layers(ffn_pair[:, :, : 2 * hid].reshape(-1, 2 * hid))
-    down_w = both_layers(
-        unfold(plane_trade(ffn_pair[:, :, 2 * hid :], q), width).reshape(-1, width)
-    )
     top_grad = whole_sequence(pick(after(out_grad, attn_w[1])[:, 0], core)).reshape(-1, width)
 
     inputs, kept, outputs = [hidden], [], []
     for layer in range(layers):
         middle, kept_attn = attention_fwd(inputs[layer], tabs, attn_w[layer], gains[layer][0])
         normed = (middle * row_scale(middle) * gains[layer][1]).astype(low)
-        both = dot(normed, ffn_w[layer])
-        gate, up = both[:, :hid], both[:, hid:]
-        act = (gate * jax.nn.sigmoid(gate) * up).astype(low)
-        kept.append((kept_attn, middle, normed, gate, up, act))
-        result = (middle + plane_sum(dot(act, down_w[layer]))).astype(low)
+        gates, ups, acts, partial = [], [], [], 0.0
+        for weights, down in zip(ffn_w[layer], down_w[layer]):
+            both = dot(normed, weights)
+            gate, up = both[:, :own_hid], both[:, own_hid:]
+            act = (gate * jax.nn.sigmoid(gate) * up).astype(low)
+            partial = partial + dot(act, down)
+            gates.append(gate)
+            ups.append(up)
+            acts.append(act)
+        kept.append((kept_attn, middle, normed, gates, ups, acts))
+        result = (middle + plane_sum(partial)).astype(low)
         if layer == 0:
             result, top_grad = lax.optimization_barrier((result, top_grad))
         outputs.append(result)
@@ -330,15 +370,10 @@
     def exchange(mine, other):
         return (mine + swap(other.astype(low)).astype(wide)).astype(low)
 
-    def halves(value):
-        first, second = value
-        return jnp.where(core == 0, first, second), jnp.where(core == 0, second, first)
-
     def sum_z(stack):
         total = lax.psum_scatter(stack, "shard", scatter_dimension=0, tiled=False)
         return teams_sum(total.astype(wide)).astype(low)
 
-    half = chunk // 2
     split = w_query.shape[2] + w_key.shape[2] * 2
 
     def attn_half(kept_attn, right, which):
@@ -353,57 +388,55 @@
     attn_sums, pair_sums = [None] * 2, [None] * 2
     grad = top_grad
     for layer in reversed(range(layers)):
-        kept_attn, middle, normed, gate, up, act = kept[layer]
-        grad_act = dot_t(grad, down_w[layer])
-        sig = jax.nn.sigmoid(gate)
-        grad_gate = (grad_act * up * sig * (1.0 + gate * (1.0 - sig))).astype(low)
-        grad_up = (grad_act * gate * sig).astype(low)
-        grad_both = jnp.concatenate([grad_gate, grad_up], axis=1)
-        grad_normed = plane_sum(dot_t(grad_both, ffn_w[layer]))
-
-        mine, other = halves((grad_gate, grad_up))
-        ffn_part = exchange(dot_l(normed, mine), dot_l(normed, other))
-        step = down_rows // 2
-        strips = [
-            jnp.concatenate(
-                [act[:, k * down_rows + c * step :][:, :step] for k in range(TEAM)], axis=1
+        kept_attn, middle, normed, gates, ups, acts = kept[layer]
+        down_part = exchange(*(dot_l(act, grad) for act in acts))
+        down_part = plane_trade(down_part.reshape(TEAM, strip, width), q)
+        sides, partial = [], 0.0
+        for side in (0, 1):
+            gate, up = gates[side], ups[side]
+            grad_act = dot_t(grad, down_w[layer][side])
+            sig = jax.nn.sigmoid(gate)
+            grad_gate = (grad_act * up * sig * (1.0 + gate * (1.0 - sig))).astype(low)
+            grad_up = (grad_act * gate * sig).astype(low)
+            sides.append(jnp.concatenate([grad_gate, grad_up], axis=1))
+            partial = partial + dot_t(sides[side], ffn_w[layer][side])
+        grad_normed = plane_sum(partial)
+        ffn_part = exchange(*(dot_l(normed, part) for part in sides))
+        pair = jnp.concatenate(
+            [ffn_part.reshape(4, -1, 2 * own_hid), fold(down_part, half)], axis=2
+        )
+        grad_normed, pair = lax.optimization_barrier((grad_normed, pair))
+        if layer == 0:
+            grad_normed, pair, layer_out, attn_sums[1] = lax.optimization_barrier(
+                (grad_normed, pair, layer_out, attn_sums[1])
             )
-            for c in (0, 1)
-        ]
-        mine, other = halves(strips)
-        down_part = exchange(dot_l(mine, grad), dot_l(other, grad))
-        grad_normed, ffn_part, down_part = lax.optimization_barrier(
-            (grad_normed, ffn_part, down_part)
-        )
-        down_part = plane_trade(down_part.reshape(TEAM, step, width), q)
+        pair_sums[layer] = sum_z(pair)
         gain_ffn, through = norm_back(grad_normed, middle, gains[layer][1])
         grad_middle = grad.astype(wide) + through
         grad_in, right, gain_attn = attention_back(
             inputs[layer], grad_middle, tabs, attn_w[layer], gains[layer][0], kept_attn
         )
         grad = grad_in.astype(low)
-        grad, down_part = lax.optimization_barrier((grad, down_part))
-        pair = jnp.concatenate(
-            [ffn_part.reshape(4, -1, hid), fold(down_part, half)], axis=2
-        )
-        pair_sums[layer] = sum_z(pair)
         attn_part = exchange(
             attn_half(kept_attn, right, core), attn_half(kept_attn, right, 1 - core)
         )
+        attn_part = after(attn_part, pair_sums[layer])
         attn_sums[layer] = sum_z(attn_part.reshape(4, -1, half))
         gain_grads[layer] = jnp.stack([gain_attn, gain_ffn])
         input_grads[layer] = grad
         if layer == 1:
             layer_out = spread(outputs)
 
+    def to_owner(first, second):
+        own = jnp.where(core == 0, first, second)
+        other = swap(jnp.where(core == 0, second, first))
+        return jnp.where(core == 0, own, other), jnp.where(core == 0, other, own)
+
+    whole_1 = plane_gather(jnp.concatenate([pair_sums[1], attn_sums[1]], axis=1), q)
+    pair_width = pair_sums[1].shape[1]
+    pair_half = to_owner(plane_gather(pair_sums[0], q), whole_1[:, :, :pair_width])
+    attn_half_sums = to_owner(plane_gather(attn_sums[0], q), whole_1[:, :, pair_width:])
     input_grad = spread(input_grads)
-    whole_1 = plane_gather(jnp.concatenate([pair_sums[1], attn_sums[1]], axis=1), q)
-    whole_0 = jnp.concatenate(
-        [plane_gather(pair_sums[0], q), plane_gather(attn_sums[0], q)], axis=2
-    )
-    own = jnp.where(core == 0, whole_0, whole_1)
-    other = swap(jnp.where(core == 0, whole_1, whole_0))
-    by_half = (jnp.where(core == 0, own, other), jnp.where(core == 0, other, own))
 
     gain_all = jnp.stack(gain_grads)
     gain_all = gain_all + swap(gain_all)
@@ -418,14 +451,22 @@
     total = lax.dynamic_index_in_dim(total.reshape(2, 4, -1), z, 1, keepdims=False)
 
     attn_cols = jnp.concatenate(
-        [part[num, :, hid + half :] for num in range(TEAM) for part in by_half], axis=1
+        [part[num] for num in range(TEAM) for part in attn_half_sums], axis=1
     ).astype(wide)
-    gate_cols, up_cols = (
-        jnp.concatenate([part[num, :, :hid] for num in range(TEAM)], axis=1).astype(wide)
-        for part in by_half
-    )
+
+    def hidden_cols(start):
+        return jnp.concatenate(
+            [
+                part[num, :, start : start + own_hid]
+                for num in range(TEAM)
+                for part in pair_half
+            ],
+            axis=1,
+        ).astype(wide)
+
+    gate_cols, up_cols = hidden_cols(0), hidden_cols(own_hid)
     down_sum = jnp.stack(
-        [unfold(part[:, :, hid : hid + half], width) for part in by_half], axis=1
+        [unfold(part[:, :, 2 * own_hid :], width) for part in pair_half]
     ).astype(wide)
     qw, kw = w_query.shape[2], w_key.shape[2]
     return (

time: 648 us -> 629 us (0.971)
  waiting for transfers between devices: 222 us -> 183 us
  local copies, waits for them, and re-layouts: 118 us -> 89.1 us
  Pallas kernels: 0 us -> 23.8 us
  other arithmetic: 66.8 us -> 82.5 us
  blocking collectives: 10.4 us -> 0 us
  starting transfers between devices: 121 us -> 131 us
  matrix products: 81.3 us -> 89.2 us
    ppermute x46 -> x49, waiting for transfers between devices: 115 us -> 69.1 us  [plane_send(): return lax.ppermute(value, ('section', 'replica'), pairs)]
    dynamic_update_slice x43 -> x0, local copies, waits for them, and re-layouts: 34.2 us -> none  [place(): stack = lax.dynamic_update_index_in_dim(stack, block, index, 0)]
    all_gather x1 -> x2, waiting for transfers between devices: 2.56 us -> 30.5 us  [local(): blocks = lax.all_gather(after(ffn_shares[layer], earlier), 'shard')]
    ppermute x9, waiting for transfers between devices: 2.33 us -> 30.1 us  [z_send(): return lax.ppermute(value, ('section', 'shard'), pairs)]
    pallas_call x0 -> x13, Pallas kernels: none -> 23.8 us  [place(): pl.pallas_call(place_kernel, out_shape=shape, in_specs=[pl.BlockSpec(memo...]
    all_to_all x2, waiting for transfers between devices: 36.8 us -> 13.4 us  [whole_sequence(): return lax.all_to_all(blocks, 'shard', 0, 0, tiled=False)]
    ppermute x6, waiting for transfers between devices: 15.9 us -> 0.02 us  [spread(): lax.ppermute(slice_for((z + hop) % 4), ('shard', 'replica'), pairs)]
    ppermute x13 -> x17, starting transfers between devices: 6.05 us -> 20.3 us  [swap(): return lax.ppermute(value, 'section', [(0, 1), (1, 0)])]
  transfers between devices with their start and end apart: 83 -> 91, of which waited for: 36 -> 35; matrix products, arithmetic and copies ran while one was open for 26% -> 36% of each run, Pallas kernels for 0% -> 4%
where the time goes in v3:
time: 629 us; the launch traced here: 617 us
  waiting for transfers between devices  183 us (29%)
  starting transfers between devices  131 us (21%)
  matrix products  89.2 us (14%)
  local copies, waits for them, and re-layouts  89.1 us (14%)
  other arithmetic  82.5 us (13%)
  Pallas kernels  23.8 us (4%)
  between operations  17.6 us (3%)
    ppermute x49, waiting for transfers between devices, plane_send(): return lax.ppermute(value, ('section', 'replica'), pairs)  69.1 us
    ppermute x49, starting transfers between devices, plane_send(): return lax.ppermute(value, ('section', 'replica'), pairs)  62.9 us
    reduce_scatter x4, waiting for transfers between devices, sum_z(): total = lax.psum_scatter(stack, 'shard', scatter_dimension=0, tiled=False)  39.8 us
    all_gather x2, waiting for transfers between devices, local(): blocks = lax.all_gather(after(ffn_shares[layer], earlier), 'shard')  30.5 us
    ppermute x9, waiting for transfers between devices, z_send(): return lax.ppermute(value, ('section', 'shard'), pairs)  30.1 us
    dot_general x18, matrix products, dot(): return jnp.dot(a, b, preferred_element_type=wide)  29 us
    unnamed x281, local copies, waits for them, and re-layouts  24.3 us
    dot_general x18, matrix products, dot_t(): lax.dot_general(a, b, (((1,), (1,)), ((), ())), preferred_element_type=wide)  23.9 us
  transfers between devices with their start and end apart: 91, of which 35 were waited for; matrix products, arithmetic and copies ran while one was open for 36% of the time, Pallas kernels for 4%

profile of v3, /device:TPU:0, one launch (start us, length us, event | category | flops | bytes accessed | tf_op | source)
XLA Modules:
  0.0 616.7 jit_solution(601798424000407503)
XLA Ops:
  10.6 4.0 collective-permute-start.5
  25.6 5.4 all-to-all-start
  32.0 5.7 collective-permute-start.2
  39.7 3.0 collective-permute-start
  42.9 2.8 collective-permute-done.2.refs_3_
  45.7 16.4 %collective-permute-done.1.refs_2_ = bf16[240,640]{1,0:T(8,128)(2,1)S(1)} collective-permute-done((bf16[240,640]{1,0:T(8,128)(2,1)S(1)}, bf16[240,640]{1,0:T(8,128)(2,1)S(1)}, u32[]{:S(2)}, u32[]{:S(2)}) %collective-permute-start.1) | collective-permute-done | bytes 307232 | tf_op jit(solution)/shard_map/ppermute | solution.py:45
  68.5 4.2 collective-permute-start.10
  79.8 8.3 %collective-permute-done.10.refs_3_ = bf16[960,640]{1,0:T(8,128)(2,1)S(1)} collective-permute-done((bf16[960,640]{1,0:T(8,128)(2,1)S(1)}, bf16[960,640]{1,0:T(8,128)(2,1)S(1)}, u32[]{:S(2)}, u32[]{:S(2)}) %collective-permute-start.10) | collective-permute-done | bytes 1228832 | tf_op jit(solution)/shard_map/ppermute | solution.py:52
  88.1 13.2 %collective-permute-done.9.refs_2_ = bf16[960,640]{1,0:T(8,128)(2,1)} collective-permute-done((bf16[960,640]{1,0:T(8,128)(2,1)S(1)}, bf16[960,640]{1,0:T(8,128)(2,1)}, u32[]{:S(2)}, u32[]{:S(2)}) %collective-permute-start.9) | collective-permute-done | bytes 1228832 | tf_op jit(solution)/shard_map/ppermute | solution.py:52
  101.4 4.0 shard_map.205
  105.4 3.7 collective-permute-start.11
  112.8 8.7 %all-gather.5.cloned.1.call-done = bf16[960,960]{1,0:T(8,128)(2,1)} async-done(((bf16[240,960]{1,0:T(8,128)(2,1)}), bf16[960,960]{1,0:T(8,128)(2,1)}) %all-gather.5.cloned.1.call-update) | async-done | bytes 1843216 | tf_op jit(solution)/shard_map/all_gather | solution.py:321
  135.5 3.7 collective-permute-done.14.refs_3_
  139.2 3.5 collective-permute-done.13.refs_2_
  144.3 21.8 %all-gather.7.cloned.1.call-done = bf16[960,960]{1,0:T(8,128)(2,1)} async-done(((bf16[240,960]{1,0:T(8,128)(2,1)}), bf16[960,960]{1,0:T(8,128)(2,1)}) %all-gather.7.cloned.1.call-update) | async-done | bytes 1843216 | tf_op jit(solution)/shard_map/all_gather | solution.py:321
  173.3 2.7 collective-permute-done.33.refs_3_
  176.0 2.8 collective-permute-done.32.refs_2_
  180.4 3.0 broadcast_select_fusion.1
  201.2 4.2 collective-permute-start.35
  205.4 4.0 shard_map.208
  210.8 4.4 fusion.180
  215.2 2.7 convolution_convert_fusion.5
  237.9 3.3 collective-permute-done.17
  244.9 5.2 broadcast_select_fusion
  253.7 2.9 collective-permute-done.30.refs_3_
  256.6 12.4 %collective-permute-start.34 = (bf16[320,960]{1,0:T(8,128)(2,1)}, bf16[320,960]{1,0:T(8,128)(2,1)}, u32[]{:S(2)}, u32[]{:S(2)}) collective-permute-start(bf16[320,960]{1,0:T(8,128)(2,1)} %bitcast.81), channel_id=1, source_target_pairs={{0,16},{16,0},{1,17},{17,1},{2,18},{18,2},{3,19},{19,3},{4,20},{20... | collective-permute-start | bytes 1843208 | tf_op jit(solution)/shard_map/ppermute | solution.py:38
  270.4 3.5 all-to-all-start.1
  276.0 13.4 %all-to-all-done.1 = bf16[4,64,960]{2,1,0:T(8,128)(2,1)S(1)} async-done(((bf16[4,64,960]{2,1,0:T(8,128)(2,1)}), bf16[4,64,960]{2,1,0:T(8,128)(2,1)S(1)}, u32[]{:S(2)}, u32[]{:S(2)}) %all-to-all-start.1) | async-done | bytes 491552 | tf_op jit(solution)/shard_map/all_to_all | solution.py:298
  291.6 2.9 fusion.37
  302.7 4.2 fusion.181
  342.0 3.6 collective-permute-done.55
  371.0 3.4 collective-permute-start.61
  385.0 3.3 fusion.5
  389.0 4.0 fusion.7
  410.3 3.6 collective-permute-done.45
  419.4 4.3 collective-permute-done.46
  424.6 4.8 reduce-scatter.5.cloned.1.call-done
  446.3 7.5 %reduce-scatter.7.cloned.1.call-done = bf16[1,240,320]{2,1,0:T(8,128)(2,1)} async-done(((bf16[4,240,320]{2,1,0:T(8,128)(2,1)}), bf16[1,240,320]{2,1,0:T(8,128)(2,1)}) %reduce-scatter.7.cloned.1.call-update) | async-done | bytes 153616 | tf_op jit(solution)/shard_map/reduce_scatter | solution.py:374
  482.8 27.6 %reduce-scatter.9.cloned.1.call-done = bf16[1,240,960]{2,1,0:T(8,128)(2,1)} async-done(((bf16[4,240,960]{2,1,0:T(8,128)(2,1)}), bf16[1,240,960]{2,1,0:T(8,128)(2,1)}) %reduce-scatter.9.cloned.1.call-update) | async-done | bytes 460816 | tf_op jit(solution)/shard_map/reduce_scatter | solution.py:374
  512.7 3.5 broadcast_select_fusion.11
  518.8 3.4 collective-permute-done.69
  527.2 5.2 collective-permute-done.68
  540.0 2.6 collective-permute-start.74
  543.2 4.5 collective-permute-done.81.refs_3_
  559.6 4.4 collective-permute-start.66
  563.9 2.6 shard_map.215
  585.5 3.1 concatenate.230
  593.5 3.3 slice_bitcast_fusion.20
  (688 shorter events, 324.5 us)
Async XLA Ops:
  20.7 42.3 %collective-permute-start.6 = (bf16[240,960]{0,1:T(8,128)(2,1)}, bf16[240,960]{0,1:T(8,128)(2,1)}, u32[]{:S(2)}, u32[]{:S(2)}) collective-permute-start(bf16[240,960]{0,1:T(8,128)(2,1)} %broadcast_select_fusion.16), channel_id=1, source_target_pairs={{0,16},{16,0},{1,17},{17,1},{2,18},{18,2},{3,19},{19,3},{4,20},{20... | collective-permute-start | bytes 1382408 | tf_op jit(solution)/shard_map/ppermute | solution.py:38
  25.6 42.0 %all-to-all-start = ((bf16[4,80,960]{2,1,0:T(8,128)(2,1)}), bf16[4,80,960]{2,1,0:T(8,128)(2,1)S(1)}, u32[]{:S(2)}, u32[]{:S(2)}) async-start(bf16[4,80,960]{2,1,0:T(8,128)(2,1)} %shard_map.204), calls=%async_computation | async-start | bytes 1310720 | tf_op jit(solution)/shard_map/all_to_all | solution.py:298
  31.0 90.6 %all-gather.5.cloned.1.call-start = ((), (), s32[]{:S(2)}) async-start(), calls=%async_computation.10 | async-start | bytes 2457600 | tf_op jit(solution)/shard_map/all_gather | solution.py:321
  37.7 24.4 %collective-permute-start.1 = (bf16[240,640]{1,0:T(8,128)(2,1)S(1)}, bf16[240,640]{1,0:T(8,128)(2,1)S(1)}, u32[]{:S(2)}, u32[]{:S(2)}) collective-permute-start(bf16[240,640]{1,0:T(8,128)(2,1)S(1)} %constant_dynamic-slice_fusion.8.refs_0_), channel_id=1, source_target_pairs={{0,8},{4,12},{8,0},{12,4},{1,9},{5,13},{9,1},{13,5},{2,10},{6,14},... | collective-permute-start | bytes 921608 | tf_op jit(solution)/shard_map/ppermute | solution.py:45
  39.7 22.5 %collective-permute-start = (bf16[240,640]{1,0:T(8,128)(2,1)S(1)}, bf16[240,640]{1,0:T(8,128)(2,1)S(1)}, u32[]{:S(2)}, u32[]{:S(2)}) collective-permute-start(bf16[240,640]{1,0:T(8,128)(2,1)S(1)} %constant_dynamic-slice_fusion.8.refs_0_), channel_id=1, source_target_pairs={{0,4},{4,8},{8,12},{12,0},{1,5},{5,9},{9,13},{13,1},{2,6},{6,10},{... | collective-permute-start | bytes 921608 | tf_op jit(solution)/shard_map/ppermute | solution.py:45
  68.5 19.6 %collective-permute-start.10 = (bf16[960,640]{1,0:T(8,128)(2,1)S(1)}, bf16[960,640]{1,0:T(8,128)(2,1)S(1)}, u32[]{:S(2)}, u32[]{:S(2)}) collective-permute-start(bf16[960,640]{1,0:T(8,128)(2,1)S(1)} %bitcast.417), channel_id=1, source_target_pairs={{0,3},{1,2},{2,1},{3,0},{4,7},{5,6},{6,5},{7,4},{8,11},{9,10},{10,... | collective-permute-start | bytes 3686408 | tf_op jit(solution)/shard_map/ppermute | solution.py:52
  72.7 28.6 %collective-permute-start.9 = (bf16[960,640]{1,0:T(8,128)(2,1)S(1)}, bf16[960,640]{1,0:T(8,128)(2,1)}, u32[]{:S(2)}, u32[]{:S(2)}) collective-permute-start(bf16[960,640]{1,0:T(8,128)(2,1)S(1)} %bitcast.418), channel_id=1, source_target_pairs={{0,2},{1,3},{2,0},{3,1},{4,6},{5,7},{6,4},{7,5},{8,10},{9,11},{10,... | collective-permute-start | bytes 3686408 | tf_op jit(solution)/shard_map/ppermute | solution.py:52
  75.3 26.1 %collective-permute-start.8 = (bf16[960,640]{1,0:T(8,128)(2,1)S(1)}, bf16[960,640]{1,0:T(8,128)(2,1)}, u32[]{:S(2)}, u32[]{:S(2)}) collective-permute-start(bf16[960,640]{1,0:T(8,128)(2,1)S(1)} %bitcast.419), channel_id=1, source_target_pairs={{0,1},{1,0},{2,3},{3,2},{4,5},{5,4},{6,7},{7,6},{8,9},{9,8},{10,11... | collective-permute-start | bytes 3686408 | tf_op jit(solution)/shard_map/ppermute | solution.py:52
  79.8 86.4 %all-gather.7.cloned.1.call-start = ((), (), s32[]{:S(2)}) async-start(), calls=%async_computation.11 | async-start | bytes 2457600 | tf_op jit(solution)/shard_map/all_gather | solution.py:321
  105.4 75.0 %collective-permute-start.11 = (bf16[4,960,640]{2,1,0:T(8,128)(2,1)}, bf16[4,960,640]{2,1,0:T(8,128)(2,1)}, u32[]{:S(2)}, u32[]{:S(2)}) collective-permute-start(bf16[4,960,640]{2,1,0:T(8,128)(2,1)} %shard_map.205), channel_id=1, source_target_pairs={{0,16},{1,17},{2,18},{3,19},{4,20},{5,21},{6,22},{7,23},{8,24},{9,... | collective-permute-start | bytes 14745608 | tf_op jit(solution)/shard_map/ppermute | solution.py:34
  135.5 90.6 %collective-permute-start.15 = (bf16[960,640]{1,0:T(8,128)(2,1)}, bf16[960,640]{1,0:T(8,128)(2,1)}, u32[]{:S(2)}, u32[]{:S(2)}) collective-permute-start(bf16[960,640]{1,0:T(8,128)(2,1)} %bitcast.48), channel_id=1, source_target_pairs={{0,16},{16,0},{1,17},{17,1},{2,18},{18,2},{3,19},{19,3},{4,20},{20... | collective-permute-start | bytes 3686408 | tf_op jit(solution)/shard_map/ppermute | solution.py:38
  176.0 57.3 %collective-permute-start.16 = (bf16[320,960]{1,0:T(8,128)(2,1)}, bf16[320,960]{1,0:T(8,128)(2,1)}, u32[]{:S(2)}, u32[]{:S(2)}) collective-permute-start(bf16[320,960]{1,0:T(8,128)(2,1)} %bitcast.53), channel_id=1, source_target_pairs={{0,16},{16,0},{1,17},{17,1},{2,18},{18,2},{3,19},{19,3},{4,20},{20... | collective-permute-start | bytes 1843208 | tf_op jit(solution)/shard_map/ppermute | solution.py:38
  185.6 15.6 %collective-permute-start.26 = (bf16[960,640]{1,0:T(8,128)(2,1)S(1)}, bf16[960,640]{1,0:T(8,128)(2,1)S(1)}, u32[]{:S(2)}, u32[]{:S(2)}) collective-permute-start(bf16[960,640]{1,0:T(8,128)(2,1)S(1)} %bitcast.413), channel_id=1, source_target_pairs={{16,19},{17,18},{18,17},{19,16},{20,23},{21,22},{22,21},{23,20},{2... | collective-permute-start | bytes 3686408 | tf_op jit(solution)/shard_map/ppermute | solution.py:52
  186.3 19.1 %collective-permute-start.25 = (bf16[960,640]{1,0:T(8,128)(2,1)S(1)}, bf16[960,640]{1,0:T(8,128)(2,1)}, u32[]{:S(2)}, u32[]{:S(2)}) collective-permute-start(bf16[960,640]{1,0:T(8,128)(2,1)S(1)} %bitcast.414), channel_id=1, source_target_pairs={{16,18},{17,19},{18,16},{19,17},{20,22},{21,23},{22,20},{23,21},{2... | collective-permute-start | bytes 3686408 | tf_op jit(solution)/shard_map/ppermute | solution.py:52
  188.1 17.3 %collective-permute-start.24 = (bf16[960,640]{1,0:T(8,128)(2,1)S(1)}, bf16[960,640]{1,0:T(8,128)(2,1)}, u32[]{:S(2)}, u32[]{:S(2)}) collective-permute-start(bf16[960,640]{1,0:T(8,128)(2,1)S(1)} %bitcast.415), channel_id=1, source_target_pairs={{16,17},{17,16},{18,19},{19,18},{20,21},{21,20},{22,23},{23,22},{2... | collective-permute-start | bytes 3686408 | tf_op jit(solution)/shard_map/ppermute | solution.py:52
  201.2 115.5 %collective-permute-start.35 = (bf16[960,640]{1,0:T(8,128)(2,1)}, bf16[960,640]{1,0:T(8,128)(2,1)}, u32[]{:S(2)}, u32[]{:S(2)}) collective-permute-start(bf16[960,640]{1,0:T(8,128)(2,1)} %bitcast.83), channel_id=1, source_target_pairs={{0,16},{16,0},{1,17},{17,1},{2,18},{18,2},{3,19},{19,3},{4,20},{20... | collective-permute-start | bytes 3686408 | tf_op jit(solution)/shard_map/ppermute | solution.py:38
  209.4 35.5 %collective-permute-start.27 = (bf16[4,960,640]{2,1,0:T(8,128)(2,1)}, bf16[4,960,640]{2,1,0:T(8,128)(2,1)}, u32[]{:S(2)}, u32[]{:S(2)}) collective-permute-start(bf16[4,960,640]{2,1,0:T(8,128)(2,1)} %shard_map.208), channel_id=1, source_target_pairs={{16,0},{17,1},{18,2},{19,3},{20,4},{21,5},{22,6},{23,7},{24,8},{25... | collective-permute-start | bytes 14745608 | tf_op jit(solution)/shard_map/ppermute | solution.py:34
  243.2 31.2 %collective-permute-start.20 = (bf16[128,960]{0,1:T(8,128)(2,1)S(1)}, bf16[128,960]{0,1:T(8,128)(2,1)S(1)}, u32[]{:S(2)}, u32[]{:S(2)}) collective-permute-start(bf16[128,960]{0,1:T(8,128)(2,1)S(1)} %get-tuple-element.282), channel_id=1, source_target_pairs={{0,1},{1,0},{2,3},{3,2},{16,17},{17,16},{18,19},{19,18},{4,5},{5,4... | collective-permute-start | bytes 737288 | tf_op jit(solution)/shard_map/ppermute | solution.py:52
  251.6 17.4 %collective-permute-start.29 = (bf16[64,960]{1,0:T(8,128)(2,1)S(1)}, bf16[64,960]{1,0:T(8,128)(2,1)S(1)}, u32[]{:S(2)}, u32[]{:S(2)}) collective-permute-start(bf16[64,960]{1,0:T(8,128)(2,1)S(1)} %dynamic-slice_bitcast_fusion.23.refs_0_), channel_id=1, source_target_pairs={{0,2},{1,3},{2,0},{3,1},{16,18},{17,19},{18,16},{19,17},{4,6},{5,7... | collective-permute-start | bytes 368648 | tf_op jit(solution)/shard_map/ppermute | solution.py:52
  251.9 17.1 %collective-permute-start.28 = (bf16[64,960]{1,0:T(8,128)(2,1)S(1)}, bf16[64,960]{1,0:T(8,128)(2,1)S(1)}, u32[]{:S(2)}, u32[]{:S(2)}) collective-permute-start(bf16[64,960]{1,0:T(8,128)(2,1)S(1)} %dynamic-slice_bitcast_fusion.23.refs_0_), channel_id=1, source_target_pairs={{0,1},{1,0},{2,3},{3,2},{16,17},{17,16},{18,19},{19,18},{4,5},{5,4... | collective-permute-start | bytes 368648 | tf_op jit(solution)/shard_map/ppermute | solution.py:52
  256.6 61.9 %collective-permute-start.34 = (bf16[320,960]{1,0:T(8,128)(2,1)}, bf16[320,960]{1,0:T(8,128)(2,1)}, u32[]{:S(2)}, u32[]{:S(2)}) collective-permute-start(bf16[320,960]{1,0:T(8,128)(2,1)} %bitcast.81), channel_id=1, source_target_pairs={{0,16},{16,0},{1,17},{17,1},{2,18},{18,2},{3,19},{19,3},{4,20},{20... | collective-permute-start | bytes 1843208 | tf_op jit(solution)/shard_map/ppermute | solution.py:38
  270.4 19.0 %all-to-all-start.1 = ((bf16[4,64,960]{2,1,0:T(8,128)(2,1)}), bf16[4,64,960]{2,1,0:T(8,128)(2,1)S(1)}, u32[]{:S(2)}, u32[]{:S(2)}) async-start(bf16[4,64,960]{2,1,0:T(8,128)(2,1)} %shard_map.209), calls=%async_computation.1 | async-start | bytes 1048576 | tf_op jit(solution)/shard_map/all_to_all | solution.py:298
  273.9 155.5 %reduce-scatter.5.cloned.1.call-start = ((), (), s32[]{:S(2)}) async-start(), calls=%async_computation.6 | async-start | bytes 2457600 | tf_op jit(solution)/shard_map/reduce_scatter | solution.py:374
  333.5 17.4 %collective-permute-start.41 = (bf16[320,960]{1,0:T(8,128)(2,1)S(1)}, bf16[320,960]{1,0:T(8,128)(2,1)S(1)}, u32[]{:S(2)}, u32[]{:S(2)}) collective-permute-start(bf16[320,960]{1,0:T(8,128)(2,1)S(1)} %convolution_convert_fusion.3), channel_id=1, source_target_pairs={{0,16},{16,0},{1,17},{17,1},{2,18},{18,2},{3,19},{19,3},{4,20},{20... | collective-permute-start | bytes 1843208 | tf_op jit(solution)/shard_map/ppermute | solution.py:38
  335.2 41.2 %collective-permute-start.40 = (bf16[960,640]{1,0:T(8,128)(2,1)}, bf16[960,640]{1,0:T(8,128)(2,1)}, u32[]{:S(2)}, u32[]{:S(2)}) collective-permute-start(bf16[960,640]{1,0:T(8,128)(2,1)} %convolution_convert_fusion.1), channel_id=1, source_target_pairs={{0,16},{16,0},{1,17},{17,1},{2,18},{18,2},{3,19},{19,3},{4,20},{20... | collective-permute-start | bytes 3686408 | tf_op jit(solution)/shard_map/ppermute | solution.py:38
  349.3 14.9 %collective-permute-start.58 = (bf16[256,960]{0,1:T(8,128)(2,1)}, bf16[256,960]{0,1:T(8,128)(2,1)}, u32[]{:S(2)}, u32[]{:S(2)}) collective-permute-start(bf16[256,960]{0,1:T(8,128)(2,1)} %broadcast_select_fusion.12), channel_id=1, source_target_pairs={{0,16},{16,0},{1,17},{17,1},{2,18},{18,2},{3,19},{19,3},{4,20},{20... | collective-permute-start | bytes 1474568 | tf_op jit(solution)/shard_map/ppermute | solution.py:38
  369.0 46.3 %collective-permute-start.59 = (bf16[2,64,960]{2,1,0:T(8,128)(2,1)}, bf16[2,64,960]{2,1,0:T(8,128)(2,1)}, u32[]{:S(2)}, u32[]{:S(2)}) collective-permute-start(bf16[2,64,960]{2,1,0:T(8,128)(2,1)} %get-tuple-element.208), channel_id=1, source_target_pairs={{0,4},{5,9},{10,14},{15,3},{16,20},{21,25},{26,30},{31,19}} | collective-permute-start | bytes 737288 | tf_op jit(solution)/shard_map/ppermute | solution.py:367
  371.0 44.4 %collective-permute-start.61 = (bf16[2,64,960]{2,1,0:T(8,128)(2,1)}, bf16[2,64,960]{2,1,0:T(8,128)(2,1)}, u32[]{:S(2)}, u32[]{:S(2)}) collective-permute-start(bf16[2,64,960]{2,1,0:T(8,128)(2,1)} %get-tuple-element.209), channel_id=1, source_target_pairs={{0,12},{5,1},{10,6},{15,11},{16,28},{21,17},{26,22},{31,27}} | collective-permute-start | bytes 737288 | tf_op jit(solution)/shard_map/ppermute | solution.py:367
  374.4 41.3 %collective-permute-start.60 = (bf16[2,64,960]{2,1,0:T(8,128)(2,1)}, bf16[2,64,960]{2,1,0:T(8,128)(2,1)}, u32[]{:S(2)}, u32[]{:S(2)}) collective-permute-start(bf16[2,64,960]{2,1,0:T(8,128)(2,1)} %get-tuple-element.210), channel_id=1, source_target_pairs={{0,8},{5,13},{10,2},{15,7},{16,24},{21,29},{26,18},{31,23}} | collective-permute-start | bytes 737288 | tf_op jit(solution)/shard_map/ppermute | solution.py:367
  388.3 65.5 %reduce-scatter.7.cloned.1.call-start = ((), (), s32[]{:S(2)}) async-start(), calls=%async_computation.7 | async-start | bytes 921600 | tf_op jit(solution)/shard_map/reduce_scatter | solution.py:374
  415.3 27.5 %collective-permute-start.49 = (bf16[960,640]{1,0:T(8,128)(2,1)}, bf16[960,640]{1,0:T(8,128)(2,1)}, u32[]{:S(2)}, u32[]{:S(2)}) collective-permute-start(bf16[960,640]{1,0:T(8,128)(2,1)} %convolution_convert_fusion), channel_id=1, source_target_pairs={{0,16},{16,0},{1,17},{17,1},{2,18},{18,2},{3,19},{19,3},{4,20},{20... | collective-permute-start | bytes 3686408 | tf_op jit(solution)/shard_map/ppermute | solution.py:38
  417.6 16.8 %collective-permute-start.48 = (bf16[128,960]{0,1:T(8,128)(2,1)}, bf16[128,960]{0,1:T(8,128)(2,1)}, u32[]{:S(2)}, u32[]{:S(2)}) collective-permute-start(bf16[128,960]{0,1:T(8,128)(2,1)} %get-tuple-element.274), channel_id=1, source_target_pairs={{0,1},{1,0},{2,3},{3,2},{16,17},{17,16},{18,19},{19,18},{4,5},{5,4... | collective-permute-start | bytes 737288 | tf_op jit(solution)/shard_map/ppermute | solution.py:52
  430.6 79.9 %reduce-scatter.9.cloned.1.call-start = ((), (), s32[]{:S(2)}) async-start(), calls=%async_computation.8 | async-start | bytes 2457600 | tf_op jit(solution)/shard_map/reduce_scatter | solution.py:374
  454.8 82.8 %collective-permute-start.77 = (bf16[240,1280]{1,0:T(8,128)(2,1)S(1)}, bf16[240,1280]{1,0:T(8,128)(2,1)S(1)}, u32[]{:S(2)}, u32[]{:S(2)}) collective-permute-start(bf16[240,1280]{1,0:T(8,128)(2,1)S(1)} %pad_maximum_fusion.11.refs_0_), channel_id=1, source_target_pairs={{0,3},{1,2},{2,1},{3,0},{16,19},{17,18},{18,17},{19,16},{4,7},{5,6... | collective-permute-start | bytes 1843208 | tf_op jit(solution)/shard_map/ppermute | solution.py:52
  457.2 82.9 %collective-permute-start.76 = (bf16[240,1280]{1,0:T(8,128)(2,1)S(1)}, bf16[240,1280]{1,0:T(8,128)(2,1)S(1)}, u32[]{:S(2)}, u32[]{:S(2)}) collective-permute-start(bf16[240,1280]{1,0:T(8,128)(2,1)S(1)} %pad_maximum_fusion.11.refs_0_), channel_id=1, source_target_pairs={{0,2},{1,3},{2,0},{3,1},{16,18},{17,19},{18,16},{19,17},{4,6},{5,7... | collective-permute-start | bytes 1843208 | tf_op jit(solution)/shard_map/ppermute | solution.py:52
  457.7 84.9 %collective-permute-start.75 = (bf16[240,1280]{1,0:T(8,128)(2,1)S(1)}, bf16[240,1280]{1,0:T(8,128)(2,1)S(1)}, u32[]{:S(2)}, u32[]{:S(2)}) collective-permute-start(bf16[240,1280]{1,0:T(8,128)(2,1)S(1)} %pad_maximum_fusion.11.refs_0_), channel_id=1, source_target_pairs={{0,1},{1,0},{2,3},{3,2},{16,17},{17,16},{18,19},{19,18},{4,5},{5,4... | collective-permute-start | bytes 1843208 | tf_op jit(solution)/shard_map/ppermute | solution.py:52
  469.7 70.3 %reduce-scatter.11.cloned.1.call-start = ((), (), s32[]{:S(2)}) async-start(), calls=%async_computation.9 | async-start | bytes 921600 | tf_op jit(solution)/shard_map/reduce_scatter | solution.py:374
  480.7 36.3 %collective-permute-start.67 = (f32[2,2,960]{2,1,0:T(2,128)S(1)}, f32[2,2,960]{2,1,0:T(2,128)S(1)}, u32[]{:S(2)}, u32[]{:S(2)}) collective-permute-start(f32[2,2,960]{2,1,0:T(2,128)S(1)} %pad_maximum_fusion.34), channel_id=1, source_target_pairs={{0,16},{16,0},{1,17},{17,1},{2,18},{18,2},{3,19},{19,3},{4,20},{20... | collective-permute-start | bytes 46088 | tf_op jit(solution)/shard_map/ppermute | solution.py:38
  517.0 20.0 %collective-permute-start.63 = (bf16[256,960]{0,1:T(8,128)(2,1)}, bf16[256,960]{0,1:T(8,128)(2,1)}, u32[]{:S(2)}, u32[]{:S(2)}) collective-permute-start(bf16[256,960]{0,1:T(8,128)(2,1)} %broadcast_select_fusion.10), channel_id=1, source_target_pairs={{0,16},{16,0},{1,17},{17,1},{2,18},{18,2},{3,19},{19,3},{4,20},{20... | collective-permute-start | bytes 1474568 | tf_op jit(solution)/shard_map/ppermute | solution.py:38
  532.4 15.3 %collective-permute-start.81 = (bf16[240,960]{1,0:T(8,128)(2,1)}, bf16[240,960]{1,0:T(8,128)(2,1)S(1)}, u32[]{:S(2)}, u32[]{:S(2)}) collective-permute-start(bf16[240,960]{1,0:T(8,128)(2,1)} %bitcast.161.refs_0_), channel_id=1, source_target_pairs={{0,3},{1,2},{2,1},{3,0},{16,19},{17,18},{18,17},{19,16},{4,7},{5,6... | collective-permute-start | bytes 1382408 | tf_op jit(solution)/shard_map/ppermute | solution.py:52
  537.1 20.5 %collective-permute-start.80 = (bf16[240,960]{1,0:T(8,128)(2,1)}, bf16[240,960]{1,0:T(8,128)(2,1)}, u32[]{:S(2)}, u32[]{:S(2)}) collective-permute-start(bf16[240,960]{1,0:T(8,128)(2,1)} %bitcast.161.refs_0_), channel_id=1, source_target_pairs={{0,2},{1,3},{2,0},{3,1},{16,18},{17,19},{18,16},{19,17},{4,6},{5,7... | collective-permute-start | bytes 1382408 | tf_op jit(solution)/shard_map/ppermute | solution.py:52
  537.6 21.9 %collective-permute-start.79 = (bf16[240,960]{1,0:T(8,128)(2,1)}, bf16[240,960]{1,0:T(8,128)(2,1)}, u32[]{:S(2)}, u32[]{:S(2)}) collective-permute-start(bf16[240,960]{1,0:T(8,128)(2,1)} %bitcast.161.refs_0_), channel_id=1, source_target_pairs={{0,1},{1,0},{2,3},{3,2},{16,17},{17,16},{18,19},{19,18},{4,5},{5,4... | collective-permute-start | bytes 1382408 | tf_op jit(solution)/shard_map/ppermute | solution.py:52
  540.0 27.8 %collective-permute-start.74 = (bf16[240,320]{1,0:T(8,128)(2,1)}, bf16[240,320]{1,0:T(8,128)(2,1)S(1)}, u32[]{:S(2)}, u32[]{:S(2)}) collective-permute-start(bf16[240,320]{1,0:T(8,128)(2,1)} %bitcast.421), channel_id=1, source_target_pairs={{0,3},{1,2},{2,1},{3,0},{16,19},{17,18},{18,17},{19,16},{4,7},{5,6... | collective-permute-start | bytes 460808 | tf_op jit(solution)/shard_map/ppermute | solution.py:52
  542.7 27.2 %collective-permute-start.73 = (bf16[240,320]{1,0:T(8,128)(2,1)}, bf16[240,320]{1,0:T(8,128)(2,1)S(1)}, u32[]{:S(2)}, u32[]{:S(2)}) collective-permute-start(bf16[240,320]{1,0:T(8,128)(2,1)} %bitcast.422), channel_id=1, source_target_pairs={{0,2},{1,3},{2,0},{3,1},{16,18},{17,19},{18,16},{19,17},{4,6},{5,7... | collective-permute-start | bytes 460808 | tf_op jit(solution)/shard_map/ppermute | solution.py:52
  547.8 22.1 %collective-permute-start.72 = (bf16[240,320]{1,0:T(8,128)(2,1)}, bf16[240,320]{1,0:T(8,128)(2,1)S(1)}, u32[]{:S(2)}, u32[]{:S(2)}) collective-permute-start(bf16[240,320]{1,0:T(8,128)(2,1)} %bitcast.423), channel_id=1, source_target_pairs={{0,1},{1,0},{2,3},{3,2},{16,17},{17,16},{18,19},{19,18},{4,5},{5,4... | collective-permute-start | bytes 460808 | tf_op jit(solution)/shard_map/ppermute | solution.py:52
  557.6 21.4 %collective-permute-start.64 = (bf16[2,64,960]{2,1,0:T(8,128)(2,1)}, bf16[2,64,960]{2,1,0:T(8,128)(2,1)}, u32[]{:S(2)}, u32[]{:S(2)}) collective-permute-start(bf16[2,64,960]{2,1,0:T(8,128)(2,1)} %get-tuple-element.205), channel_id=1, source_target_pairs={{0,4},{5,9},{10,14},{15,3},{16,20},{21,25},{26,30},{31,19}} | collective-permute-start | bytes 737288 | tf_op jit(solution)/shard_map/ppermute | solution.py:367
  559.6 19.4 %collective-permute-start.66 = (bf16[2,64,960]{2,1,0:T(8,128)(2,1)}, bf16[2,64,960]{2,1,0:T(8,128)(2,1)}, u32[]{:S(2)}, u32[]{:S(2)}) collective-permute-start(bf16[2,64,960]{2,1,0:T(8,128)(2,1)} %get-tuple-element.206), channel_id=1, source_target_pairs={{0,12},{5,1},{10,6},{15,11},{16,28},{21,17},{26,22},{31,27}} | collective-permute-start | bytes 737288 | tf_op jit(solution)/shard_map/ppermute | solution.py:367
  576.3 20.5 %collective-permute-start.82 = (bf16[4,240,960]{2,1,0:T(8,128)(2,1)}, bf16[4,240,960]{2,1,0:T(8,128)(2,1)}, u32[]{:S(2)}, u32[]{:S(2)}) collective-permute-start(bf16[4,240,960]{2,1,0:T(8,128)(2,1)} %broadcast_select_fusion.4), channel_id=1, source_target_pairs={{0,16},{16,0},{1,17},{17,1},{2,18},{18,2},{3,19},{19,3},{4,20},{20... | collective-permute-start | bytes 5529608 | tf_op jit(solution)/shard_map/ppermute | solution.py:38
  (178 other events, 1195.8 us)
Sparse Core Ops, SparseCore 0:
  79.9 41.6 all-gather.4
  123.7 42.3 all-gather.6
  388.4 40.9 reduce-scatter.4
  431.5 22.1 reduce-scatter.6
  469.9 40.5 reduce-scatter.8
  513.1 22.4 reduce-scatter.10

commit v4 on v3

--- a/solution.py
+++ b/solution.py
@@ -302,34 +302,42 @@
     marks = marks.at[0, :group].set(own_segments.astype(low))
     marks = marks.at[1, : norm_attn.shape[1]].set(norm_attn[0])
     marks = marks.at[2, : norm_ffn.shape[1]].set(norm_ffn[0])
-    entry = whole_sequence(jnp.concatenate([pick(hidden_in[:, 0], core), marks]))
+    entry = whole_sequence(
+        jnp.concatenate([pick(hidden_in[:, 0], core), pick(out_grad[:, 0], core), marks])
+    )
     attn_rows = z_gather(attn_share, z, 0).reshape(-1, chunk)
-    attn_rows, entry, ffn_shares = lax.optimization_barrier((attn_rows, entry, ffn_shares))
+    attn_rows, entry = lax.optimization_barrier((attn_rows, entry))
     turn = to_core(attn_rows[:16, :128], 1)
     hidden = entry[:, :group].reshape(-1, width)
-    segments = entry[:, group, :group].reshape(-1).astype(jnp.int32)
+    top_grad = entry[:, group : 2 * group].reshape(-1, width)
+    entry_marks = entry[:, 2 * group :]
+    segments = entry_marks[:, 0, :group].reshape(-1).astype(jnp.int32)
     tabs = tables(segments)
-    own_gains = entry[:, group + 1 : group + 3, : norm_attn.shape[1]]
+    own_gains = entry_marks[:, 1:3, : norm_attn.shape[1]]
     gains = both_layers(own_gains.transpose(1, 0, 2).reshape(2, -1))
     gains = [gain.astype(wide) for gain in gains]
 
     attn_w, ffn_w, down_w = [None] * 2, [None] * 2, [None] * 2
-    attn_w[0] = give(plane_gather(attn_rows, q, 0), 0)
     rows = z_gather(after(attn_share, turn), z, 1).reshape(-1, chunk)
-    earlier = entry
-    for layer in range(layers):
-        blocks = lax.all_gather(after(ffn_shares[layer], earlier), "shard")
-        own = blocks[:, :, : 2 * own_hid].reshape(-1, 2 * own_hid)
-        ffn_w[layer] = (own, swap(own))
-        own = unfold(plane_trade(blocks[:, :, 2 * own_hid :], q), width).reshape(-1, width)
-        down_w[layer] = (own, swap(own))
-        earlier = blocks
+    blocks = [lax.all_gather(after(ffn_shares[0], entry), "shard"), None]
+    attn_stack, blocks[0] = lax.optimization_barrier((plane_gather(attn_rows, q, 0), blocks[0]))
+    blocks[1] = lax.all_gather(after(ffn_shares[1], blocks[0]), "shard")
+    attn_w[0] = give(attn_stack, 0)
+
+    def unpack(stack):
+        own = stack[:, :, : 2 * own_hid].reshape(-1, 2 * own_hid)
+        down = unfold(plane_trade(stack[:, :, 2 * own_hid :], q), width).reshape(-1, width)
+        return (own, swap(own)), (down, swap(down))
+
+    ffn_w[0], down_w[0] = unpack(blocks[0])
     attn_w[1] = give(plane_gather(after(rows, attn_w[0]), q, 1), 1)
-    top_grad = whole_sequence(pick(after(out_grad, attn_w[1])[:, 0], core)).reshape(-1, width)
 
     inputs, kept, outputs = [hidden], [], []
     for layer in range(layers):
         middle, kept_attn = attention_fwd(inputs[layer], tabs, attn_w[layer], gains[layer][0])
+        if layer == 0:
+            middle, second = lax.optimization_barrier((middle, blocks[1]))
+            ffn_w[1], down_w[1] = unpack(second)
         normed = (middle * row_scale(middle) * gains[layer][1]).astype(low)
         gates, ups, acts, partial = [], [], [], 0.0
         for weights, down in zip(ffn_w[layer], down_w[layer]):
@@ -341,11 +349,10 @@
             ups.append(up)
             acts.append(act)
         kept.append((kept_attn, middle, normed, gates, ups, acts))
-        result = (middle + plane_sum(partial)).astype(low)
-        if layer == 0:
-            result, top_grad = lax.optimization_barrier((result, top_grad))
-        outputs.append(result)
-        inputs.append(result)
+        if layer < layers - 1:
+            result = (middle + plane_sum(partial)).astype(low)
+            outputs.append(result)
+            inputs.append(result)
 
     def spread(by_layer):
         mine = jnp.where(core == 0, by_layer[0], by_layer[1])
@@ -376,6 +383,10 @@
 
     split = w_query.shape[2] + w_key.shape[2] * 2
 
+    def gather_halves(own, owner):
+        other = to_core(own, owner)
+        return jnp.concatenate([own, other] if owner == 0 else [other, own], axis=1)
+
     def attn_half(kept_attn, right, which):
         start = q * chunk + which * half
         part = lax.dynamic_slice_in_dim(right, start, half, axis=1)
@@ -391,7 +402,7 @@
         kept_attn, middle, normed, gates, ups, acts = kept[layer]
         down_part = exchange(*(dot_l(act, grad) for act in acts))
         down_part = plane_trade(down_part.reshape(TEAM, strip, width), q)
-        sides, partial = [], 0.0
+        sides, grad_partial = [], 0.0
         for side in (0, 1):
             gate, up = gates[side], ups[side]
             grad_act = dot_t(grad, down_w[layer][side])
@@ -399,8 +410,8 @@
             grad_gate = (grad_act * up * sig * (1.0 + gate * (1.0 - sig))).astype(low)
             grad_up = (grad_act * gate * sig).astype(low)
             sides.append(jnp.concatenate([grad_gate, grad_up], axis=1))
-            partial = partial + dot_t(sides[side], ffn_w[layer][side])
-        grad_normed = plane_sum(partial)
+            grad_partial = grad_partial + dot_t(sides[side], ffn_w[layer][side])
+        grad_normed = plane_sum(grad_partial)
         ffn_part = exchange(*(dot_l(normed, part) for part in sides))
         pair = jnp.concatenate(
             [ffn_part.reshape(4, -1, 2 * own_hid), fold(down_part, half)], axis=2
@@ -417,38 +428,59 @@
             inputs[layer], grad_middle, tabs, attn_w[layer], gains[layer][0], kept_attn
         )
         grad = grad_in.astype(low)
+        gain_grads[layer] = jnp.stack([gain_attn, gain_ffn])
+        input_grads[layer] = grad
         attn_part = exchange(
             attn_half(kept_attn, right, core), attn_half(kept_attn, right, 1 - core)
-        )
+        ).reshape(4, -1, half)
+        if layer == 1:
+            result = (middle + plane_sum(after(partial, grad_normed))).astype(low)
+            grad, result = lax.optimization_barrier((grad, result))
+            outputs.append(result)
+            layer_out = spread(outputs)
+        else:
+            gain_part = exchange(
+                jnp.where(core == 0, gain_grads[0], gain_grads[1]),
+                jnp.where(core == 0, gain_grads[1], gain_grads[0]),
+            )
+            gain_part = gain_part.reshape(2, 4, -1).transpose(1, 0, 2)
+            gain_width = gain_part.shape[2]
+            gain_part = jnp.pad(gain_part, ((0, 0), (0, 14), (0, half - gain_width)))
+            attn_part = jnp.concatenate([attn_part, gain_part], axis=1)
+            input_grad = spread(input_grads)
+        if layer == 0:
+            pair_sums[0], input_grad, whole_1 = lax.optimization_barrier(
+                (pair_sums[0], input_grad, whole_1)
+            )
         attn_part = after(attn_part, pair_sums[layer])
-        attn_sums[layer] = sum_z(attn_part.reshape(4, -1, half))
-        gain_grads[layer] = jnp.stack([gain_attn, gain_ffn])
-        input_grads[layer] = grad
+        attn_sums[layer] = sum_z(attn_part)
         if layer == 1:
-            layer_out = spread(outputs)
-
-    def to_owner(first, second):
-        own = jnp.where(core == 0, first, second)
-        other = swap(jnp.where(core == 0, second, first))
-        return jnp.where(core == 0, own, other), jnp.where(core == 0, other, own)
-
-    whole_1 = plane_gather(jnp.concatenate([pair_sums[1], attn_sums[1]], axis=1), q)
-    pair_width = pair_sums[1].shape[1]
-    pair_half = to_owner(plane_gather(pair_sums[0], q), whole_1[:, :, :pair_width])
-    attn_half_sums = to_owner(plane_gather(attn_sums[0], q), whole_1[:, :, pair_width:])
-    input_grad = spread(input_grads)
-
-    gain_all = jnp.stack(gain_grads)
-    gain_all = gain_all + swap(gain_all)
-    total = gain_all
-    for hop in (1, 2, 3):
-        total = total + z_send(gain_all, hop)
-    flip = TEAM
-    while flip < lax.axis_size("replica"):
-        total = total + plane_send(total, flip)
-        flip *= 2
-    total = jnp.where(core == 0, total[0], total[1])
-    total = lax.dynamic_index_in_dim(total.reshape(2, 4, -1), z, 1, keepdims=False)
+            pair_width = pair_sums[1].shape[1]
+            whole_1 = plane_gather(
+                gather_halves(jnp.concatenate([pair_sums[1], attn_sums[1]], axis=1), 1), q, 1
+            )
+
+    gain_rows = attn_sums[0].shape[0] - 16
+    total = attn_sums[0][gain_rows : gain_rows + 2, :gain_width].astype(wide)
+    pair_0 = plane_gather(gather_halves(pair_sums[0], 0), q, 0)
+    attn_0 = plane_gather(gather_halves(attn_sums[0][:gain_rows], 0), q, 0)
+    whole_width = pair_width + half
+    pair_half = [
+        jnp.where(
+            core == 0,
+            pair_0[:, :, c * pair_width :][:, :, :pair_width],
+            whole_1[:, :, c * whole_width :][:, :, :pair_width],
+        )
+        for c in (0, 1)
+    ]
+    attn_half_sums = [
+        jnp.where(
+            core == 0,
+            attn_0[:, :, c * half :][:, :, :half],
+            whole_1[:, :, c * whole_width + pair_width :][:, :, :half],
+        )
+        for c in (0, 1)
+    ]
 
     attn_cols = jnp.concatenate(
         [part[num] for num in range(TEAM) for part in attn_half_sums], axis=1

time: 629 us -> 591 us (0.940)
  the two profiles are of different devices: /device:TPU:0 before, /device:TPU:10 now
where the time goes in v4:
time: 591 us; the launch traced here: 579 us
  waiting for transfers between devices  151 us (26%)
  starting transfers between devices  143 us (24%)
  matrix products  101 us (17%)
  local copies, waits for them, and re-layouts  74.1 us (13%)
  other arithmetic  71.1 us (12%)
  Pallas kernels  21.7 us (4%)
  between operations  17 us (3%)
    ppermute x46, waiting for transfers between devices, plane_send(): return lax.ppermute(value, ('section', 'replica'), pairs)  95.7 us
    ppermute x46, starting transfers between devices, plane_send(): return lax.ppermute(value, ('section', 'replica'), pairs)  75.1 us
    dot_general x18, matrix products, dot(): return jnp.dot(a, b, preferred_element_type=wide)  29 us
    dot_general x18, matrix products, dot_t(): lax.dot_general(a, b, (((1,), (1,)), ((), ())), preferred_element_type=wide)  27 us
    dot_general x16, matrix products, dot_l(): lax.dot_general(a, b, (((0,), (0,)), ((), ())), preferred_element_type=wide)  23.4 us
    pallas_call x12, Pallas kernels, place(): pl.pallas_call(place_kernel, out_shape=shape, in_specs=[pl.BlockSpec(memo...  21.7 us
    ppermute x15, starting transfers between devices, swap(): return lax.ppermute(value, 'section', [(0, 1), (1, 0)])  21.4 us
    ppermute x6, waiting for transfers between devices, z_send(): return lax.ppermute(value, ('section', 'shard'), pairs)  20.5 us
  transfers between devices with their start and end apart: 85, of which 36 were waited for; matrix products, arithmetic and copies ran while one was open for 34% of the time, Pallas kernels for 3%

profile of v4, /device:TPU:10, one launch (start us, length us, event | category | flops | bytes accessed | tf_op | source)
XLA Modules:
  0.0 579.1 jit_solution(1889906965278079980)
XLA Ops:
  14.3 7.3 %collective-permute-done.5.refs_3_ = bf16[144,960]{1,0:T(8,128)(2,1)S(1)} collective-permute-done((bf16[144,960]{1,0:T(8,128)(2,1)S(1)}, bf16[144,960]{1,0:T(8,128)(2,1)S(1)}, u32[]{:S(2)}, u32[]{:S(2)}) %collective-permute-start.5) | collective-permute-done | bytes 276512 | tf_op jit(solution)/shard_map/ppermute | solution.py:52
  21.6 5.1 collective-permute-done.4.refs_2_
  28.4 5.3 all-to-all-start
  42.4 4.8 collective-permute-start.1
  47.2 4.3 collective-permute-start
  51.6 19.1 %collective-permute-done.2.refs_3_ = bf16[240,640]{1,0:T(8,128)(2,1)S(1)} collective-permute-done((bf16[240,640]{1,0:T(8,128)(2,1)S(1)}, bf16[240,640]{1,0:T(8,128)(2,1)S(1)}, u32[]{:S(2)}, u32[]{:S(2)}) %collective-permute-start.2) | collective-permute-done | bytes 307232 | tf_op jit(solution)/shard_map/ppermute | solution.py:45
  75.4 3.4 collective-permute-start.9
  81.3 3.4 collective-permute-start.7
  84.7 10.4 %collective-permute-done.9.refs_3_ = bf16[960,640]{1,0:T(8,128)(2,1)S(1)} collective-permute-done((bf16[960,640]{1,0:T(8,128)(2,1)S(1)}, bf16[960,640]{1,0:T(8,128)(2,1)S(1)}, u32[]{:S(2)}, u32[]{:S(2)}) %collective-permute-start.9) | collective-permute-done | bytes 1228832 | tf_op jit(solution)/shard_map/ppermute | solution.py:52
  95.1 13.1 %collective-permute-done.8.refs_2_ = bf16[960,640]{1,0:T(8,128)(2,1)S(1)} collective-permute-done((bf16[960,640]{1,0:T(8,128)(2,1)S(1)}, bf16[960,640]{1,0:T(8,128)(2,1)S(1)}, u32[]{:S(2)}, u32[]{:S(2)}) %collective-permute-start.8) | collective-permute-done | bytes 1228832 | tf_op jit(solution)/shard_map/ppermute | solution.py:52
  112.1 5.8 all-gather.5.cloned.1.call-done
  117.9 3.7 collective-permute-start.11
  128.5 13.1 %collective-permute-start.6 = (bf16[2,960]{1,0:T(2,128)(2,1)S(1)}, bf16[2,960]{1,0:T(2,128)(2,1)S(1)}, u32[]{:S(2)}, u32[]{:S(2)}) collective-permute-start(bf16[2,960]{1,0:T(2,128)(2,1)S(1)} %reshape.680), channel_id=1, source_target_pairs={{0,16},{16,0},{1,17},{17,1},{2,18},{18,2},{3,19},{19,3},{4,20},{20... | collective-permute-start | bytes 11528 | tf_op jit(solution)/shard_map/ppermute | solution.py:38
  159.1 3.0 collective-permute-done.13.refs_2_
  164.8 3.2 broadcast_select_fusion.1
  186.2 4.4 fusion.180
  190.6 2.6 convolution_convert_fusion.5
  195.4 4.0 shard_map.208
  218.4 5.9 %collective-permute-done.29.refs_2_ = bf16[240,320]{1,0:T(8,128)(2,1)S(1)} collective-permute-done((bf16[240,320]{1,0:T(8,128)(2,1)S(1)}, bf16[240,320]{1,0:T(8,128)(2,1)S(1)}, u32[]{:S(2)}, u32[]{:S(2)}) %collective-permute-start.29) | collective-permute-done | bytes 153632 | tf_op jit(solution)/shard_map/ppermute | solution.py:52
  224.3 6.6 %collective-permute-start.32 = (bf16[960,640]{1,0:T(8,128)(2,1)}, bf16[960,640]{1,0:T(8,128)(2,1)}, u32[]{:S(2)}, u32[]{:S(2)}) collective-permute-start(bf16[960,640]{1,0:T(8,128)(2,1)} %bitcast.80), channel_id=1, source_target_pairs={{0,16},{16,0},{1,17},{17,1},{2,18},{18,2},{3,19},{19,3},{4,20},{20... | collective-permute-start | bytes 3686408 | tf_op jit(solution)/shard_map/ppermute | solution.py:38
  236.2 4.8 collective-permute-done.18
  241.1 2.7 collective-permute-done.20
  244.1 2.9 broadcast_select_fusion
  260.3 4.3 fusion.181
  264.6 2.6 convolution_convert_fusion.4
  287.0 3.3 collective-permute-done.33
  303.9 2.5 collective-permute-done.41.refs_3_
  314.8 4.2 collective-permute-done.42
  329.4 2.6 collective-permute-done.45
  364.8 2.7 convolution_convert_fusion
  372.2 5.1 collective-permute-done.47
  378.3 6.6 %collective-permute-done.49 = bf16[128,960]{0,1:T(8,128)(2,1)S(1)} collective-permute-done((bf16[128,960]{0,1:T(8,128)(2,1)S(1)}, bf16[128,960]{0,1:T(8,128)(2,1)S(1)}, u32[]{:S(2)}, u32[]{:S(2)}) %collective-permute-start.49) | collective-permute-done | bytes 245792 | tf_op jit(solution)/shard_map/ppermute | solution.py:52
  390.8 4.7 collective-permute-start.56
  406.1 3.4 collective-permute-start.52
  419.2 5.7 reduce-scatter.7.cloned.1.call-done
  462.3 4.3 collective-permute-start.61
  471.2 12.4 %collective-permute-done.61 = bf16[2,64,960]{2,1,0:T(8,128)(2,1)} collective-permute-done((bf16[2,64,960]{2,1,0:T(8,128)(2,1)}, bf16[2,64,960]{2,1,0:T(8,128)(2,1)}, u32[]{:S(2)}, u32[]{:S(2)}) %collective-permute-start.61) | collective-permute-done | bytes 245792 | tf_op jit(solution)/shard_map/ppermute | solution.py:374
  485.5 2.8 add_convert_fusion.2
  493.7 2.9 shard_map.212
  500.2 2.7 collective-permute-done.74
  506.1 8.7 %collective-permute-start.76 = (bf16[240,1920]{1,0:T(8,128)(2,1)S(1)}, bf16[240,1920]{1,0:T(8,128)(2,1)S(1)}, u32[]{:S(2)}, u32[]{:S(2)}) collective-permute-start(bf16[240,1920]{1,0:T(8,128)(2,1)S(1)} %pad_maximum_fusion.9.refs_0_), channel_id=1, source_target_pairs={{0,2},{1,3},{2,0},{3,1},{4,6},{5,7},{6,4},{7,5},{8,10},{9,11},{10,... | collective-permute-start | bytes 2764808 | tf_op jit(solution)/shard_map/ppermute | solution.py:52
  514.8 3.4 collective-permute-start.75
  518.1 7.3 %reduce-scatter.11.cloned.1.call-done = bf16[1,256,320]{2,1,0:T(8,128)(2,1)} async-done(((bf16[4,256,320]{2,1,0:T(8,128)(2,1)}), bf16[1,256,320]{2,1,0:T(8,128)(2,1)}) %reduce-scatter.11.cloned.1.call-update) | async-done | bytes 163856 | tf_op jit(solution)/shard_map/reduce_scatter | solution.py:381
  529.0 5.6 collective-permute-done.76.refs_2_
  543.2 3.2 collective-permute-start.72
  546.4 4.2 collective-permute-start.71
  551.9 2.8 copy.440
  556.0 2.5 concatenate.237
  (611 shorter events, 313.0 us)
Async XLA Ops:
  12.2 14.5 %collective-permute-start.4 = (bf16[144,960]{1,0:T(8,128)(2,1)S(1)}, bf16[144,960]{1,0:T(8,128)(2,1)S(1)}, u32[]{:S(2)}, u32[]{:S(2)}) collective-permute-start(bf16[144,960]{1,0:T(8,128)(2,1)S(1)} %pad_maximum_fusion.22.refs_0_), channel_id=1, source_target_pairs={{0,2},{1,3},{2,0},{3,1},{16,18},{17,19},{18,16},{19,17},{4,6},{5,7... | collective-permute-start | bytes 829448 | tf_op jit(solution)/shard_map/ppermute | solution.py:52
  28.4 46.0 %all-to-all-start = ((bf16[4,144,960]{2,1,0:T(8,128)(2,1)}), bf16[4,144,960]{2,1,0:T(8,128)(2,1)}, u32[]{:S(2)}, u32[]{:S(2)}) async-start(bf16[4,144,960]{2,1,0:T(8,128)(2,1)} %shard_map.204), calls=%async_computation | async-start | bytes 2359296 | tf_op jit(solution)/shard_map/all_to_all | solution.py:298
  33.7 84.2 %all-gather.5.cloned.1.call-start = ((), (), s32[]{:S(2)}) async-start(), calls=%async_computation.9 | async-start | bytes 2457600 | tf_op jit(solution)/shard_map/all_gather | solution.py:322
  39.1 33.9 %collective-permute-start.10 = (bf16[240,960]{0,1:T(8,128)(2,1)}, bf16[240,960]{0,1:T(8,128)(2,1)}, u32[]{:S(2)}, u32[]{:S(2)}) collective-permute-start(bf16[240,960]{0,1:T(8,128)(2,1)} %broadcast_select_fusion.8), channel_id=1, source_target_pairs={{0,16},{16,0},{1,17},{17,1},{2,18},{18,2},{3,19},{19,3},{4,20},{20... | collective-permute-start | bytes 1382408 | tf_op jit(solution)/shard_map/ppermute | solution.py:38
  40.3 30.4 %collective-permute-start.2 = (bf16[240,640]{1,0:T(8,128)(2,1)S(1)}, bf16[240,640]{1,0:T(8,128)(2,1)S(1)}, u32[]{:S(2)}, u32[]{:S(2)}) collective-permute-start(bf16[240,640]{1,0:T(8,128)(2,1)S(1)} %constant_dynamic-slice_fusion.6.refs_0_), channel_id=1, source_target_pairs={{0,12},{4,0},{8,4},{12,8},{1,13},{5,1},{9,5},{13,9},{2,14},{6,2},{... | collective-permute-start | bytes 921608 | tf_op jit(solution)/shard_map/ppermute | solution.py:45
  42.4 28.3 %collective-permute-start.1 = (bf16[240,640]{1,0:T(8,128)(2,1)S(1)}, bf16[240,640]{1,0:T(8,128)(2,1)S(1)}, u32[]{:S(2)}, u32[]{:S(2)}) collective-permute-start(bf16[240,640]{1,0:T(8,128)(2,1)S(1)} %constant_dynamic-slice_fusion.6.refs_0_), channel_id=1, source_target_pairs={{0,8},{4,12},{8,0},{12,4},{1,9},{5,13},{9,1},{13,5},{2,10},{6,14},... | collective-permute-start | bytes 921608 | tf_op jit(solution)/shard_map/ppermute | solution.py:45
  47.2 24.9 %collective-permute-start = (bf16[240,640]{1,0:T(8,128)(2,1)S(1)}, bf16[240,640]{1,0:T(8,128)(2,1)S(1)}, u32[]{:S(2)}, u32[]{:S(2)}) collective-permute-start(bf16[240,640]{1,0:T(8,128)(2,1)S(1)} %constant_dynamic-slice_fusion.6.refs_0_), channel_id=1, source_target_pairs={{0,4},{4,8},{8,12},{12,0},{1,5},{5,9},{9,13},{13,1},{2,6},{6,10},{... | collective-permute-start | bytes 921608 | tf_op jit(solution)/shard_map/ppermute | solution.py:45
  75.4 126.5 %all-gather.7.cloned.1.call-start = ((), (), s32[]{:S(2)}) async-start(), calls=%async_computation.10 | async-start | bytes 2457600 | tf_op jit(solution)/shard_map/all_gather | solution.py:324
  75.4 19.6 %collective-permute-start.9 = (bf16[960,640]{1,0:T(8,128)(2,1)S(1)}, bf16[960,640]{1,0:T(8,128)(2,1)S(1)}, u32[]{:S(2)}, u32[]{:S(2)}) collective-permute-start(bf16[960,640]{1,0:T(8,128)(2,1)S(1)} %bitcast.410), channel_id=1, source_target_pairs={{0,3},{1,2},{2,1},{3,0},{4,7},{5,6},{6,5},{7,4},{8,11},{9,10},{10,... | collective-permute-start | bytes 3686408 | tf_op jit(solution)/shard_map/ppermute | solution.py:52
  78.9 29.3 %collective-permute-start.8 = (bf16[960,640]{1,0:T(8,128)(2,1)S(1)}, bf16[960,640]{1,0:T(8,128)(2,1)S(1)}, u32[]{:S(2)}, u32[]{:S(2)}) collective-permute-start(bf16[960,640]{1,0:T(8,128)(2,1)S(1)} %bitcast.411), channel_id=1, source_target_pairs={{0,2},{1,3},{2,0},{3,1},{4,6},{5,7},{6,4},{7,5},{8,10},{9,11},{10,... | collective-permute-start | bytes 3686408 | tf_op jit(solution)/shard_map/ppermute | solution.py:52
  81.3 26.9 %collective-permute-start.7 = (bf16[960,640]{1,0:T(8,128)(2,1)S(1)}, bf16[960,640]{1,0:T(8,128)(2,1)S(1)}, u32[]{:S(2)}, u32[]{:S(2)}) collective-permute-start(bf16[960,640]{1,0:T(8,128)(2,1)S(1)} %bitcast.412), channel_id=1, source_target_pairs={{0,1},{1,0},{2,3},{3,2},{4,5},{5,4},{6,7},{7,6},{8,9},{9,8},{10,11... | collective-permute-start | bytes 3686408 | tf_op jit(solution)/shard_map/ppermute | solution.py:52
  117.9 46.9 %collective-permute-start.11 = (bf16[4,960,640]{2,1,0:T(8,128)(2,1)}, bf16[4,960,640]{2,1,0:T(8,128)(2,1)}, u32[]{:S(2)}, u32[]{:S(2)}) collective-permute-start(bf16[4,960,640]{2,1,0:T(8,128)(2,1)} %copy-done.2), channel_id=1, source_target_pairs={{0,16},{1,17},{2,18},{3,19},{4,20},{5,21},{6,22},{7,23},{8,24},{9,... | collective-permute-start | bytes 14745608 | tf_op jit(solution)/shard_map/ppermute | solution.py:34
  128.5 18.6 %collective-permute-start.6 = (bf16[2,960]{1,0:T(2,128)(2,1)S(1)}, bf16[2,960]{1,0:T(2,128)(2,1)S(1)}, u32[]{:S(2)}, u32[]{:S(2)}) collective-permute-start(bf16[2,960]{1,0:T(2,128)(2,1)S(1)} %reshape.680), channel_id=1, source_target_pairs={{0,16},{16,0},{1,17},{17,1},{2,18},{18,2},{3,19},{19,3},{4,20},{20... | collective-permute-start | bytes 11528 | tf_op jit(solution)/shard_map/ppermute | solution.py:38
  157.3 246.8 %reduce-scatter.5.cloned.1.call-start = ((), (), s32[]{:S(2)}) async-start(), calls=%async_computation.5 | async-start | bytes 2457600 | tf_op jit(solution)/shard_map/reduce_scatter | solution.py:381
  157.4 46.2 %collective-permute-start.15 = (bf16[960,640]{1,0:T(8,128)(2,1)}, bf16[960,640]{1,0:T(8,128)(2,1)}, u32[]{:S(2)}, u32[]{:S(2)}) collective-permute-start(bf16[960,640]{1,0:T(8,128)(2,1)} %bitcast.48), channel_id=1, source_target_pairs={{0,16},{16,0},{1,17},{17,1},{2,18},{18,2},{3,19},{19,3},{4,20},{20... | collective-permute-start | bytes 3686408 | tf_op jit(solution)/shard_map/ppermute | solution.py:38
  164.8 46.6 %collective-permute-start.16 = (bf16[320,960]{1,0:T(8,128)(2,1)}, bf16[320,960]{1,0:T(8,128)(2,1)}, u32[]{:S(2)}, u32[]{:S(2)}) collective-permute-start(bf16[320,960]{1,0:T(8,128)(2,1)} %bitcast.53), channel_id=1, source_target_pairs={{0,16},{16,0},{1,17},{17,1},{2,18},{18,2},{3,19},{19,3},{4,20},{20... | collective-permute-start | bytes 1843208 | tf_op jit(solution)/shard_map/ppermute | solution.py:38
  171.5 23.8 %collective-permute-start.26 = (bf16[960,640]{1,0:T(8,128)(2,1)S(1)}, bf16[960,640]{1,0:T(8,128)(2,1)S(1)}, u32[]{:S(2)}, u32[]{:S(2)}) collective-permute-start(bf16[960,640]{1,0:T(8,128)(2,1)S(1)} %bitcast.406), channel_id=1, source_target_pairs={{16,19},{17,18},{18,17},{19,16},{20,23},{21,22},{22,21},{23,20},{2... | collective-permute-start | bytes 3686408 | tf_op jit(solution)/shard_map/ppermute | solution.py:52
  172.3 23.1 %collective-permute-start.25 = (bf16[960,640]{1,0:T(8,128)(2,1)S(1)}, bf16[960,640]{1,0:T(8,128)(2,1)}, u32[]{:S(2)}, u32[]{:S(2)}) collective-permute-start(bf16[960,640]{1,0:T(8,128)(2,1)S(1)} %bitcast.407), channel_id=1, source_target_pairs={{16,18},{17,19},{18,16},{19,17},{20,22},{21,23},{22,20},{23,21},{2... | collective-permute-start | bytes 3686408 | tf_op jit(solution)/shard_map/ppermute | solution.py:52
  174.0 21.4 %collective-permute-start.24 = (bf16[960,640]{1,0:T(8,128)(2,1)S(1)}, bf16[960,640]{1,0:T(8,128)(2,1)}, u32[]{:S(2)}, u32[]{:S(2)}) collective-permute-start(bf16[960,640]{1,0:T(8,128)(2,1)S(1)} %bitcast.408), channel_id=1, source_target_pairs={{16,17},{17,16},{18,19},{19,18},{20,21},{21,20},{22,23},{23,22},{2... | collective-permute-start | bytes 3686408 | tf_op jit(solution)/shard_map/ppermute | solution.py:52
  199.4 44.7 %collective-permute-start.27 = (bf16[4,960,640]{2,1,0:T(8,128)(2,1)}, bf16[4,960,640]{2,1,0:T(8,128)(2,1)}, u32[]{:S(2)}, u32[]{:S(2)}) collective-permute-start(bf16[4,960,640]{2,1,0:T(8,128)(2,1)} %shard_map.208), channel_id=1, source_target_pairs={{16,0},{17,1},{18,2},{19,3},{20,4},{21,5},{22,6},{23,7},{24,8},{25... | collective-permute-start | bytes 14745608 | tf_op jit(solution)/shard_map/ppermute | solution.py:34
  213.1 19.8 %collective-permute-start.17 = (bf16[128,960]{0,1:T(8,128)(2,1)S(1)}, bf16[128,960]{0,1:T(8,128)(2,1)S(1)}, u32[]{:S(2)}, u32[]{:S(2)}) collective-permute-start(bf16[128,960]{0,1:T(8,128)(2,1)S(1)} %get-tuple-element.294), channel_id=1, source_target_pairs={{0,1},{1,0},{2,3},{3,2},{16,17},{17,16},{18,19},{19,18},{4,5},{5,4... | collective-permute-start | bytes 737288 | tf_op jit(solution)/shard_map/ppermute | solution.py:52
  214.1 18.8 %collective-permute-start.19 = (bf16[128,960]{0,1:T(8,128)(2,1)S(1)}, bf16[128,960]{0,1:T(8,128)(2,1)S(1)}, u32[]{:S(2)}, u32[]{:S(2)}) collective-permute-start(bf16[128,960]{0,1:T(8,128)(2,1)S(1)} %get-tuple-element.295), channel_id=1, source_target_pairs={{0,2},{1,3},{2,0},{3,1},{16,18},{17,19},{18,16},{19,17},{4,6},{5,7... | collective-permute-start | bytes 737288 | tf_op jit(solution)/shard_map/ppermute | solution.py:52
  216.2 14.7 %collective-permute-start.28 = (bf16[240,320]{1,0:T(8,128)(2,1)S(1)}, bf16[240,320]{1,0:T(8,128)(2,1)S(1)}, u32[]{:S(2)}, u32[]{:S(2)}) collective-permute-start(bf16[240,320]{1,0:T(8,128)(2,1)S(1)} %get-tuple-element.251), channel_id=1, source_target_pairs={{0,1},{1,0},{2,3},{3,2},{16,17},{17,16},{18,19},{19,18},{4,5},{5,4... | collective-permute-start | bytes 460808 | tf_op jit(solution)/shard_map/ppermute | solution.py:52
  224.3 48.4 %collective-permute-start.32 = (bf16[960,640]{1,0:T(8,128)(2,1)}, bf16[960,640]{1,0:T(8,128)(2,1)}, u32[]{:S(2)}, u32[]{:S(2)}) collective-permute-start(bf16[960,640]{1,0:T(8,128)(2,1)} %bitcast.80), channel_id=1, source_target_pairs={{0,16},{16,0},{1,17},{17,1},{2,18},{18,2},{3,19},{19,3},{4,20},{20... | collective-permute-start | bytes 3686408 | tf_op jit(solution)/shard_map/ppermute | solution.py:38
  235.4 39.2 %collective-permute-start.31 = (bf16[320,960]{1,0:T(8,128)(2,1)}, bf16[320,960]{1,0:T(8,128)(2,1)}, u32[]{:S(2)}, u32[]{:S(2)}) collective-permute-start(bf16[320,960]{1,0:T(8,128)(2,1)} %bitcast.78), channel_id=1, source_target_pairs={{0,16},{16,0},{1,17},{17,1},{2,18},{18,2},{3,19},{19,3},{4,20},{20... | collective-permute-start | bytes 1843208 | tf_op jit(solution)/shard_map/ppermute | solution.py:38
  284.8 24.7 %collective-permute-start.37 = (bf16[960,640]{1,0:T(8,128)(2,1)S(1)}, bf16[960,640]{1,0:T(8,128)(2,1)S(1)}, u32[]{:S(2)}, u32[]{:S(2)}) collective-permute-start(bf16[960,640]{1,0:T(8,128)(2,1)S(1)} %convolution_convert_fusion.1), channel_id=1, source_target_pairs={{0,16},{16,0},{1,17},{17,1},{2,18},{18,2},{3,19},{19,3},{4,20},{20... | collective-permute-start | bytes 3686408 | tf_op jit(solution)/shard_map/ppermute | solution.py:38
  325.5 99.4 %reduce-scatter.7.cloned.1.call-start = ((), (), s32[]{:S(2)}) async-start(), calls=%async_computation.6 | async-start | bytes 921600 | tf_op jit(solution)/shard_map/reduce_scatter | solution.py:381
  346.7 50.8 %collective-permute-start.59 = (bf16[960,320]{0,1:T(8,128)(2,1)}, bf16[960,320]{0,1:T(8,128)(2,1)}, u32[]{:S(2)}, u32[]{:S(2)}) collective-permute-start(bf16[960,320]{0,1:T(8,128)(2,1)} %fusion.17), channel_id=1, source_target_pairs={{0,16},{16,0},{1,17},{17,1},{2,18},{18,2},{3,19},{19,3},{4,20},{20... | collective-permute-start | bytes 1843208 | tf_op jit(solution)/shard_map/ppermute | solution.py:38
  362.1 22.9 %collective-permute-start.55 = (bf16[256,960]{0,1:T(8,128)(2,1)}, bf16[256,960]{0,1:T(8,128)(2,1)}, u32[]{:S(2)}, u32[]{:S(2)}) collective-permute-start(bf16[256,960]{0,1:T(8,128)(2,1)} %get-tuple-element.230), channel_id=1, source_target_pairs={{0,16},{16,0},{1,17},{17,1},{2,18},{18,2},{3,19},{19,3},{4,20},{20... | collective-permute-start | bytes 1474568 | tf_op jit(solution)/shard_map/ppermute | solution.py:38
  364.4 39.8 %collective-permute-start.51 = (bf16[320,960]{1,0:T(8,128)(2,1)}, bf16[320,960]{1,0:T(8,128)(2,1)}, u32[]{:S(2)}, u32[]{:S(2)}) collective-permute-start(bf16[320,960]{1,0:T(8,128)(2,1)} %convolution_convert_fusion.2), channel_id=1, source_target_pairs={{0,16},{16,0},{1,17},{17,1},{2,18},{18,2},{3,19},{19,3},{4,20},{20... | collective-permute-start | bytes 1843208 | tf_op jit(solution)/shard_map/ppermute | solution.py:38
  367.5 48.2 %collective-permute-start.50 = (bf16[960,640]{1,0:T(8,128)(2,1)}, bf16[960,640]{1,0:T(8,128)(2,1)}, u32[]{:S(2)}, u32[]{:S(2)}) collective-permute-start(bf16[960,640]{1,0:T(8,128)(2,1)} %convolution_convert_fusion), channel_id=1, source_target_pairs={{0,16},{16,0},{1,17},{17,1},{2,18},{18,2},{3,19},{19,3},{4,20},{20... | collective-permute-start | bytes 3686408 | tf_op jit(solution)/shard_map/ppermute | solution.py:38
  390.8 15.2 %collective-permute-start.56 = (bf16[2,64,960]{2,1,0:T(8,128)(2,1)}, bf16[2,64,960]{2,1,0:T(8,128)(2,1)}, u32[]{:S(2)}, u32[]{:S(2)}) collective-permute-start(bf16[2,64,960]{2,1,0:T(8,128)(2,1)} %get-tuple-element.216), channel_id=1, source_target_pairs={{0,4},{5,9},{10,14},{15,3},{16,20},{21,25},{26,30},{31,19}} | collective-permute-start | bytes 737288 | tf_op jit(solution)/shard_map/ppermute | solution.py:374
  404.1 94.7 %reduce-scatter.9.cloned.1.call-start = ((), (), s32[]{:S(2)}) async-start(), calls=%async_computation.7 | async-start | bytes 2457600 | tf_op jit(solution)/shard_map/reduce_scatter | solution.py:381
  437.1 16.9 %collective-permute-start.64 = (bf16[240,1280]{1,0:T(8,128)(2,1)}, bf16[240,1280]{1,0:T(8,128)(2,1)}, u32[]{:S(2)}, u32[]{:S(2)}) collective-permute-start(bf16[240,1280]{1,0:T(8,128)(2,1)} %pad_maximum_fusion.12), channel_id=1, source_target_pairs={{0,16},{1,17},{2,18},{3,19},{4,20},{5,21},{6,22},{7,23},{8,24},{9,... | collective-permute-start | bytes 1843208 | tf_op jit(solution)/shard_map/ppermute | solution.py:34
  439.5 85.9 %reduce-scatter.11.cloned.1.call-start = ((), (), s32[]{:S(2)}) async-start(), calls=%async_computation.8 | async-start | bytes 983040 | tf_op jit(solution)/shard_map/reduce_scatter | solution.py:381
  451.8 17.3 %collective-permute-start.68 = (bf16[960,320]{0,1:T(8,128)(2,1)}, bf16[960,320]{0,1:T(8,128)(2,1)}, u32[]{:S(2)}, u32[]{:S(2)}) collective-permute-start(bf16[960,320]{0,1:T(8,128)(2,1)} %fusion.18), channel_id=1, source_target_pairs={{0,16},{16,0},{1,17},{17,1},{2,18},{18,2},{3,19},{19,3},{4,20},{20... | collective-permute-start | bytes 1843208 | tf_op jit(solution)/shard_map/ppermute | solution.py:38
  456.1 37.6 %collective-permute-start.67 = (bf16[240,2560]{1,0:T(8,128)(2,1)S(1)}, bf16[240,2560]{1,0:T(8,128)(2,1)S(1)}, u32[]{:S(2)}, u32[]{:S(2)}) collective-permute-start(bf16[240,2560]{1,0:T(8,128)(2,1)S(1)} %concatenate.231.refs_0_), channel_id=1, source_target_pairs={{16,19},{17,18},{18,17},{19,16},{20,23},{21,22},{22,21},{23,20},{2... | collective-permute-start | bytes 3686408 | tf_op jit(solution)/shard_map/ppermute | solution.py:52
  456.9 36.9 %collective-permute-start.66 = (bf16[240,2560]{1,0:T(8,128)(2,1)S(1)}, bf16[240,2560]{1,0:T(8,128)(2,1)}, u32[]{:S(2)}, u32[]{:S(2)}) collective-permute-start(bf16[240,2560]{1,0:T(8,128)(2,1)S(1)} %concatenate.231.refs_0_), channel_id=1, source_target_pairs={{16,18},{17,19},{18,16},{19,17},{20,22},{21,23},{22,20},{23,21},{2... | collective-permute-start | bytes 3686408 | tf_op jit(solution)/shard_map/ppermute | solution.py:52
  458.6 35.1 %collective-permute-start.65 = (bf16[240,2560]{1,0:T(8,128)(2,1)S(1)}, bf16[240,2560]{1,0:T(8,128)(2,1)}, u32[]{:S(2)}, u32[]{:S(2)}) collective-permute-start(bf16[240,2560]{1,0:T(8,128)(2,1)S(1)} %concatenate.231.refs_0_), channel_id=1, source_target_pairs={{16,17},{17,16},{18,19},{19,18},{20,21},{21,20},{22,23},{23,22},{2... | collective-permute-start | bytes 3686408 | tf_op jit(solution)/shard_map/ppermute | solution.py:52
  462.3 21.2 %collective-permute-start.61 = (bf16[2,64,960]{2,1,0:T(8,128)(2,1)}, bf16[2,64,960]{2,1,0:T(8,128)(2,1)}, u32[]{:S(2)}, u32[]{:S(2)}) collective-permute-start(bf16[2,64,960]{2,1,0:T(8,128)(2,1)} %get-tuple-element.213), channel_id=1, source_target_pairs={{0,4},{5,9},{10,14},{15,3},{16,20},{21,25},{26,30},{31,19}} | collective-permute-start | bytes 737288 | tf_op jit(solution)/shard_map/ppermute | solution.py:374
  469.1 21.7 %collective-permute-start.63 = (bf16[2,64,960]{2,1,0:T(8,128)(2,1)}, bf16[2,64,960]{2,1,0:T(8,128)(2,1)}, u32[]{:S(2)}, u32[]{:S(2)}) collective-permute-start(bf16[2,64,960]{2,1,0:T(8,128)(2,1)} %get-tuple-element.214), channel_id=1, source_target_pairs={{0,12},{5,1},{10,6},{15,11},{16,28},{21,17},{26,22},{31,27}} | collective-permute-start | bytes 737288 | tf_op jit(solution)/shard_map/ppermute | solution.py:374
  504.1 24.8 %collective-permute-start.77 = (bf16[240,1920]{1,0:T(8,128)(2,1)S(1)}, bf16[240,1920]{1,0:T(8,128)(2,1)S(1)}, u32[]{:S(2)}, u32[]{:S(2)}) collective-permute-start(bf16[240,1920]{1,0:T(8,128)(2,1)S(1)} %pad_maximum_fusion.9.refs_0_), channel_id=1, source_target_pairs={{0,3},{1,2},{2,1},{3,0},{4,7},{5,6},{6,5},{7,4},{8,11},{9,10},{10,... | collective-permute-start | bytes 2764808 | tf_op jit(solution)/shard_map/ppermute | solution.py:52
  506.1 28.5 %collective-permute-start.76 = (bf16[240,1920]{1,0:T(8,128)(2,1)S(1)}, bf16[240,1920]{1,0:T(8,128)(2,1)S(1)}, u32[]{:S(2)}, u32[]{:S(2)}) collective-permute-start(bf16[240,1920]{1,0:T(8,128)(2,1)S(1)} %pad_maximum_fusion.9.refs_0_), channel_id=1, source_target_pairs={{0,2},{1,3},{2,0},{3,1},{4,6},{5,7},{6,4},{7,5},{8,10},{9,11},{10,... | collective-permute-start | bytes 2764808 | tf_op jit(solution)/shard_map/ppermute | solution.py:52
  514.8 20.9 %collective-permute-start.75 = (bf16[240,1920]{1,0:T(8,128)(2,1)S(1)}, bf16[240,1920]{1,0:T(8,128)(2,1)}, u32[]{:S(2)}, u32[]{:S(2)}) collective-permute-start(bf16[240,1920]{1,0:T(8,128)(2,1)S(1)} %pad_maximum_fusion.9.refs_0_), channel_id=1, source_target_pairs={{0,1},{1,0},{2,3},{3,2},{4,5},{5,4},{6,7},{7,6},{8,9},{9,8},{10,11... | collective-permute-start | bytes 2764808 | tf_op jit(solution)/shard_map/ppermute | solution.py:52
  526.4 14.7 %collective-permute-start.70 = (bf16[240,320]{1,0:T(8,128)(2,1)S(1)}, bf16[240,320]{1,0:T(8,128)(2,1)S(1)}, u32[]{:S(2)}, u32[]{:S(2)}) collective-permute-start(bf16[240,320]{1,0:T(8,128)(2,1)S(1)} %slice_bitcast_fusion.32), channel_id=1, source_target_pairs={{16,0},{17,1},{18,2},{19,3},{20,4},{21,5},{22,6},{23,7},{24,8},{25... | collective-permute-start | bytes 460808 | tf_op jit(solution)/shard_map/ppermute | solution.py:34
  541.3 22.9 %collective-permute-start.73 = (bf16[240,640]{1,0:T(8,128)(2,1)S(1)}, bf16[240,640]{1,0:T(8,128)(2,1)S(1)}, u32[]{:S(2)}, u32[]{:S(2)}) collective-permute-start(bf16[240,640]{1,0:T(8,128)(2,1)S(1)} %pad_maximum_fusion.21.refs_0_), channel_id=1, source_target_pairs={{0,3},{1,2},{2,1},{3,0},{4,7},{5,6},{6,5},{7,4},{8,11},{9,10},{10,... | collective-permute-start | bytes 921608 | tf_op jit(solution)/shard_map/ppermute | solution.py:52
  543.2 21.0 %collective-permute-start.72 = (bf16[240,640]{1,0:T(8,128)(2,1)S(1)}, bf16[240,640]{1,0:T(8,128)(2,1)S(1)}, u32[]{:S(2)}, u32[]{:S(2)}) collective-permute-start(bf16[240,640]{1,0:T(8,128)(2,1)S(1)} %pad_maximum_fusion.21.refs_0_), channel_id=1, source_target_pairs={{0,2},{1,3},{2,0},{3,1},{4,6},{5,7},{6,4},{7,5},{8,10},{9,11},{10,... | collective-permute-start | bytes 921608 | tf_op jit(solution)/shard_map/ppermute | solution.py:52
  546.4 17.8 %collective-permute-start.71 = (bf16[240,640]{1,0:T(8,128)(2,1)S(1)}, bf16[240,640]{1,0:T(8,128)(2,1)S(1)}, u32[]{:S(2)}, u32[]{:S(2)}) collective-permute-start(bf16[240,640]{1,0:T(8,128)(2,1)S(1)} %pad_maximum_fusion.21.refs_0_), channel_id=1, source_target_pairs={{0,1},{1,0},{2,3},{3,2},{4,5},{5,4},{6,7},{7,6},{8,9},{9,8},{10,11... | collective-permute-start | bytes 921608 | tf_op jit(solution)/shard_map/ppermute | solution.py:52
  (144 other events, 714.5 us)
Sparse Core Ops, SparseCore 0:
  75.5 42.3 all-gather.4
  157.4 42.9 all-gather.6
  325.7 40.7 reduce-scatter.4
  404.3 20.6 reduce-scatter.6
  439.6 44.5 reduce-scatter.8
  499.0 26.4 reduce-scatter.10

commit v5 on v4

--- a/solution.py
+++ b/solution.py
@@ -50,6 +50,16 @@
     cores = range(lax.axis_size("section")) if core is None else (core,)
     pairs = [(c * count + r, c * count + (r ^ flip)) for c in cores for r in range(count)]
     return lax.ppermute(value, ("section", "replica"), pairs)
+
+
+def turn_over(value):
+    count = lax.axis_size("replica")
+    pairs = [
+        (b * count + r, (r % TEAM) * count + r - r % TEAM + b)
+        for b in range(TEAM)
+        for r in range(count)
+    ]
+    return lax.ppermute(value, ("shard", "replica"), pairs)
 
 
 def pick(stack, index):
@@ -188,7 +198,7 @@
     return gain_grad, factor * weighted - values * factor * factor * factor * inner
 
 
-def attention_fwd(layer_in, tabs, attn_w, gain):
+def attention_fwd(layer_in, tabs, attn_w, gain, blocks):
     allowed, cos_tab, sin_tab = tabs
     count = layer_in.shape[0]
     x = layer_in.astype(wide)
@@ -199,6 +209,7 @@
     queries = queries.reshape(count, KVH, QH // KVH, HD)
     keys = rotate_fwd(mixed[:, 320:].reshape(count, KVH, HD), cos_tab, sin_tab).astype(low)
     values = dot(normed, attn_w[2][:, :320]).astype(low).reshape(count, KVH, HD)
+    values, blocks = lax.optimization_barrier((values, blocks))
     scores = jnp.einsum("cgrd,sgd->grcs", queries, keys, preferred_element_type=wide) * HD**-0.5
     scores = jnp.where(allowed[None, None], scores, mask_fill)
     exponent = jnp.exp(scores - jnp.max(scores, axis=-1, keepdims=True))
@@ -206,7 +217,7 @@
     attended = jnp.einsum("grcs,sgd->cgrd", probs.astype(low), values, preferred_element_type=wide)
     attended = attended.reshape(count, QH * HD).astype(low)
     branch = jnp.concatenate([dot(attended, attn_w[2][:, 320:]), dot(attended, attn_w[3])], axis=1)
-    return x + branch, (normed, queries, keys, values, probs, attended)
+    return x + branch, (normed, queries, keys, values, probs, attended), blocks
 
 
 def attention_back(layer_in, grad_middle, tabs, attn_w, gain, kept):
@@ -293,20 +304,17 @@
         other = swap(own)
         return [jnp.where(core == layer, own, other) for layer in range(layers)]
 
-    def whole_sequence(mine):
-        blocks = plane_gather(mine, q)
-        return lax.all_to_all(blocks, "shard", 0, 0, tiled=False)
-
     own_segments = lax.dynamic_slice_in_dim(pick(segment_ids[:, 0], core), z * group, group)
     marks = jnp.zeros((16, width), low)
     marks = marks.at[0, :group].set(own_segments.astype(low))
     marks = marks.at[1, : norm_attn.shape[1]].set(norm_attn[0])
     marks = marks.at[2, : norm_ffn.shape[1]].set(norm_ffn[0])
-    entry = whole_sequence(
-        jnp.concatenate([pick(hidden_in[:, 0], core), pick(out_grad[:, 0], core), marks])
-    )
+    entry = jnp.concatenate([pick(hidden_in[:, 0], core), pick(out_grad[:, 0], core), marks])
     attn_rows = z_gather(attn_share, z, 0).reshape(-1, chunk)
-    attn_rows, entry = lax.optimization_barrier((attn_rows, entry))
+    attn_rows, entry, ffn_shares = lax.optimization_barrier(
+        (attn_rows, turn_over(entry), ffn_shares)
+    )
+    entry = plane_gather(entry, q)
     turn = to_core(attn_rows[:16, :128], 1)
     hidden = entry[:, :group].reshape(-1, width)
     top_grad = entry[:, group : 2 * group].reshape(-1, width)
@@ -319,9 +327,11 @@
 
     attn_w, ffn_w, down_w = [None] * 2, [None] * 2, [None] * 2
     rows = z_gather(after(attn_share, turn), z, 1).reshape(-1, chunk)
-    blocks = [lax.all_gather(after(ffn_shares[0], entry), "shard"), None]
-    attn_stack, blocks[0] = lax.optimization_barrier((plane_gather(attn_rows, q, 0), blocks[0]))
-    blocks[1] = lax.all_gather(after(ffn_shares[1], blocks[0]), "shard")
+    blocks = [lax.all_gather(ffn_shares[0], "shard"), None]
+    attn_stack, gains, blocks[0], ffn_shares[1] = lax.optimization_barrier(
+        (plane_gather(attn_rows, q, 0), gains, blocks[0], ffn_shares[1])
+    )
+    blocks[1] = lax.all_gather(ffn_shares[1], "shard")
     attn_w[0] = give(attn_stack, 0)
 
     def unpack(stack):
@@ -329,15 +339,15 @@
         down = unfold(plane_trade(stack[:, :, 2 * own_hid :], q), width).reshape(-1, width)
         return (own, swap(own)), (down, swap(down))
 
-    ffn_w[0], down_w[0] = unpack(blocks[0])
     attn_w[1] = give(plane_gather(after(rows, attn_w[0]), q, 1), 1)
 
     inputs, kept, outputs = [hidden], [], []
     for layer in range(layers):
-        middle, kept_attn = attention_fwd(inputs[layer], tabs, attn_w[layer], gains[layer][0])
+        middle, kept_attn, ready = attention_fwd(
+            inputs[layer], tabs, attn_w[layer], gains[layer][0], blocks[0] if layer == 0 else ()
+        )
         if layer == 0:
-            middle, second = lax.optimization_barrier((middle, blocks[1]))
-            ffn_w[1], down_w[1] = unpack(second)
+            ffn_w[0], down_w[0] = unpack(ready)
         normed = (middle * row_scale(middle) * gains[layer][1]).astype(low)
         gates, ups, acts, partial = [], [], [], 0.0
         for weights, down in zip(ffn_w[layer], down_w[layer]):
@@ -351,6 +361,8 @@
         kept.append((kept_attn, middle, normed, gates, ups, acts))
         if layer < layers - 1:
             result = (middle + plane_sum(partial)).astype(low)
+            result, second = lax.optimization_barrier((result, blocks[1]))
+            ffn_w[1], down_w[1] = unpack(second)
             outputs.append(result)
             inputs.append(result)
 
@@ -360,19 +372,7 @@
         stack = jnp.where(
             core == 0, jnp.stack([mine, other]), jnp.stack([other, mine])
         ).reshape(2, 4, group, width)
-        replicas = lax.axis_size("replica")
-
-        def slice_for(target):
-            return lax.dynamic_index_in_dim(stack, target, 1, keepdims=False)
-
-        total = jnp.where(z == q, slice_for(z), 0)
-        for hop in (1, 2, 3):
-            pairs = [
-                ((r % TEAM) * replicas + r, (r % TEAM + hop) % 4 * replicas + r)
-                for r in range(replicas)
-            ]
-            total = total + lax.ppermute(slice_for((z + hop) % 4), ("shard", "replica"), pairs)
-        return total[None, :, None]
+        return turn_over(lax.dynamic_index_in_dim(stack, q, 1, keepdims=False))[None, :, None]
 
     def exchange(mine, other):
         return (mine + swap(other.astype(low)).astype(wide)).astype(low)
@@ -382,10 +382,6 @@
         return teams_sum(total.astype(wide)).astype(low)
 
     split = w_query.shape[2] + w_key.shape[2] * 2
-
-    def gather_halves(own, owner):
-        other = to_core(own, owner)
-        return jnp.concatenate([own, other] if owner == 0 else [other, own], axis=1)
 
     def attn_half(kept_attn, right, which):
         start = q * chunk + which * half
@@ -396,7 +392,7 @@
         )
 
     gain_grads, input_grads = [None] * 2, [None] * 2
-    attn_sums, pair_sums = [None] * 2, [None] * 2
+    attn_parts, pair_sums = [None] * 2, [None] * 2
     grad = top_grad
     for layer in reversed(range(layers)):
         kept_attn, middle, normed, gates, ups, acts = kept[layer]
@@ -418,8 +414,8 @@
         )
         grad_normed, pair = lax.optimization_barrier((grad_normed, pair))
         if layer == 0:
-            grad_normed, pair, layer_out, attn_sums[1] = lax.optimization_barrier(
-                (grad_normed, pair, layer_out, attn_sums[1])
+            grad_normed, pair, pair_sums[1] = lax.optimization_barrier(
+                (grad_normed, pair, pair_sums[1])
             )
         pair_sums[layer] = sum_z(pair)
         gain_ffn, through = norm_back(grad_normed, middle, gains[layer][1])
@@ -446,41 +442,34 @@
             gain_part = gain_part.reshape(2, 4, -1).transpose(1, 0, 2)
             gain_width = gain_part.shape[2]
             gain_part = jnp.pad(gain_part, ((0, 0), (0, 14), (0, half - gain_width)))
-            attn_part = jnp.concatenate([attn_part, gain_part], axis=1)
             input_grad = spread(input_grads)
-        if layer == 0:
-            pair_sums[0], input_grad, whole_1 = lax.optimization_barrier(
-                (pair_sums[0], input_grad, whole_1)
-            )
-        attn_part = after(attn_part, pair_sums[layer])
-        attn_sums[layer] = sum_z(attn_part)
-        if layer == 1:
-            pair_width = pair_sums[1].shape[1]
-            whole_1 = plane_gather(
-                gather_halves(jnp.concatenate([pair_sums[1], attn_sums[1]], axis=1), 1), q, 1
-            )
-
-    gain_rows = attn_sums[0].shape[0] - 16
-    total = attn_sums[0][gain_rows : gain_rows + 2, :gain_width].astype(wide)
-    pair_0 = plane_gather(gather_halves(pair_sums[0], 0), q, 0)
-    attn_0 = plane_gather(gather_halves(attn_sums[0][:gain_rows], 0), q, 0)
-    whole_width = pair_width + half
-    pair_half = [
-        jnp.where(
-            core == 0,
-            pair_0[:, :, c * pair_width :][:, :, :pair_width],
-            whole_1[:, :, c * whole_width :][:, :, :pair_width],
-        )
-        for c in (0, 1)
-    ]
-    attn_half_sums = [
-        jnp.where(
-            core == 0,
-            attn_0[:, :, c * half :][:, :, :half],
-            whole_1[:, :, c * whole_width + pair_width :][:, :, :half],
-        )
-        for c in (0, 1)
-    ]
+        attn_parts[layer] = attn_part
+
+    rows = attn_parts[0].shape[1]
+    attn_pair = jnp.concatenate(
+        [
+            jnp.concatenate([attn_parts[0], gain_part], axis=1),
+            jnp.pad(attn_parts[1], ((0, 0), (0, 16), (0, 0))),
+        ],
+        axis=2,
+    )
+    attn_pair, pair_sums[0] = lax.optimization_barrier((attn_pair, pair_sums[0]))
+    attn_pair = sum_z(attn_pair)
+    attn_pair, input_grad, layer_out = lax.optimization_barrier((attn_pair, input_grad, layer_out))
+    total = attn_pair[rows : rows + 2, :gain_width].astype(wide)
+
+    def to_owner(first, second):
+        own = jnp.where(core == 0, first, second)
+        other = swap(jnp.where(core == 0, second, first))
+        both = [jnp.where(core == 0, own, other), jnp.where(core == 0, other, own)]
+        return plane_gather(jnp.concatenate(both, axis=1), q)
+
+    def split_halves(stack):
+        cut = stack.shape[2] // 2
+        return stack[:, :, :cut], stack[:, :, cut:]
+
+    pair_half = split_halves(to_owner(*pair_sums))
+    attn_half_sums = split_halves(to_owner(attn_pair[:rows, :half], attn_pair[:rows, half:]))
 
     attn_cols = jnp.concatenate(
         [part[num] for num in range(TEAM) for part in attn_half_sums], axis=1

time: 591 us -> 564 us (0.954)
  the two profiles are of different devices: /device:TPU:10 before, /device:TPU:0 now
where the time goes in v5:
time: 564 us; the launch traced here: 553 us
  waiting for transfers between devices  161 us (29%)
  starting transfers between devices  133 us (24%)
  local copies, waits for them, and re-layouts  84.2 us (15%)
  matrix products  78.7 us (14%)
  other arithmetic  60.6 us (11%)
  Pallas kernels  19.6 us (3%)
  between operations  16.7 us (3%)
    ppermute x43, waiting for transfers between devices, plane_send(): return lax.ppermute(value, ('section', 'replica'), pairs)  131 us
    ppermute x43, starting transfers between devices, plane_send(): return lax.ppermute(value, ('section', 'replica'), pairs)  82 us
    unnamed x221, local copies, waits for them, and re-layouts  34.2 us
    reduce_scatter x3, waiting for transfers between devices, sum_z(): total = lax.psum_scatter(stack, 'shard', scatter_dimension=0, tiled=False)  25.4 us
    dot_general x18, matrix products, dot(): return jnp.dot(a, b, preferred_element_type=wide)  25.3 us
    ppermute x17, starting transfers between devices, swap(): return lax.ppermute(value, 'section', [(0, 1), (1, 0)])  22.3 us
    dot_general x18, matrix products, dot_t(): lax.dot_general(a, b, (((1,), (1,)), ((), ())), preferred_element_type=wide)  21.7 us
    pallas_call x11, Pallas kernels, place(): pl.pallas_call(place_kernel, out_shape=shape, in_specs=[pl.BlockSpec(memo...  19.6 us
  transfers between devices with their start and end apart: 76, of which 35 were waited for; matrix products, arithmetic and copies ran while one was open for 29% of the time, Pallas kernels for 3%

profile of v5, /device:TPU:0, one launch (start us, length us, event | category | flops | bytes accessed | tf_op | source)
XLA Modules:
  0.0 553.4 jit_solution(15107915352202100887)
XLA Ops:
  9.4 2.4 concatenate.192
  11.8 7.0 %collective-permute-start.2 = (bf16[240,640]{1,0:T(8,128)(2,1)S(1)}, bf16[240,640]{1,0:T(8,128)(2,1)S(1)}, u32[]{:S(2)}, u32[]{:S(2)}) collective-permute-start(bf16[240,640]{1,0:T(8,128)(2,1)S(1)} %constant_dynamic-slice_fusion.3.refs_0_), channel_id=1, source_target_pairs={{0,12},{4,0},{8,4},{12,8},{1,13},{5,1},{9,5},{13,9},{2,14},{6,2},{... | collective-permute-start | bytes 921608 | tf_op jit(solution)/shard_map/ppermute | solution.py:45
  20.7 2.9 collective-permute-start
  37.1 2.2 broadcast_select_fusion.6
  39.4 10.7 %collective-permute-start.10 = (bf16[960,640]{1,0:T(8,128)(2,1)S(1)}, bf16[960,640]{1,0:T(8,128)(2,1)}, u32[]{:S(2)}, u32[]{:S(2)}) collective-permute-start(bf16[960,640]{1,0:T(8,128)(2,1)S(1)} %bitcast.390), channel_id=1, source_target_pairs={{0,3},{1,2},{2,1},{3,0},{4,7},{5,6},{6,5},{7,4},{8,11},{9,10},{10,... | collective-permute-start | bytes 3686408 | tf_op jit(solution)/shard_map/ppermute | solution.py:52
  50.1 12.4 %collective-permute-start.9 = (bf16[960,640]{1,0:T(8,128)(2,1)S(1)}, bf16[960,640]{1,0:T(8,128)(2,1)}, u32[]{:S(2)}, u32[]{:S(2)}) collective-permute-start(bf16[960,640]{1,0:T(8,128)(2,1)S(1)} %bitcast.391), channel_id=1, source_target_pairs={{0,2},{1,3},{2,0},{3,1},{4,6},{5,7},{6,4},{7,5},{8,10},{9,11},{10,... | collective-permute-start | bytes 3686408 | tf_op jit(solution)/shard_map/ppermute | solution.py:52
  68.0 22.5 %collective-permute-done.7.refs_3_ = bf16[144,960]{1,0:T(8,128)(2,1)S(1)} collective-permute-done((bf16[144,960]{1,0:T(8,128)(2,1)S(1)}, bf16[144,960]{1,0:T(8,128)(2,1)S(1)}, u32[]{:S(2)}, u32[]{:S(2)}) %collective-permute-start.7) | collective-permute-done | bytes 276512 | tf_op jit(solution)/shard_map/ppermute | solution.py:52
  90.5 9.1 %collective-permute-start.5 = (bf16[144,960]{1,0:T(8,128)(2,1)S(1)}, bf16[144,960]{1,0:T(8,128)(2,1)S(1)}, u32[]{:S(2)}, u32[]{:S(2)}) collective-permute-start(bf16[144,960]{1,0:T(8,128)(2,1)S(1)} %collective-permute-done.3.refs_0_), channel_id=1, source_target_pairs={{0,1},{1,0},{2,3},{3,2},{16,17},{17,16},{18,19},{19,18},{4,5},{5,4... | collective-permute-start | bytes 829448 | tf_op jit(solution)/shard_map/ppermute | solution.py:52
  100.4 3.9 collective-permute-done.5.refs_1_
  109.1 3.3 shard_map.205
  114.6 4.3 collective-permute-start.12
  125.3 2.5 copy.196
  130.9 3.1 broadcast_select_fusion.1
  147.3 2.5 copy.199
  152.9 3.5 collective-permute-start.14
  157.5 4.3 fusion.191
  161.8 2.8 convolution_convert_fusion.5
  171.5 16.4 %collective-permute-start.16 = (bf16[960,640]{1,0:T(8,128)(2,1)}, bf16[960,640]{1,0:T(8,128)(2,1)}, u32[]{:S(2)}, u32[]{:S(2)}) collective-permute-start(bf16[960,640]{1,0:T(8,128)(2,1)} %bitcast.52), channel_id=1, source_target_pairs={{0,16},{16,0},{1,17},{17,1},{2,18},{18,2},{3,19},{19,3},{4,20},{20... | collective-permute-start | bytes 3686408 | tf_op jit(solution)/shard_map/ppermute | solution.py:38
  187.9 4.3 shard_map.208
  193.8 2.8 fusion.193
  201.3 3.3 collective-permute-start.17
  211.0 5.7 %collective-permute-done.18 = bf16[128,960]{0,1:T(8,128)(2,1)S(1)} collective-permute-done((bf16[128,960]{0,1:T(8,128)(2,1)S(1)}, bf16[128,960]{0,1:T(8,128)(2,1)S(1)}, u32[]{:S(2)}, u32[]{:S(2)}) %collective-permute-start.18) | collective-permute-done | bytes 245792 | tf_op jit(solution)/shard_map/ppermute | solution.py:52
  220.5 4.1 collective-permute-done.19
  227.0 2.4 slice.554
  233.2 3.8 collective-permute-done.31.refs_3_
  241.9 2.9 broadcast_select_fusion
  255.8 4.2 fusion.192
  260.1 2.6 convolution_convert_fusion.4
  282.1 4.4 collective-permute-done.34
  288.3 2.5 convolution_add_fusion.7
  291.6 3.0 collective-permute-done.35
  300.0 3.3 collective-permute-done.42.refs_3_
  312.0 4.4 collective-permute-done.43
  353.3 3.9 collective-permute-done.47
  360.4 4.8 collective-permute-done.48
  373.0 2.3 copy.228
  406.8 25.4 %reduce-scatter.6.cloned.1.call-done = bf16[1,240,960]{2,1,0:T(8,128)(2,1)} async-done(((bf16[4,240,960]{2,1,0:T(8,128)(2,1)}), bf16[1,240,960]{2,1,0:T(8,128)(2,1)}) %reduce-scatter.6.cloned.1.call-update) | async-done | bytes 460816 | tf_op jit(solution)/shard_map/reduce_scatter | solution.py:381
  436.2 2.5 collective-permute-start.70
  439.7 2.7 broadcast_select_fusion.5
  448.3 3.6 collective-permute-start.62
  456.9 3.9 collective-permute-start.60
  460.8 2.7 collective-permute-done.70.refs_3_
  463.5 26.3 %collective-permute-done.69.refs_2_ = bf16[240,1920]{1,0:T(8,128)(2,1)S(1)} collective-permute-done((bf16[240,1920]{1,0:T(8,128)(2,1)S(1)}, bf16[240,1920]{1,0:T(8,128)(2,1)S(1)}, u32[]{:S(2)}, u32[]{:S(2)}) %collective-permute-start.69) | collective-permute-done | bytes 921632 | tf_op jit(solution)/shard_map/ppermute | solution.py:52
  489.8 11.3 %collective-permute-done.68.refs_1_ = bf16[240,1920]{1,0:T(8,128)(2,1)} collective-permute-done((bf16[240,1920]{1,0:T(8,128)(2,1)S(1)}, bf16[240,1920]{1,0:T(8,128)(2,1)}, u32[]{:S(2)}, u32[]{:S(2)}) %collective-permute-start.68) | collective-permute-done | bytes 921632 | tf_op jit(solution)/shard_map/ppermute | solution.py:52
  508.7 3.6 fusion.170
  520.0 4.0 collective-permute-start.65
  524.7 6.4 %collective-permute-done.66.refs_3_ = bf16[240,640]{1,0:T(8,128)(2,1)S(1)} collective-permute-done((bf16[240,640]{1,0:T(8,128)(2,1)S(1)}, bf16[240,640]{1,0:T(8,128)(2,1)S(1)}, u32[]{:S(2)}, u32[]{:S(2)}) %collective-permute-start.66) | collective-permute-done | bytes 307232 | tf_op jit(solution)/shard_map/ppermute | solution.py:52
  531.0 6.2 %collective-permute-done.65.refs_2_ = bf16[240,640]{1,0:T(8,128)(2,1)S(1)} collective-permute-done((bf16[240,640]{1,0:T(8,128)(2,1)S(1)}, bf16[240,640]{1,0:T(8,128)(2,1)S(1)}, u32[]{:S(2)}, u32[]{:S(2)}) %collective-permute-start.65) | collective-permute-done | bytes 307232 | tf_op jit(solution)/shard_map/ppermute | solution.py:52
  (581 shorter events, 257.9 us)
Async XLA Ops:
  7.2 107.4 %all-gather.5.cloned.1.call-start = ((), (), s32[]{:S(2)}) async-start(), calls=%async_computation.6 | async-start | bytes 2457600 | tf_op jit(solution)/shard_map/all_gather | solution.py:330
  11.8 20.4 %collective-permute-start.2 = (bf16[240,640]{1,0:T(8,128)(2,1)S(1)}, bf16[240,640]{1,0:T(8,128)(2,1)S(1)}, u32[]{:S(2)}, u32[]{:S(2)}) collective-permute-start(bf16[240,640]{1,0:T(8,128)(2,1)S(1)} %constant_dynamic-slice_fusion.3.refs_0_), channel_id=1, source_target_pairs={{0,12},{4,0},{8,4},{12,8},{1,13},{5,1},{9,5},{13,9},{2,14},{6,2},{... | collective-permute-start | bytes 921608 | tf_op jit(solution)/shard_map/ppermute | solution.py:45
  18.8 15.1 %collective-permute-start.1 = (bf16[240,640]{1,0:T(8,128)(2,1)S(1)}, bf16[240,640]{1,0:T(8,128)(2,1)S(1)}, u32[]{:S(2)}, u32[]{:S(2)}) collective-permute-start(bf16[240,640]{1,0:T(8,128)(2,1)S(1)} %constant_dynamic-slice_fusion.3.refs_0_), channel_id=1, source_target_pairs={{0,8},{4,12},{8,0},{12,4},{1,9},{5,13},{9,1},{13,5},{2,10},{6,14},... | collective-permute-start | bytes 921608 | tf_op jit(solution)/shard_map/ppermute | solution.py:45
  20.7 13.2 %collective-permute-start = (bf16[240,640]{1,0:T(8,128)(2,1)S(1)}, bf16[240,640]{1,0:T(8,128)(2,1)S(1)}, u32[]{:S(2)}, u32[]{:S(2)}) collective-permute-start(bf16[240,640]{1,0:T(8,128)(2,1)S(1)} %constant_dynamic-slice_fusion.3.refs_0_), channel_id=1, source_target_pairs={{0,4},{4,8},{8,12},{12,0},{1,5},{5,9},{9,13},{13,1},{2,6},{6,10},{... | collective-permute-start | bytes 921608 | tf_op jit(solution)/shard_map/ppermute | solution.py:45
  30.6 8.8 %collective-permute-start.3 = (bf16[144,960]{1,0:T(8,128)(2,1)}, bf16[144,960]{1,0:T(8,128)(2,1)S(1)}, u32[]{:S(2)}, u32[]{:S(2)}) collective-permute-start(bf16[144,960]{1,0:T(8,128)(2,1)} %pad_maximum_fusion.21), channel_id=1, source_target_pairs={{0,0},{1,4},{2,8},{3,12},{4,1},{5,5},{6,9},{7,13},{8,2},{9,6},{10,... | collective-permute-start | bytes 829448 | tf_op jit(solution)/shard_map/ppermute | solution.py:62
  39.3 186.4 %all-gather.7.cloned.1.call-start = ((), (), s32[]{:S(2)}) async-start(), calls=%async_computation.7 | async-start | bytes 2457600 | tf_op jit(solution)/shard_map/all_gather | solution.py:334
  39.4 69.7 %collective-permute-start.10 = (bf16[960,640]{1,0:T(8,128)(2,1)S(1)}, bf16[960,640]{1,0:T(8,128)(2,1)}, u32[]{:S(2)}, u32[]{:S(2)}) collective-permute-start(bf16[960,640]{1,0:T(8,128)(2,1)S(1)} %bitcast.390), channel_id=1, source_target_pairs={{0,3},{1,2},{2,1},{3,0},{4,7},{5,6},{6,5},{7,4},{8,11},{9,10},{10,... | collective-permute-start | bytes 3686408 | tf_op jit(solution)/shard_map/ppermute | solution.py:52
  50.1 59.0 %collective-permute-start.9 = (bf16[960,640]{1,0:T(8,128)(2,1)S(1)}, bf16[960,640]{1,0:T(8,128)(2,1)}, u32[]{:S(2)}, u32[]{:S(2)}) collective-permute-start(bf16[960,640]{1,0:T(8,128)(2,1)S(1)} %bitcast.391), channel_id=1, source_target_pairs={{0,2},{1,3},{2,0},{3,1},{4,6},{5,7},{6,4},{7,5},{8,10},{9,11},{10,... | collective-permute-start | bytes 3686408 | tf_op jit(solution)/shard_map/ppermute | solution.py:52
  62.5 46.5 %collective-permute-start.8 = (bf16[960,640]{1,0:T(8,128)(2,1)S(1)}, bf16[960,640]{1,0:T(8,128)(2,1)}, u32[]{:S(2)}, u32[]{:S(2)}) collective-permute-start(bf16[960,640]{1,0:T(8,128)(2,1)S(1)} %bitcast.392), channel_id=1, source_target_pairs={{0,1},{1,0},{2,3},{3,2},{4,5},{5,4},{6,7},{7,6},{8,9},{9,8},{10,11... | collective-permute-start | bytes 3686408 | tf_op jit(solution)/shard_map/ppermute | solution.py:52
  64.5 26.0 %collective-permute-start.7 = (bf16[144,960]{1,0:T(8,128)(2,1)S(1)}, bf16[144,960]{1,0:T(8,128)(2,1)S(1)}, u32[]{:S(2)}, u32[]{:S(2)}) collective-permute-start(bf16[144,960]{1,0:T(8,128)(2,1)S(1)} %collective-permute-done.3.refs_0_), channel_id=1, source_target_pairs={{0,3},{1,2},{2,1},{3,0},{16,19},{17,18},{18,17},{19,16},{4,7},{5,6... | collective-permute-start | bytes 829448 | tf_op jit(solution)/shard_map/ppermute | solution.py:52
  66.0 33.6 %collective-permute-start.6 = (bf16[144,960]{1,0:T(8,128)(2,1)S(1)}, bf16[144,960]{1,0:T(8,128)(2,1)S(1)}, u32[]{:S(2)}, u32[]{:S(2)}) collective-permute-start(bf16[144,960]{1,0:T(8,128)(2,1)S(1)} %collective-permute-done.3.refs_0_), channel_id=1, source_target_pairs={{0,2},{1,3},{2,0},{3,1},{16,18},{17,19},{18,16},{19,17},{4,6},{5,7... | collective-permute-start | bytes 829448 | tf_op jit(solution)/shard_map/ppermute | solution.py:52
  90.5 13.8 %collective-permute-start.5 = (bf16[144,960]{1,0:T(8,128)(2,1)S(1)}, bf16[144,960]{1,0:T(8,128)(2,1)S(1)}, u32[]{:S(2)}, u32[]{:S(2)}) collective-permute-start(bf16[144,960]{1,0:T(8,128)(2,1)S(1)} %collective-permute-done.3.refs_0_), channel_id=1, source_target_pairs={{0,1},{1,0},{2,3},{3,2},{16,17},{17,16},{18,19},{19,18},{4,5},{5,4... | collective-permute-start | bytes 829448 | tf_op jit(solution)/shard_map/ppermute | solution.py:52
  114.6 16.4 %collective-permute-start.12 = (bf16[4,960,640]{2,1,0:T(8,128)(2,1)}, bf16[4,960,640]{2,1,0:T(8,128)(2,1)}, u32[]{:S(2)}, u32[]{:S(2)}) collective-permute-start(bf16[4,960,640]{2,1,0:T(8,128)(2,1)} %copy-done), channel_id=1, source_target_pairs={{0,16},{1,17},{2,18},{3,19},{4,20},{5,21},{6,22},{7,23},{8,24},{9,... | collective-permute-start | bytes 14745608 | tf_op jit(solution)/shard_map/ppermute | solution.py:34
  129.5 252.7 %reduce-scatter.4.cloned.1.call-start = ((), (), s32[]{:S(2)}) async-start(), calls=%async_computation.3 | async-start | bytes 2457600 | tf_op jit(solution)/shard_map/reduce_scatter | solution.py:381
  139.9 31.5 %collective-permute-start.27 = (bf16[960,640]{1,0:T(8,128)(2,1)S(1)}, bf16[960,640]{1,0:T(8,128)(2,1)}, u32[]{:S(2)}, u32[]{:S(2)}) collective-permute-start(bf16[960,640]{1,0:T(8,128)(2,1)S(1)} %bitcast.386), channel_id=1, source_target_pairs={{16,19},{17,18},{18,17},{19,16},{20,23},{21,22},{22,21},{23,20},{2... | collective-permute-start | bytes 3686408 | tf_op jit(solution)/shard_map/ppermute | solution.py:52
  141.6 29.9 %collective-permute-start.26 = (bf16[960,640]{1,0:T(8,128)(2,1)S(1)}, bf16[960,640]{1,0:T(8,128)(2,1)}, u32[]{:S(2)}, u32[]{:S(2)}) collective-permute-start(bf16[960,640]{1,0:T(8,128)(2,1)S(1)} %bitcast.387), channel_id=1, source_target_pairs={{16,18},{17,19},{18,16},{19,17},{20,22},{21,23},{22,20},{23,21},{2... | collective-permute-start | bytes 3686408 | tf_op jit(solution)/shard_map/ppermute | solution.py:52
  143.3 44.5 %collective-permute-start.25 = (bf16[960,640]{1,0:T(8,128)(2,1)S(1)}, bf16[960,640]{1,0:T(8,128)(2,1)}, u32[]{:S(2)}, u32[]{:S(2)}) collective-permute-start(bf16[960,640]{1,0:T(8,128)(2,1)S(1)} %bitcast.388), channel_id=1, source_target_pairs={{16,17},{17,16},{18,19},{19,18},{20,21},{21,20},{22,23},{23,22},{2... | collective-permute-start | bytes 3686408 | tf_op jit(solution)/shard_map/ppermute | solution.py:52
  152.9 46.5 %collective-permute-start.15 = (bf16[240,320]{1,0:T(8,128)(2,1)}, bf16[240,320]{1,0:T(8,128)(2,1)S(1)}, u32[]{:S(2)}, u32[]{:S(2)}) collective-permute-start(bf16[240,320]{1,0:T(8,128)(2,1)} %get-tuple-element.236), channel_id=1, source_target_pairs={{0,3},{1,2},{2,1},{3,0},{16,19},{17,18},{18,17},{19,16},{4,7},{5,6... | collective-permute-start | bytes 460808 | tf_op jit(solution)/shard_map/ppermute | solution.py:52
  152.9 46.6 %collective-permute-start.14 = (bf16[240,320]{1,0:T(8,128)(2,1)}, bf16[240,320]{1,0:T(8,128)(2,1)S(1)}, u32[]{:S(2)}, u32[]{:S(2)}) collective-permute-start(bf16[240,320]{1,0:T(8,128)(2,1)} %get-tuple-element.237), channel_id=1, source_target_pairs={{0,2},{1,3},{2,0},{3,1},{16,18},{17,19},{18,16},{19,17},{4,6},{5,7... | collective-permute-start | bytes 460808 | tf_op jit(solution)/shard_map/ppermute | solution.py:52
  171.4 28.1 %collective-permute-start.13 = (bf16[240,320]{1,0:T(8,128)(2,1)S(1)}, bf16[240,320]{1,0:T(8,128)(2,1)S(1)}, u32[]{:S(2)}, u32[]{:S(2)}) collective-permute-start(bf16[240,320]{1,0:T(8,128)(2,1)S(1)} %get-tuple-element.238), channel_id=1, source_target_pairs={{0,1},{1,0},{2,3},{3,2},{16,17},{17,16},{18,19},{19,18},{4,5},{5,4... | collective-permute-start | bytes 460808 | tf_op jit(solution)/shard_map/ppermute | solution.py:52
  171.5 33.7 %collective-permute-start.16 = (bf16[960,640]{1,0:T(8,128)(2,1)}, bf16[960,640]{1,0:T(8,128)(2,1)}, u32[]{:S(2)}, u32[]{:S(2)}) collective-permute-start(bf16[960,640]{1,0:T(8,128)(2,1)} %bitcast.52), channel_id=1, source_target_pairs={{0,16},{16,0},{1,17},{17,1},{2,18},{18,2},{3,19},{19,3},{4,20},{20... | collective-permute-start | bytes 3686408 | tf_op jit(solution)/shard_map/ppermute | solution.py:38
  192.1 49.8 %collective-permute-start.28 = (bf16[4,960,640]{2,1,0:T(8,128)(2,1)}, bf16[4,960,640]{2,1,0:T(8,128)(2,1)}, u32[]{:S(2)}, u32[]{:S(2)}) collective-permute-start(bf16[4,960,640]{2,1,0:T(8,128)(2,1)} %shard_map.208), channel_id=1, source_target_pairs={{16,0},{17,1},{18,2},{19,3},{20,4},{21,5},{22,6},{23,7},{24,8},{25... | collective-permute-start | bytes 14745608 | tf_op jit(solution)/shard_map/ppermute | solution.py:34
  230.8 8.0 %collective-permute-start.30 = (bf16[240,320]{1,0:T(8,128)(2,1)S(1)}, bf16[240,320]{1,0:T(8,128)(2,1)S(1)}, u32[]{:S(2)}, u32[]{:S(2)}) collective-permute-start(bf16[240,320]{1,0:T(8,128)(2,1)S(1)} %get-tuple-element.230), channel_id=1, source_target_pairs={{0,2},{1,3},{2,0},{3,1},{16,18},{17,19},{18,16},{19,17},{4,6},{5,7... | collective-permute-start | bytes 460808 | tf_op jit(solution)/shard_map/ppermute | solution.py:52
  233.0 35.0 %collective-permute-start.33 = (bf16[960,640]{1,0:T(8,128)(2,1)}, bf16[960,640]{1,0:T(8,128)(2,1)}, u32[]{:S(2)}, u32[]{:S(2)}) collective-permute-start(bf16[960,640]{1,0:T(8,128)(2,1)} %bitcast.85), channel_id=1, source_target_pairs={{0,16},{16,0},{1,17},{17,1},{2,18},{18,2},{3,19},{19,3},{4,20},{20... | collective-permute-start | bytes 3686408 | tf_op jit(solution)/shard_map/ppermute | solution.py:38
  241.9 28.1 %collective-permute-start.32 = (bf16[320,960]{1,0:T(8,128)(2,1)}, bf16[320,960]{1,0:T(8,128)(2,1)}, u32[]{:S(2)}, u32[]{:S(2)}) collective-permute-start(bf16[320,960]{1,0:T(8,128)(2,1)} %bitcast.83), channel_id=1, source_target_pairs={{0,16},{16,0},{1,17},{17,1},{2,18},{18,2},{3,19},{19,3},{4,20},{20... | collective-permute-start | bytes 1843208 | tf_op jit(solution)/shard_map/ppermute | solution.py:38
  278.1 8.4 %collective-permute-start.34 = (bf16[128,960]{0,1:T(8,128)(2,1)S(1)}, bf16[128,960]{0,1:T(8,128)(2,1)S(1)}, u32[]{:S(2)}, u32[]{:S(2)}) collective-permute-start(bf16[128,960]{0,1:T(8,128)(2,1)S(1)} %get-tuple-element.272), channel_id=1, source_target_pairs={{0,1},{1,0},{2,3},{3,2},{16,17},{17,16},{18,19},{19,18},{4,5},{5,4... | collective-permute-start | bytes 737288 | tf_op jit(solution)/shard_map/ppermute | solution.py:52
  279.1 8.1 %collective-permute-start.36 = (bf16[128,960]{0,1:T(8,128)(2,1)S(1)}, bf16[128,960]{0,1:T(8,128)(2,1)S(1)}, u32[]{:S(2)}, u32[]{:S(2)}) collective-permute-start(bf16[128,960]{0,1:T(8,128)(2,1)S(1)} %get-tuple-element.273), channel_id=1, source_target_pairs={{0,2},{1,3},{2,0},{3,1},{16,18},{17,19},{18,16},{19,17},{4,6},{5,7... | collective-permute-start | bytes 737288 | tf_op jit(solution)/shard_map/ppermute | solution.py:52
  280.0 14.7 %collective-permute-start.39 = (bf16[320,960]{1,0:T(8,128)(2,1)S(1)}, bf16[320,960]{1,0:T(8,128)(2,1)S(1)}, u32[]{:S(2)}, u32[]{:S(2)}) collective-permute-start(bf16[320,960]{1,0:T(8,128)(2,1)S(1)} %convolution_convert_fusion.3), channel_id=1, source_target_pairs={{0,16},{16,0},{1,17},{17,1},{2,18},{18,2},{3,19},{19,3},{4,20},{20... | collective-permute-start | bytes 1843208 | tf_op jit(solution)/shard_map/ppermute | solution.py:38
  280.0 26.5 %collective-permute-start.38 = (bf16[960,640]{1,0:T(8,128)(2,1)S(1)}, bf16[960,640]{1,0:T(8,128)(2,1)S(1)}, u32[]{:S(2)}, u32[]{:S(2)}) collective-permute-start(bf16[960,640]{1,0:T(8,128)(2,1)S(1)} %convolution_convert_fusion.1), channel_id=1, source_target_pairs={{0,16},{16,0},{1,17},{17,1},{2,18},{18,2},{3,19},{19,3},{4,20},{20... | collective-permute-start | bytes 3686408 | tf_op jit(solution)/shard_map/ppermute | solution.py:38
  290.8 8.1 %collective-permute-start.37 = (bf16[128,960]{0,1:T(8,128)(2,1)S(1)}, bf16[128,960]{0,1:T(8,128)(2,1)S(1)}, u32[]{:S(2)}, u32[]{:S(2)}) collective-permute-start(bf16[128,960]{0,1:T(8,128)(2,1)S(1)} %get-tuple-element.271), channel_id=1, source_target_pairs={{0,1},{1,0},{2,3},{3,2},{16,17},{17,16},{18,19},{19,18},{4,5},{5,4... | collective-permute-start | bytes 737288 | tf_op jit(solution)/shard_map/ppermute | solution.py:52
  295.1 8.1 %collective-permute-start.42 = (bf16[80,960]{1,0:T(8,128)(2,1)S(1)}, bf16[80,960]{1,0:T(8,128)(2,1)S(1)}, u32[]{:S(2)}, u32[]{:S(2)}) collective-permute-start(bf16[80,960]{1,0:T(8,128)(2,1)S(1)} %get-tuple-element.250), channel_id=1, source_target_pairs={{0,3},{1,2},{2,1},{3,0},{16,19},{17,18},{18,17},{19,16},{4,7},{5,6... | collective-permute-start | bytes 460808 | tf_op jit(solution)/shard_map/ppermute | solution.py:52
  321.3 110.8 %reduce-scatter.6.cloned.1.call-start = ((), (), s32[]{:S(2)}) async-start(), calls=%async_computation.4 | async-start | bytes 2457600 | tf_op jit(solution)/shard_map/reduce_scatter | solution.py:381
  341.2 30.6 %collective-permute-start.58 = (bf16[960,320]{0,1:T(8,128)(2,1)S(1)}, bf16[960,320]{0,1:T(8,128)(2,1)S(1)}, u32[]{:S(2)}, u32[]{:S(2)}) collective-permute-start(bf16[960,320]{0,1:T(8,128)(2,1)S(1)} %fusion.21), channel_id=1, source_target_pairs={{0,16},{16,0},{1,17},{17,1},{2,18},{18,2},{3,19},{19,3},{4,20},{20... | collective-permute-start | bytes 1843208 | tf_op jit(solution)/shard_map/ppermute | solution.py:38
  348.7 8.4 %collective-permute-start.47 = (bf16[128,960]{0,1:T(8,128)(2,1)S(1)}, bf16[128,960]{0,1:T(8,128)(2,1)S(1)}, u32[]{:S(2)}, u32[]{:S(2)}) collective-permute-start(bf16[128,960]{0,1:T(8,128)(2,1)S(1)} %get-tuple-element.264), channel_id=1, source_target_pairs={{0,1},{1,0},{2,3},{3,2},{16,17},{17,16},{18,19},{19,18},{4,5},{5,4... | collective-permute-start | bytes 737288 | tf_op jit(solution)/shard_map/ppermute | solution.py:52
  351.1 16.6 %collective-permute-start.52 = (bf16[320,960]{1,0:T(8,128)(2,1)S(1)}, bf16[320,960]{1,0:T(8,128)(2,1)S(1)}, u32[]{:S(2)}, u32[]{:S(2)}) collective-permute-start(bf16[320,960]{1,0:T(8,128)(2,1)S(1)} %convolution_convert_fusion.2), channel_id=1, source_target_pairs={{0,16},{16,0},{1,17},{17,1},{2,18},{18,2},{3,19},{19,3},{4,20},{20... | collective-permute-start | bytes 1843208 | tf_op jit(solution)/shard_map/ppermute | solution.py:38
  352.8 25.9 %collective-permute-start.51 = (bf16[960,640]{1,0:T(8,128)(2,1)}, bf16[960,640]{1,0:T(8,128)(2,1)}, u32[]{:S(2)}, u32[]{:S(2)}) collective-permute-start(bf16[960,640]{1,0:T(8,128)(2,1)} %convolution_convert_fusion), channel_id=1, source_target_pairs={{0,16},{16,0},{1,17},{17,1},{2,18},{18,2},{3,19},{19,3},{4,20},{20... | collective-permute-start | bytes 3686408 | tf_op jit(solution)/shard_map/ppermute | solution.py:38
  390.8 116.1 %reduce-scatter.8.cloned.1.call-start = ((), (), s32[]{:S(2)}) async-start(), calls=%async_computation.5 | async-start | bytes 1638400 | tf_op jit(solution)/shard_map/reduce_scatter | solution.py:381
  434.0 10.5 %collective-permute-start.61 = (bf16[256,960]{0,1:T(8,128)(2,1)}, bf16[256,960]{0,1:T(8,128)(2,1)}, u32[]{:S(2)}, u32[]{:S(2)}) collective-permute-start(bf16[256,960]{0,1:T(8,128)(2,1)} %get-tuple-element.216), channel_id=1, source_target_pairs={{0,16},{16,0},{1,17},{17,1},{2,18},{18,2},{3,19},{19,3},{4,20},{20... | collective-permute-start | bytes 1474568 | tf_op jit(solution)/shard_map/ppermute | solution.py:38
  436.2 27.3 %collective-permute-start.70 = (bf16[240,1920]{1,0:T(8,128)(2,1)S(1)}, bf16[240,1920]{1,0:T(8,128)(2,1)S(1)}, u32[]{:S(2)}, u32[]{:S(2)}) collective-permute-start(bf16[240,1920]{1,0:T(8,128)(2,1)S(1)} %pad_maximum_fusion.9.refs_0_), channel_id=1, source_target_pairs={{0,3},{1,2},{2,1},{3,0},{16,19},{17,18},{18,17},{19,16},{4,7},{5,6... | collective-permute-start | bytes 2764808 | tf_op jit(solution)/shard_map/ppermute | solution.py:52
  438.6 51.2 %collective-permute-start.69 = (bf16[240,1920]{1,0:T(8,128)(2,1)S(1)}, bf16[240,1920]{1,0:T(8,128)(2,1)S(1)}, u32[]{:S(2)}, u32[]{:S(2)}) collective-permute-start(bf16[240,1920]{1,0:T(8,128)(2,1)S(1)} %pad_maximum_fusion.9.refs_0_), channel_id=1, source_target_pairs={{0,2},{1,3},{2,0},{3,1},{16,18},{17,19},{18,16},{19,17},{4,6},{5,7... | collective-permute-start | bytes 2764808 | tf_op jit(solution)/shard_map/ppermute | solution.py:52
  439.2 61.9 %collective-permute-start.68 = (bf16[240,1920]{1,0:T(8,128)(2,1)S(1)}, bf16[240,1920]{1,0:T(8,128)(2,1)}, u32[]{:S(2)}, u32[]{:S(2)}) collective-permute-start(bf16[240,1920]{1,0:T(8,128)(2,1)S(1)} %pad_maximum_fusion.9.refs_0_), channel_id=1, source_target_pairs={{0,1},{1,0},{2,3},{3,2},{16,17},{17,16},{18,19},{19,18},{4,5},{5,4... | collective-permute-start | bytes 2764808 | tf_op jit(solution)/shard_map/ppermute | solution.py:52
  443.3 9.8 %collective-permute-start.59 = (bf16[256,960]{0,1:T(8,128)(2,1)}, bf16[256,960]{0,1:T(8,128)(2,1)}, u32[]{:S(2)}, u32[]{:S(2)}) collective-permute-start(bf16[256,960]{0,1:T(8,128)(2,1)} %broadcast_select_fusion.4), channel_id=1, source_target_pairs={{0,16},{16,0},{1,17},{17,1},{2,18},{18,2},{3,19},{19,3},{4,20},{20... | collective-permute-start | bytes 1474568 | tf_op jit(solution)/shard_map/ppermute | solution.py:38
  448.3 58.6 %collective-permute-start.62 = (bf16[2,64,960]{2,1,0:T(8,128)(2,1)}, bf16[2,64,960]{2,1,0:T(8,128)(2,1)}, u32[]{:S(2)}, u32[]{:S(2)}) collective-permute-start(bf16[2,64,960]{2,1,0:T(8,128)(2,1)} %fusion.100), channel_id=1, source_target_pairs={{0,0},{1,4},{2,8},{3,12},{4,1},{5,5},{6,9},{7,13},{8,2},{9,6},{10,... | collective-permute-start | bytes 737288 | tf_op jit(solution)/shard_map/ppermute | solution.py:62
  456.9 50.0 %collective-permute-start.60 = (bf16[2,64,960]{2,1,0:T(8,128)(2,1)}, bf16[2,64,960]{2,1,0:T(8,128)(2,1)}, u32[]{:S(2)}, u32[]{:S(2)}) collective-permute-start(bf16[2,64,960]{2,1,0:T(8,128)(2,1)} %fusion.104), channel_id=1, source_target_pairs={{0,0},{1,4},{2,8},{3,12},{4,1},{5,5},{6,9},{7,13},{8,2},{9,6},{10,... | collective-permute-start | bytes 737288 | tf_op jit(solution)/shard_map/ppermute | solution.py:62
  508.7 10.1 %collective-permute-start.63 = (bf16[240,320]{1,0:T(8,128)(2,1)}, bf16[240,320]{1,0:T(8,128)(2,1)}, u32[]{:S(2)}, u32[]{:S(2)}) collective-permute-start(bf16[240,320]{1,0:T(8,128)(2,1)} %broadcast_select_fusion.16), channel_id=1, source_target_pairs={{0,16},{16,0},{1,17},{17,1},{2,18},{18,2},{3,19},{19,3},{4,20},{20... | collective-permute-start | bytes 460808 | tf_op jit(solution)/shard_map/ppermute | solution.py:38
  520.0 11.1 %collective-permute-start.66 = (bf16[240,640]{1,0:T(8,128)(2,1)S(1)}, bf16[240,640]{1,0:T(8,128)(2,1)S(1)}, u32[]{:S(2)}, u32[]{:S(2)}) collective-permute-start(bf16[240,640]{1,0:T(8,128)(2,1)S(1)} %pad_maximum_fusion.20.refs_0_), channel_id=1, source_target_pairs={{0,3},{1,2},{2,1},{3,0},{16,19},{17,18},{18,17},{19,16},{4,7},{5,6... | collective-permute-start | bytes 921608 | tf_op jit(solution)/shard_map/ppermute | solution.py:52
  520.0 17.2 %collective-permute-start.65 = (bf16[240,640]{1,0:T(8,128)(2,1)S(1)}, bf16[240,640]{1,0:T(8,128)(2,1)S(1)}, u32[]{:S(2)}, u32[]{:S(2)}) collective-permute-start(bf16[240,640]{1,0:T(8,128)(2,1)S(1)} %pad_maximum_fusion.20.refs_0_), channel_id=1, source_target_pairs={{0,2},{1,3},{2,0},{3,1},{16,18},{17,19},{18,16},{19,17},{4,6},{5,7... | collective-permute-start | bytes 921608 | tf_op jit(solution)/shard_map/ppermute | solution.py:52
  524.1 13.1 %collective-permute-start.64 = (bf16[240,640]{1,0:T(8,128)(2,1)S(1)}, bf16[240,640]{1,0:T(8,128)(2,1)S(1)}, u32[]{:S(2)}, u32[]{:S(2)}) collective-permute-start(bf16[240,640]{1,0:T(8,128)(2,1)S(1)} %pad_maximum_fusion.20.refs_0_), channel_id=1, source_target_pairs={{0,1},{1,0},{2,3},{3,2},{16,17},{17,16},{18,19},{19,18},{4,5},{5,4... | collective-permute-start | bytes 921608 | tf_op jit(solution)/shard_map/ppermute | solution.py:52
  (135 other events, 539.7 us)
Sparse Core Ops, SparseCore 0:
  39.5 59.4 all-gather.4
  129.6 56.7 all-gather.6
  321.5 40.6 reduce-scatter.3
  390.9 41.2 reduce-scatter.5
  434.9 55.2 reduce-scatter.7

commit v6 on v5

--- a/solution.py
+++ b/solution.py
@@ -382,6 +382,10 @@
         return teams_sum(total.astype(wide)).astype(low)
 
     split = w_query.shape[2] + w_key.shape[2] * 2
+
+    def gather_halves(own, owner):
+        other = to_core(own, owner)
+        return jnp.concatenate([own, other] if owner == 0 else [other, own], axis=1)
 
     def attn_half(kept_attn, right, which):
         start = q * chunk + which * half
@@ -453,7 +457,8 @@
         ],
         axis=2,
     )
-    attn_pair, pair_sums[0] = lax.optimization_barrier((attn_pair, pair_sums[0]))
+    whole_1 = plane_gather(gather_halves(pair_sums[1], 1), q, 1)
+    attn_pair, pair_sums[0], whole_1 = lax.optimization_barrier((attn_pair, pair_sums[0], whole_1))
     attn_pair = sum_z(attn_pair)
     attn_pair, input_grad, layer_out = lax.optimization_barrier((attn_pair, input_grad, layer_out))
     total = attn_pair[rows : rows + 2, :gain_width].astype(wide)
@@ -468,7 +473,8 @@
         cut = stack.shape[2] // 2
         return stack[:, :, :cut], stack[:, :, cut:]
 
-    pair_half = split_halves(to_owner(*pair_sums))
+    whole_0 = plane_gather(gather_halves(pair_sums[0], 0), q, 0)
+    pair_half = split_halves(jnp.where(core == 0, whole_0, whole_1))
     attn_half_sums = split_halves(to_owner(attn_pair[:rows, :half], attn_pair[:rows, half:]))
 
     attn_cols = jnp.concatenate(

time: 564 us -> 561 us (level)
  waiting for transfers between devices: 161 us -> 109 us
  starting transfers between devices: 133 us -> 166 us
  local copies, waits for them, and re-layouts: 84.2 us -> 90.6 us
    ppermute x43 -> x46, waiting for transfers between devices: 131 us -> 90.1 us  [plane_send(): return lax.ppermute(value, ('section', 'replica'), pairs)]
    ppermute x43 -> x46, starting transfers between devices: 82 us -> 112 us  [plane_send(): return lax.ppermute(value, ('section', 'replica'), pairs)]
    reduce_scatter x3, waiting for transfers between devices: 25.4 us -> 17.5 us  [sum_z(): total = lax.psum_scatter(stack, 'shard', scatter_dimension=0, tiled=False)]
    pallas_call x11 -> x12, Pallas kernels: 19.6 us -> 21.9 us  [place(): pl.pallas_call(place_kernel, out_shape=shape, in_specs=[pl.BlockSpec(memo...]
    unnamed x221 -> x231, local copies, waits for them, and re-layouts: 34.2 us -> 34.8 us
    ppermute x17 -> x16, starting transfers between devices: 22.3 us -> 22.6 us  [swap(): return lax.ppermute(value, 'section', [(0, 1), (1, 0)])]
  transfers between devices with their start and end apart: 76 -> 80, of which waited for: 35 -> 31; matrix products, arithmetic and copies ran while one was open for 29% -> 32% of each run, Pallas kernels for 3% -> 4%
where the time goes in v6:
time: 561 us; the launch traced here: 550 us
  starting transfers between devices  166 us (30%)
  waiting for transfers between devices  109 us (19%)
  local copies, waits for them, and re-layouts  90.6 us (16%)
  matrix products  80.2 us (14%)
  other arithmetic  65.4 us (12%)
  Pallas kernels  21.9 us (4%)
  between operations  16.8 us (3%)
    ppermute x46, starting transfers between devices, plane_send(): return lax.ppermute(value, ('section', 'replica'), pairs)  112 us
    ppermute x46, waiting for transfers between devices, plane_send(): return lax.ppermute(value, ('section', 'replica'), pairs)  90.1 us
    unnamed x231, local copies, waits for them, and re-layouts  34.8 us
    dot_general x18, matrix products, dot(): return jnp.dot(a, b, preferred_element_type=wide)  25.3 us
    ppermute x16, starting transfers between devices, swap(): return lax.ppermute(value, 'section', [(0, 1), (1, 0)])  22.6 us
    pallas_call x12, Pallas kernels, place(): pl.pallas_call(place_kernel, out_shape=shape, in_specs=[pl.BlockSpec(memo...  21.9 us
    dot_general x18, matrix products, dot_t(): lax.dot_general(a, b, (((1,), (1,)), ((), ())), preferred_element_type=wide)  21.7 us
    reduce_scatter x3, waiting for transfers between devices, sum_z(): total = lax.psum_scatter(stack, 'shard', scatter_dimension=0, tiled=False)  17.5 us
  transfers between devices with their start and end apart: 80, of which 31 were waited for; matrix products, arithmetic and copies ran while one was open for 32% of the time, Pallas kernels for 4%

profile of v6, /device:TPU:0, one launch (start us, length us, event | category | flops | bytes accessed | tf_op | source)
XLA Modules:
  0.0 550.1 jit_solution(17844327686726671700)
XLA Ops:
  9.4 2.4 concatenate.195
  11.8 7.0 %collective-permute-start.2 = (bf16[240,640]{1,0:T(8,128)(2,1)S(1)}, bf16[240,640]{1,0:T(8,128)(2,1)S(1)}, u32[]{:S(2)}, u32[]{:S(2)}) collective-permute-start(bf16[240,640]{1,0:T(8,128)(2,1)S(1)} %constant_dynamic-slice_fusion.6.refs_0_), channel_id=1, source_target_pairs={{0,12},{4,0},{8,4},{12,8},{1,13},{5,1},{9,5},{13,9},{2,14},{6,2},{... | collective-permute-start | bytes 921608 | tf_op jit(solution)/shard_map/ppermute | solution.py:45
  20.7 2.9 collective-permute-start
  39.6 13.0 %collective-permute-start.10 = (bf16[960,640]{1,0:T(8,128)(2,1)S(1)}, bf16[960,640]{1,0:T(8,128)(2,1)}, u32[]{:S(2)}, u32[]{:S(2)}) collective-permute-start(bf16[960,640]{1,0:T(8,128)(2,1)S(1)} %bitcast.388), channel_id=1, source_target_pairs={{0,3},{1,2},{2,1},{3,0},{4,7},{5,6},{6,5},{7,4},{8,11},{9,10},{10,... | collective-permute-start | bytes 3686408 | tf_op jit(solution)/shard_map/ppermute | solution.py:52
  52.6 12.4 %collective-permute-start.9 = (bf16[960,640]{1,0:T(8,128)(2,1)S(1)}, bf16[960,640]{1,0:T(8,128)(2,1)}, u32[]{:S(2)}, u32[]{:S(2)}) collective-permute-start(bf16[960,640]{1,0:T(8,128)(2,1)S(1)} %bitcast.389), channel_id=1, source_target_pairs={{0,2},{1,3},{2,0},{3,1},{4,6},{5,7},{6,4},{7,5},{8,10},{9,11},{10,... | collective-permute-start | bytes 3686408 | tf_op jit(solution)/shard_map/ppermute | solution.py:52
  70.6 21.5 %collective-permute-done.7.refs_3_ = bf16[144,960]{1,0:T(8,128)(2,1)S(1)} collective-permute-done((bf16[144,960]{1,0:T(8,128)(2,1)S(1)}, bf16[144,960]{1,0:T(8,128)(2,1)S(1)}, u32[]{:S(2)}, u32[]{:S(2)}) %collective-permute-start.7) | collective-permute-done | bytes 276512 | tf_op jit(solution)/shard_map/ppermute | solution.py:52
  92.1 10.1 %collective-permute-start.5 = (bf16[144,960]{1,0:T(8,128)(2,1)S(1)}, bf16[144,960]{1,0:T(8,128)(2,1)S(1)}, u32[]{:S(2)}, u32[]{:S(2)}) collective-permute-start(bf16[144,960]{1,0:T(8,128)(2,1)S(1)} %collective-permute-done.3.refs_0_), channel_id=1, source_target_pairs={{0,1},{1,0},{2,3},{3,2},{16,17},{17,16},{18,19},{19,18},{4,5},{5,4... | collective-permute-start | bytes 829448 | tf_op jit(solution)/shard_map/ppermute | solution.py:52
  102.9 3.9 collective-permute-done.5.refs_1_
  111.6 3.3 shard_map.205
  117.1 4.3 collective-permute-start.12
  127.8 2.5 copy.364
  134.1 3.1 broadcast_select_fusion.1
  150.2 2.5 copy.368
  157.0 3.5 collective-permute-start.14
  162.5 4.3 fusion.191
  166.8 2.8 convolution_convert_fusion.5
  176.5 16.3 %collective-permute-start.16 = (bf16[960,640]{1,0:T(8,128)(2,1)}, bf16[960,640]{1,0:T(8,128)(2,1)}, u32[]{:S(2)}, u32[]{:S(2)}) collective-permute-start(bf16[960,640]{1,0:T(8,128)(2,1)} %bitcast.52), channel_id=1, source_target_pairs={{0,16},{16,0},{1,17},{17,1},{2,18},{18,2},{3,19},{19,3},{4,20},{20... | collective-permute-start | bytes 3686408 | tf_op jit(solution)/shard_map/ppermute | solution.py:38
  192.8 4.3 shard_map.208
  198.8 2.8 fusion.193
  206.3 3.3 collective-permute-start.17
  215.6 5.7 %collective-permute-done.18 = bf16[128,960]{0,1:T(8,128)(2,1)S(1)} collective-permute-done((bf16[128,960]{0,1:T(8,128)(2,1)S(1)}, bf16[128,960]{0,1:T(8,128)(2,1)S(1)}, u32[]{:S(2)}, u32[]{:S(2)}) %collective-permute-start.18) | collective-permute-done | bytes 245792 | tf_op jit(solution)/shard_map/ppermute | solution.py:52
  225.2 4.0 collective-permute-done.19
  231.7 2.4 slice.554
  237.9 3.8 collective-permute-done.31.refs_3_
  246.6 2.9 broadcast_select_fusion
  261.1 3.2 fusion.192
  264.3 2.6 convolution_convert_fusion.4
  286.3 4.4 collective-permute-done.34
  292.5 2.5 convolution_add_fusion.7
  295.9 3.0 collective-permute-done.35
  304.2 3.2 collective-permute-done.42.refs_3_
  316.2 4.4 collective-permute-done.43
  332.7 2.5 multiply_reduce_fusion.3
  358.3 3.9 collective-permute-done.47
  365.4 4.9 collective-permute-done.48
  412.7 3.0 add_convert_fusion.3
  417.9 2.8 fusion.25
  424.7 12.9 %reduce-scatter.6.cloned.1.call-done = bf16[1,240,960]{2,1,0:T(8,128)(2,1)} async-done(((bf16[4,240,960]{2,1,0:T(8,128)(2,1)}), bf16[1,240,960]{2,1,0:T(8,128)(2,1)}) %reduce-scatter.6.cloned.1.call-update) | async-done | bytes 460816 | tf_op jit(solution)/shard_map/reduce_scatter | solution.py:381
  442.7 4.3 collective-permute-start.74
  447.0 2.4 collective-permute-start.73
  449.4 2.5 collective-permute-start.72
  451.9 3.6 broadcast_select_fusion.6
  461.4 3.6 collective-permute-start.66
  470.0 3.6 collective-permute-start.64
  480.9 4.5 reduce-scatter.8.cloned.1.call-done
  487.3 3.6 fusion.170
  499.9 21.0 %collective-permute-start.69 = (bf16[240,640]{1,0:T(8,128)(2,1)S(1)}, bf16[240,640]{1,0:T(8,128)(2,1)S(1)}, u32[]{:S(2)}, u32[]{:S(2)}) collective-permute-start(bf16[240,640]{1,0:T(8,128)(2,1)S(1)} %pad_maximum_fusion.21.refs_0_), channel_id=1, source_target_pairs={{0,2},{1,3},{2,0},{3,1},{16,18},{17,19},{18,16},{19,17},{4,6},{5,7... | collective-permute-start | bytes 921608 | tf_op jit(solution)/shard_map/ppermute | solution.py:52
  521.4 11.4 %collective-permute-done.69.refs_2_ = bf16[240,640]{1,0:T(8,128)(2,1)S(1)} collective-permute-done((bf16[240,640]{1,0:T(8,128)(2,1)S(1)}, bf16[240,640]{1,0:T(8,128)(2,1)S(1)}, u32[]{:S(2)}, u32[]{:S(2)}) %collective-permute-start.69) | collective-permute-done | bytes 307232 | tf_op jit(solution)/shard_map/ppermute | solution.py:52
  (603 shorter events, 274.4 us)
Async XLA Ops:
  7.2 109.9 %all-gather.5.cloned.1.call-start = ((), (), s32[]{:S(2)}) async-start(), calls=%async_computation.6 | async-start | bytes 2457600 | tf_op jit(solution)/shard_map/all_gather | solution.py:330
  11.8 22.0 %collective-permute-start.2 = (bf16[240,640]{1,0:T(8,128)(2,1)S(1)}, bf16[240,640]{1,0:T(8,128)(2,1)S(1)}, u32[]{:S(2)}, u32[]{:S(2)}) collective-permute-start(bf16[240,640]{1,0:T(8,128)(2,1)S(1)} %constant_dynamic-slice_fusion.6.refs_0_), channel_id=1, source_target_pairs={{0,12},{4,0},{8,4},{12,8},{1,13},{5,1},{9,5},{13,9},{2,14},{6,2},{... | collective-permute-start | bytes 921608 | tf_op jit(solution)/shard_map/ppermute | solution.py:45
  18.8 15.1 %collective-permute-start.1 = (bf16[240,640]{1,0:T(8,128)(2,1)S(1)}, bf16[240,640]{1,0:T(8,128)(2,1)S(1)}, u32[]{:S(2)}, u32[]{:S(2)}) collective-permute-start(bf16[240,640]{1,0:T(8,128)(2,1)S(1)} %constant_dynamic-slice_fusion.6.refs_0_), channel_id=1, source_target_pairs={{0,8},{4,12},{8,0},{12,4},{1,9},{5,13},{9,1},{13,5},{2,10},{6,14},... | collective-permute-start | bytes 921608 | tf_op jit(solution)/shard_map/ppermute | solution.py:45
  20.7 13.2 %collective-permute-start = (bf16[240,640]{1,0:T(8,128)(2,1)S(1)}, bf16[240,640]{1,0:T(8,128)(2,1)S(1)}, u32[]{:S(2)}, u32[]{:S(2)}) collective-permute-start(bf16[240,640]{1,0:T(8,128)(2,1)S(1)} %constant_dynamic-slice_fusion.6.refs_0_), channel_id=1, source_target_pairs={{0,4},{4,8},{8,12},{12,0},{1,5},{5,9},{9,13},{13,1},{2,6},{6,10},{... | collective-permute-start | bytes 921608 | tf_op jit(solution)/shard_map/ppermute | solution.py:45
  39.5 190.9 %all-gather.7.cloned.1.call-start = ((), (), s32[]{:S(2)}) async-start(), calls=%async_computation.7 | async-start | bytes 2457600 | tf_op jit(solution)/shard_map/all_gather | solution.py:334
  39.6 72.0 %collective-permute-start.10 = (bf16[960,640]{1,0:T(8,128)(2,1)S(1)}, bf16[960,640]{1,0:T(8,128)(2,1)}, u32[]{:S(2)}, u32[]{:S(2)}) collective-permute-start(bf16[960,640]{1,0:T(8,128)(2,1)S(1)} %bitcast.388), channel_id=1, source_target_pairs={{0,3},{1,2},{2,1},{3,0},{4,7},{5,6},{6,5},{7,4},{8,11},{9,10},{10,... | collective-permute-start | bytes 3686408 | tf_op jit(solution)/shard_map/ppermute | solution.py:52
  52.6 59.0 %collective-permute-start.9 = (bf16[960,640]{1,0:T(8,128)(2,1)S(1)}, bf16[960,640]{1,0:T(8,128)(2,1)}, u32[]{:S(2)}, u32[]{:S(2)}) collective-permute-start(bf16[960,640]{1,0:T(8,128)(2,1)S(1)} %bitcast.389), channel_id=1, source_target_pairs={{0,2},{1,3},{2,0},{3,1},{4,6},{5,7},{6,4},{7,5},{8,10},{9,11},{10,... | collective-permute-start | bytes 3686408 | tf_op jit(solution)/shard_map/ppermute | solution.py:52
  65.1 46.5 %collective-permute-start.8 = (bf16[960,640]{1,0:T(8,128)(2,1)S(1)}, bf16[960,640]{1,0:T(8,128)(2,1)}, u32[]{:S(2)}, u32[]{:S(2)}) collective-permute-start(bf16[960,640]{1,0:T(8,128)(2,1)S(1)} %bitcast.390), channel_id=1, source_target_pairs={{0,1},{1,0},{2,3},{3,2},{4,5},{5,4},{6,7},{7,6},{8,9},{9,8},{10,11... | collective-permute-start | bytes 3686408 | tf_op jit(solution)/shard_map/ppermute | solution.py:52
  67.0 25.0 %collective-permute-start.7 = (bf16[144,960]{1,0:T(8,128)(2,1)S(1)}, bf16[144,960]{1,0:T(8,128)(2,1)S(1)}, u32[]{:S(2)}, u32[]{:S(2)}) collective-permute-start(bf16[144,960]{1,0:T(8,128)(2,1)S(1)} %collective-permute-done.3.refs_0_), channel_id=1, source_target_pairs={{0,3},{1,2},{2,1},{3,0},{16,19},{17,18},{18,17},{19,16},{4,7},{5,6... | collective-permute-start | bytes 829448 | tf_op jit(solution)/shard_map/ppermute | solution.py:52
  68.5 33.6 %collective-permute-start.6 = (bf16[144,960]{1,0:T(8,128)(2,1)S(1)}, bf16[144,960]{1,0:T(8,128)(2,1)S(1)}, u32[]{:S(2)}, u32[]{:S(2)}) collective-permute-start(bf16[144,960]{1,0:T(8,128)(2,1)S(1)} %collective-permute-done.3.refs_0_), channel_id=1, source_target_pairs={{0,2},{1,3},{2,0},{3,1},{16,18},{17,19},{18,16},{19,17},{4,6},{5,7... | collective-permute-start | bytes 829448 | tf_op jit(solution)/shard_map/ppermute | solution.py:52
  92.1 14.8 %collective-permute-start.5 = (bf16[144,960]{1,0:T(8,128)(2,1)S(1)}, bf16[144,960]{1,0:T(8,128)(2,1)S(1)}, u32[]{:S(2)}, u32[]{:S(2)}) collective-permute-start(bf16[144,960]{1,0:T(8,128)(2,1)S(1)} %collective-permute-done.3.refs_0_), channel_id=1, source_target_pairs={{0,1},{1,0},{2,3},{3,2},{16,17},{17,16},{18,19},{19,18},{4,5},{5,4... | collective-permute-start | bytes 829448 | tf_op jit(solution)/shard_map/ppermute | solution.py:52
  117.1 17.0 %collective-permute-start.12 = (bf16[4,960,640]{2,1,0:T(8,128)(2,1)}, bf16[4,960,640]{2,1,0:T(8,128)(2,1)}, u32[]{:S(2)}, u32[]{:S(2)}) collective-permute-start(bf16[4,960,640]{2,1,0:T(8,128)(2,1)} %copy-done), channel_id=1, source_target_pairs={{0,16},{1,17},{2,18},{3,19},{4,20},{5,21},{6,22},{7,23},{8,24},{9,... | collective-permute-start | bytes 14745608 | tf_op jit(solution)/shard_map/ppermute | solution.py:34
  132.4 255.7 %reduce-scatter.4.cloned.1.call-start = ((), (), s32[]{:S(2)}) async-start(), calls=%async_computation.3 | async-start | bytes 2457600 | tf_op jit(solution)/shard_map/reduce_scatter | solution.py:381
  143.5 32.9 %collective-permute-start.27 = (bf16[960,640]{1,0:T(8,128)(2,1)S(1)}, bf16[960,640]{1,0:T(8,128)(2,1)}, u32[]{:S(2)}, u32[]{:S(2)}) collective-permute-start(bf16[960,640]{1,0:T(8,128)(2,1)S(1)} %bitcast.384), channel_id=1, source_target_pairs={{16,19},{17,18},{18,17},{19,16},{20,23},{21,22},{22,21},{23,20},{2... | collective-permute-start | bytes 3686408 | tf_op jit(solution)/shard_map/ppermute | solution.py:52
  145.3 31.2 %collective-permute-start.26 = (bf16[960,640]{1,0:T(8,128)(2,1)S(1)}, bf16[960,640]{1,0:T(8,128)(2,1)}, u32[]{:S(2)}, u32[]{:S(2)}) collective-permute-start(bf16[960,640]{1,0:T(8,128)(2,1)S(1)} %bitcast.385), channel_id=1, source_target_pairs={{16,18},{17,19},{18,16},{19,17},{20,22},{21,23},{22,20},{23,21},{2... | collective-permute-start | bytes 3686408 | tf_op jit(solution)/shard_map/ppermute | solution.py:52
  147.0 45.8 %collective-permute-start.25 = (bf16[960,640]{1,0:T(8,128)(2,1)S(1)}, bf16[960,640]{1,0:T(8,128)(2,1)}, u32[]{:S(2)}, u32[]{:S(2)}) collective-permute-start(bf16[960,640]{1,0:T(8,128)(2,1)S(1)} %bitcast.386), channel_id=1, source_target_pairs={{16,17},{17,16},{18,19},{19,18},{20,21},{21,20},{22,23},{23,22},{2... | collective-permute-start | bytes 3686408 | tf_op jit(solution)/shard_map/ppermute | solution.py:52
  157.0 47.5 %collective-permute-start.15 = (bf16[240,320]{1,0:T(8,128)(2,1)}, bf16[240,320]{1,0:T(8,128)(2,1)S(1)}, u32[]{:S(2)}, u32[]{:S(2)}) collective-permute-start(bf16[240,320]{1,0:T(8,128)(2,1)} %get-tuple-element.258), channel_id=1, source_target_pairs={{0,3},{1,2},{2,1},{3,0},{16,19},{17,18},{18,17},{19,16},{4,7},{5,6... | collective-permute-start | bytes 460808 | tf_op jit(solution)/shard_map/ppermute | solution.py:52
  157.0 47.5 %collective-permute-start.14 = (bf16[240,320]{1,0:T(8,128)(2,1)}, bf16[240,320]{1,0:T(8,128)(2,1)S(1)}, u32[]{:S(2)}, u32[]{:S(2)}) collective-permute-start(bf16[240,320]{1,0:T(8,128)(2,1)} %get-tuple-element.259), channel_id=1, source_target_pairs={{0,2},{1,3},{2,0},{3,1},{16,18},{17,19},{18,16},{19,17},{4,6},{5,7... | collective-permute-start | bytes 460808 | tf_op jit(solution)/shard_map/ppermute | solution.py:52
  176.4 28.0 %collective-permute-start.13 = (bf16[240,320]{1,0:T(8,128)(2,1)}, bf16[240,320]{1,0:T(8,128)(2,1)S(1)}, u32[]{:S(2)}, u32[]{:S(2)}) collective-permute-start(bf16[240,320]{1,0:T(8,128)(2,1)} %get-tuple-element.260), channel_id=1, source_target_pairs={{0,1},{1,0},{2,3},{3,2},{16,17},{17,16},{18,19},{19,18},{4,5},{5,4... | collective-permute-start | bytes 460808 | tf_op jit(solution)/shard_map/ppermute | solution.py:52
  176.5 33.6 %collective-permute-start.16 = (bf16[960,640]{1,0:T(8,128)(2,1)}, bf16[960,640]{1,0:T(8,128)(2,1)}, u32[]{:S(2)}, u32[]{:S(2)}) collective-permute-start(bf16[960,640]{1,0:T(8,128)(2,1)} %bitcast.52), channel_id=1, source_target_pairs={{0,16},{16,0},{1,17},{17,1},{2,18},{18,2},{3,19},{19,3},{4,20},{20... | collective-permute-start | bytes 3686408 | tf_op jit(solution)/shard_map/ppermute | solution.py:38
  197.1 49.5 %collective-permute-start.28 = (bf16[4,960,640]{2,1,0:T(8,128)(2,1)}, bf16[4,960,640]{2,1,0:T(8,128)(2,1)}, u32[]{:S(2)}, u32[]{:S(2)}) collective-permute-start(bf16[4,960,640]{2,1,0:T(8,128)(2,1)} %shard_map.208), channel_id=1, source_target_pairs={{16,0},{17,1},{18,2},{19,3},{20,4},{21,5},{22,6},{23,7},{24,8},{25... | collective-permute-start | bytes 14745608 | tf_op jit(solution)/shard_map/ppermute | solution.py:34
  237.7 34.6 %collective-permute-start.33 = (bf16[960,640]{1,0:T(8,128)(2,1)}, bf16[960,640]{1,0:T(8,128)(2,1)}, u32[]{:S(2)}, u32[]{:S(2)}) collective-permute-start(bf16[960,640]{1,0:T(8,128)(2,1)} %bitcast.85), channel_id=1, source_target_pairs={{0,16},{16,0},{1,17},{17,1},{2,18},{18,2},{3,19},{19,3},{4,20},{20... | collective-permute-start | bytes 3686408 | tf_op jit(solution)/shard_map/ppermute | solution.py:38
  246.6 27.6 %collective-permute-start.32 = (bf16[320,960]{1,0:T(8,128)(2,1)}, bf16[320,960]{1,0:T(8,128)(2,1)}, u32[]{:S(2)}, u32[]{:S(2)}) collective-permute-start(bf16[320,960]{1,0:T(8,128)(2,1)} %bitcast.83), channel_id=1, source_target_pairs={{0,16},{16,0},{1,17},{17,1},{2,18},{18,2},{3,19},{19,3},{4,20},{20... | collective-permute-start | bytes 1843208 | tf_op jit(solution)/shard_map/ppermute | solution.py:38
  282.3 8.4 %collective-permute-start.34 = (bf16[128,960]{0,1:T(8,128)(2,1)S(1)}, bf16[128,960]{0,1:T(8,128)(2,1)S(1)}, u32[]{:S(2)}, u32[]{:S(2)}) collective-permute-start(bf16[128,960]{0,1:T(8,128)(2,1)S(1)} %get-tuple-element.294), channel_id=1, source_target_pairs={{0,1},{1,0},{2,3},{3,2},{16,17},{17,16},{18,19},{19,18},{4,5},{5,4... | collective-permute-start | bytes 737288 | tf_op jit(solution)/shard_map/ppermute | solution.py:52
  284.2 14.7 %collective-permute-start.39 = (bf16[320,960]{1,0:T(8,128)(2,1)S(1)}, bf16[320,960]{1,0:T(8,128)(2,1)S(1)}, u32[]{:S(2)}, u32[]{:S(2)}) collective-permute-start(bf16[320,960]{1,0:T(8,128)(2,1)S(1)} %convolution_convert_fusion.3), channel_id=1, source_target_pairs={{0,16},{16,0},{1,17},{17,1},{2,18},{18,2},{3,19},{19,3},{4,20},{20... | collective-permute-start | bytes 1843208 | tf_op jit(solution)/shard_map/ppermute | solution.py:38
  284.2 26.5 %collective-permute-start.38 = (bf16[960,640]{1,0:T(8,128)(2,1)S(1)}, bf16[960,640]{1,0:T(8,128)(2,1)S(1)}, u32[]{:S(2)}, u32[]{:S(2)}) collective-permute-start(bf16[960,640]{1,0:T(8,128)(2,1)S(1)} %convolution_convert_fusion.1), channel_id=1, source_target_pairs={{0,16},{16,0},{1,17},{17,1},{2,18},{18,2},{3,19},{19,3},{4,20},{20... | collective-permute-start | bytes 3686408 | tf_op jit(solution)/shard_map/ppermute | solution.py:38
  325.5 112.2 %reduce-scatter.6.cloned.1.call-start = ((), (), s32[]{:S(2)}) async-start(), calls=%async_computation.4 | async-start | bytes 2457600 | tf_op jit(solution)/shard_map/reduce_scatter | solution.py:381
  346.2 31.4 %collective-permute-start.58 = (bf16[960,320]{0,1:T(8,128)(2,1)S(1)}, bf16[960,320]{0,1:T(8,128)(2,1)S(1)}, u32[]{:S(2)}, u32[]{:S(2)}) collective-permute-start(bf16[960,320]{0,1:T(8,128)(2,1)S(1)} %fusion.21), channel_id=1, source_target_pairs={{0,16},{16,0},{1,17},{17,1},{2,18},{18,2},{3,19},{19,3},{4,20},{20... | collective-permute-start | bytes 1843208 | tf_op jit(solution)/shard_map/ppermute | solution.py:38
  353.7 8.4 %collective-permute-start.47 = (bf16[128,960]{0,1:T(8,128)(2,1)S(1)}, bf16[128,960]{0,1:T(8,128)(2,1)S(1)}, u32[]{:S(2)}, u32[]{:S(2)}) collective-permute-start(bf16[128,960]{0,1:T(8,128)(2,1)S(1)} %get-tuple-element.286), channel_id=1, source_target_pairs={{0,1},{1,0},{2,3},{3,2},{16,17},{17,16},{18,19},{19,18},{4,5},{5,4... | collective-permute-start | bytes 737288 | tf_op jit(solution)/shard_map/ppermute | solution.py:52
  356.1 16.7 %collective-permute-start.52 = (bf16[320,960]{1,0:T(8,128)(2,1)S(1)}, bf16[320,960]{1,0:T(8,128)(2,1)S(1)}, u32[]{:S(2)}, u32[]{:S(2)}) collective-permute-start(bf16[320,960]{1,0:T(8,128)(2,1)S(1)} %convolution_convert_fusion.2), channel_id=1, source_target_pairs={{0,16},{16,0},{1,17},{17,1},{2,18},{18,2},{3,19},{19,3},{4,20},{20... | collective-permute-start | bytes 1843208 | tf_op jit(solution)/shard_map/ppermute | solution.py:38
  357.8 26.9 %collective-permute-start.51 = (bf16[960,640]{1,0:T(8,128)(2,1)}, bf16[960,640]{1,0:T(8,128)(2,1)}, u32[]{:S(2)}, u32[]{:S(2)}) collective-permute-start(bf16[960,640]{1,0:T(8,128)(2,1)} %convolution_convert_fusion), channel_id=1, source_target_pairs={{0,16},{16,0},{1,17},{17,1},{2,18},{18,2},{3,19},{19,3},{4,20},{20... | collective-permute-start | bytes 3686408 | tf_op jit(solution)/shard_map/ppermute | solution.py:38
  396.8 88.6 %reduce-scatter.8.cloned.1.call-start = ((), (), s32[]{:S(2)}) async-start(), calls=%async_computation.5 | async-start | bytes 1638400 | tf_op jit(solution)/shard_map/reduce_scatter | solution.py:381
  396.9 10.7 %collective-permute-start.59 = (bf16[240,960]{1,0:T(8,128)(2,1)}, bf16[240,960]{1,0:T(8,128)(2,1)S(1)}, u32[]{:S(2)}, u32[]{:S(2)}) collective-permute-start(bf16[240,960]{1,0:T(8,128)(2,1)} %bitcast.479), channel_id=1, source_target_pairs={{0,16},{1,17},{2,18},{3,19},{4,20},{5,21},{6,22},{7,23},{8,24},{9,... | collective-permute-start | bytes 1382408 | tf_op jit(solution)/shard_map/ppermute | solution.py:34
  404.3 8.4 %collective-permute-start.56 = (bf16[960,320]{0,1:T(8,128)(2,1)}, bf16[960,320]{0,1:T(8,128)(2,1)}, u32[]{:S(2)}, u32[]{:S(2)}) collective-permute-start(bf16[960,320]{0,1:T(8,128)(2,1)} %fusion.20), channel_id=1, source_target_pairs={{0,16},{16,0},{1,17},{17,1},{2,18},{18,2},{3,19},{19,3},{4,20},{20... | collective-permute-start | bytes 1843208 | tf_op jit(solution)/shard_map/ppermute | solution.py:38
  407.8 12.9 %collective-permute-start.62 = (bf16[240,1920]{1,0:T(8,128)(2,1)S(1)}, bf16[240,1920]{1,0:T(8,128)(2,1)S(1)}, u32[]{:S(2)}, u32[]{:S(2)}) collective-permute-start(bf16[240,1920]{1,0:T(8,128)(2,1)S(1)} %pad_maximum_fusion.9.refs_0_), channel_id=1, source_target_pairs={{16,19},{17,18},{18,17},{19,16},{20,23},{21,22},{22,21},{23,20},{2... | collective-permute-start | bytes 2764808 | tf_op jit(solution)/shard_map/ppermute | solution.py:52
  408.5 12.2 %collective-permute-start.61 = (bf16[240,1920]{1,0:T(8,128)(2,1)S(1)}, bf16[240,1920]{1,0:T(8,128)(2,1)S(1)}, u32[]{:S(2)}, u32[]{:S(2)}) collective-permute-start(bf16[240,1920]{1,0:T(8,128)(2,1)S(1)} %pad_maximum_fusion.9.refs_0_), channel_id=1, source_target_pairs={{16,18},{17,19},{18,16},{19,17},{20,22},{21,23},{22,20},{23,21},{2... | collective-permute-start | bytes 2764808 | tf_op jit(solution)/shard_map/ppermute | solution.py:52
  409.3 11.4 %collective-permute-start.60 = (bf16[240,1920]{1,0:T(8,128)(2,1)S(1)}, bf16[240,1920]{1,0:T(8,128)(2,1)}, u32[]{:S(2)}, u32[]{:S(2)}) collective-permute-start(bf16[240,1920]{1,0:T(8,128)(2,1)S(1)} %pad_maximum_fusion.9.refs_0_), channel_id=1, source_target_pairs={{16,17},{17,16},{18,19},{19,18},{20,21},{21,20},{22,23},{23,22},{2... | collective-permute-start | bytes 2764808 | tf_op jit(solution)/shard_map/ppermute | solution.py:52
  441.2 16.4 %collective-permute-start.65 = (bf16[256,960]{0,1:T(8,128)(2,1)}, bf16[256,960]{0,1:T(8,128)(2,1)}, u32[]{:S(2)}, u32[]{:S(2)}) collective-permute-start(bf16[256,960]{0,1:T(8,128)(2,1)} %get-tuple-element.238), channel_id=1, source_target_pairs={{0,16},{16,0},{1,17},{17,1},{2,18},{18,2},{3,19},{19,3},{4,20},{20... | collective-permute-start | bytes 1474568 | tf_op jit(solution)/shard_map/ppermute | solution.py:38
  442.7 30.9 %collective-permute-start.74 = (bf16[240,1920]{1,0:T(8,128)(2,1)S(1)}, bf16[240,1920]{1,0:T(8,128)(2,1)S(1)}, u32[]{:S(2)}, u32[]{:S(2)}) collective-permute-start(bf16[240,1920]{1,0:T(8,128)(2,1)S(1)} %pad_maximum_fusion.10.refs_0_), channel_id=1, source_target_pairs={{0,3},{1,2},{2,1},{3,0},{4,7},{5,6},{6,5},{7,4},{8,11},{9,10},{10,... | collective-permute-start | bytes 2764808 | tf_op jit(solution)/shard_map/ppermute | solution.py:52
  447.0 26.6 %collective-permute-start.73 = (bf16[240,1920]{1,0:T(8,128)(2,1)S(1)}, bf16[240,1920]{1,0:T(8,128)(2,1)S(1)}, u32[]{:S(2)}, u32[]{:S(2)}) collective-permute-start(bf16[240,1920]{1,0:T(8,128)(2,1)S(1)} %pad_maximum_fusion.10.refs_0_), channel_id=1, source_target_pairs={{0,2},{1,3},{2,0},{3,1},{4,6},{5,7},{6,4},{7,5},{8,10},{9,11},{10,... | collective-permute-start | bytes 2764808 | tf_op jit(solution)/shard_map/ppermute | solution.py:52
  449.4 24.2 %collective-permute-start.72 = (bf16[240,1920]{1,0:T(8,128)(2,1)S(1)}, bf16[240,1920]{1,0:T(8,128)(2,1)}, u32[]{:S(2)}, u32[]{:S(2)}) collective-permute-start(bf16[240,1920]{1,0:T(8,128)(2,1)S(1)} %pad_maximum_fusion.10.refs_0_), channel_id=1, source_target_pairs={{0,1},{1,0},{2,3},{3,2},{4,5},{5,4},{6,7},{7,6},{8,9},{9,8},{10,11... | collective-permute-start | bytes 2764808 | tf_op jit(solution)/shard_map/ppermute | solution.py:52
  456.4 9.9 %collective-permute-start.63 = (bf16[256,960]{0,1:T(8,128)(2,1)}, bf16[256,960]{0,1:T(8,128)(2,1)}, u32[]{:S(2)}, u32[]{:S(2)}) collective-permute-start(bf16[256,960]{0,1:T(8,128)(2,1)} %broadcast_select_fusion.5), channel_id=1, source_target_pairs={{0,16},{16,0},{1,17},{17,1},{2,18},{18,2},{3,19},{19,3},{4,20},{20... | collective-permute-start | bytes 1474568 | tf_op jit(solution)/shard_map/ppermute | solution.py:38
  461.4 19.5 %collective-permute-start.66 = (bf16[2,64,960]{2,1,0:T(8,128)(2,1)}, bf16[2,64,960]{2,1,0:T(8,128)(2,1)}, u32[]{:S(2)}, u32[]{:S(2)}) collective-permute-start(bf16[2,64,960]{2,1,0:T(8,128)(2,1)} %fusion.100), channel_id=1, source_target_pairs={{0,0},{1,4},{2,8},{3,12},{4,1},{5,5},{6,9},{7,13},{8,2},{9,6},{10,... | collective-permute-start | bytes 737288 | tf_op jit(solution)/shard_map/ppermute | solution.py:62
  470.0 10.9 %collective-permute-start.64 = (bf16[2,64,960]{2,1,0:T(8,128)(2,1)}, bf16[2,64,960]{2,1,0:T(8,128)(2,1)}, u32[]{:S(2)}, u32[]{:S(2)}) collective-permute-start(bf16[2,64,960]{2,1,0:T(8,128)(2,1)} %fusion.104), channel_id=1, source_target_pairs={{0,0},{1,4},{2,8},{3,12},{4,1},{5,5},{6,9},{7,13},{8,2},{9,6},{10,... | collective-permute-start | bytes 737288 | tf_op jit(solution)/shard_map/ppermute | solution.py:62
  487.2 10.1 %collective-permute-start.67 = (bf16[240,320]{1,0:T(8,128)(2,1)}, bf16[240,320]{1,0:T(8,128)(2,1)}, u32[]{:S(2)}, u32[]{:S(2)}) collective-permute-start(bf16[240,320]{1,0:T(8,128)(2,1)} %broadcast_select_fusion.13), channel_id=1, source_target_pairs={{0,16},{16,0},{1,17},{17,1},{2,18},{18,2},{3,19},{19,3},{4,20},{20... | collective-permute-start | bytes 460808 | tf_op jit(solution)/shard_map/ppermute | solution.py:38
  498.5 22.9 %collective-permute-start.70 = (bf16[240,640]{1,0:T(8,128)(2,1)S(1)}, bf16[240,640]{1,0:T(8,128)(2,1)S(1)}, u32[]{:S(2)}, u32[]{:S(2)}) collective-permute-start(bf16[240,640]{1,0:T(8,128)(2,1)S(1)} %pad_maximum_fusion.21.refs_0_), channel_id=1, source_target_pairs={{0,3},{1,2},{2,1},{3,0},{16,19},{17,18},{18,17},{19,16},{4,7},{5,6... | collective-permute-start | bytes 921608 | tf_op jit(solution)/shard_map/ppermute | solution.py:52
  499.9 33.0 %collective-permute-start.69 = (bf16[240,640]{1,0:T(8,128)(2,1)S(1)}, bf16[240,640]{1,0:T(8,128)(2,1)S(1)}, u32[]{:S(2)}, u32[]{:S(2)}) collective-permute-start(bf16[240,640]{1,0:T(8,128)(2,1)S(1)} %pad_maximum_fusion.21.refs_0_), channel_id=1, source_target_pairs={{0,2},{1,3},{2,0},{3,1},{16,18},{17,19},{18,16},{19,17},{4,6},{5,7... | collective-permute-start | bytes 921608 | tf_op jit(solution)/shard_map/ppermute | solution.py:52
  520.9 13.1 %collective-permute-start.68 = (bf16[240,640]{1,0:T(8,128)(2,1)S(1)}, bf16[240,640]{1,0:T(8,128)(2,1)S(1)}, u32[]{:S(2)}, u32[]{:S(2)}) collective-permute-start(bf16[240,640]{1,0:T(8,128)(2,1)S(1)} %pad_maximum_fusion.21.refs_0_), channel_id=1, source_target_pairs={{0,1},{1,0},{2,3},{3,2},{16,17},{17,16},{18,19},{19,18},{4,5},{5,4... | collective-permute-start | bytes 921608 | tf_op jit(solution)/shard_map/ppermute | solution.py:52
  (141 other events, 642.1 us)
Sparse Core Ops, SparseCore 0:
  39.7 61.7 all-gather.4
  132.5 56.7 all-gather.6
  325.6 40.5 reduce-scatter.3
  396.9 40.7 reduce-scatter.5
  442.5 42.8 reduce-scatter.7
